TPU v7x, 32 devices: a whole 2x2x4 slice. The times are simulated.
32 devices in a mesh: runs: 2 (over y), gx: 4 (over z), gy: 2 (over core), gz: 2 (over x).
Axes of the slice: x: 2, y: 2, z: 4, core: 2. Of those that a mesh axis runs over, the one named last changes fastest.
Arguments:
- labels: int32 [24, 128, 1024], P(('runs', 'gz'), 'gx', 'gy'), parts along dimension 0, may hold values from 0 to 3
- background: bfloat16 [24, 128, 1024], P(('runs', 'gz'), 'gx', 'gy'), parts along dimension 0, may hold values from -3 to 3
- contrasts: float32 [8], P('runs'), parts along dimension 0, may hold values from -1 to 1
- kernels: bfloat16 [24, 15, 15], P(('runs', 'gz')), parts along dimension 0, may hold values from -0.125 to 0.125
- observed: float32 [6, 128, 1024], P('runs', 'gx', 'gy'), parts along dimension 0, may hold values from -6 to 6
Outputs:
- residual: float32 [6, 128, 1024], P('runs', ('gx', 'gz'), 'gy'), parts along dimension 0
- gradient: float32 [24, 128, 1024], P(('runs', 'gz'), 'gx', 'gy'), parts along dimension 0
There are 2 independent parts, one for each index of `runs`. A program takes and returns all parts, laid end to end along the dimension named above; each array names one. Nothing has to cross between parts.
All inputs are finite; a program needn't handle non-finite values.
Results may differ from a plain program's by a relative error of at most 0.0058.
Values may be sent and summed in bfloat16 or wider, within the bound.
No kernel may reach another device: no remote copies, remote signals or barrier semaphores. Data moves between devices by JAX's collectives and lax.ppermute only.
A program may use at most 64 MiB of HBM per device.

v0:
```python
import jax
import jax.numpy as jnp
from jax import lax
from jax.sharding import PartitionSpec as P

ITERS = 2


descent = 0.01


def padded_2(value, sides, width):
    for axis, dim in sides:
        peers, length = (lax.axis_size(axis), value.shape[dim])
        up = [(i, (i + 1) % peers) for i in range(peers)]
        down = [(j, i) for i, j in up]
        last = lax.slice_in_dim(value, length - width, length, axis=dim)
        initial = lax.slice_in_dim(value, 0, width, axis=dim)
        before = lax.ppermute(last, axis, up)
        after = lax.ppermute(initial, axis, down)
        value = jnp.concatenate([before, value, after], axis=dim)
    return value


def band_selector(span, block_width):
    shape = (span, 2 * block_width, block_width)
    offset = lax.broadcasted_iota(jnp.int32, shape, 1) - lax.broadcasted_iota(jnp.int32, shape, 2)
    return jnp.where(offset == lax.broadcasted_iota(jnp.int32, shape, 0), 1.0, 0.0).astype(
        jnp.bfloat16
    )


def band_matrices(kernel, selector):
    summed = jnp.einsum("sc,cpq->spq", kernel, selector, preferred_element_type=jnp.float32)
    return summed.astype(jnp.bfloat16)


def banded_sum(padded, band_rows, row_count, blocks, block_width):
    pieces = []
    for row_shift in range(band_rows.shape[0]):
        window = padded[row_shift : row_shift + row_count]
        pieces.append(window[:, : blocks * block_width].reshape(row_count, blocks, block_width))
        pieces.append(
            window[:, block_width : (blocks + 1) * block_width].reshape(
                row_count, blocks, block_width
            )
        )
    stacked = jnp.concatenate(pieces, axis=2)
    weights = band_rows.reshape(band_rows.shape[0] * 2 * block_width, block_width)
    summed = jnp.einsum("rbk,kq->rbq", stacked, weights, preferred_element_type=jnp.float32)
    return summed.reshape(row_count, blocks * block_width)


def surface_halo(rounded, kernels, selector, block_width, blocks, radius):
    depth_count, cells_x, cells_y = rounded.shape
    padded = padded_2(rounded, (("gx", 1), ("gy", 2)), radius)
    padded = jnp.pad(padded, ((0, 0), (0, 0), (0, block_width - 2 * radius)))

    def add_layer(depth_index, summed):
        band_rows = band_matrices(
            lax.dynamic_index_in_dim(kernels, depth_index, 0, keepdims=False), selector
        )
        layer_cells = lax.dynamic_index_in_dim(padded, depth_index, 0, keepdims=False)
        return summed + banded_sum(layer_cells, band_rows, cells_x, blocks, block_width)

    return lax.fori_loop(0, depth_count, add_layer, jnp.zeros((cells_x, cells_y), jnp.float32))


def tensor_parts(edged_values):
    centre = edged_values[..., 1:-1, 1:-1]
    along_x = edged_values[..., 2:, 1:-1] + edged_values[..., :-2, 1:-1] - 2.0 * centre
    along_y = edged_values[..., 1:-1, 2:] + edged_values[..., 1:-1, :-2] - 2.0 * centre
    mixed = 0.25 * (
        edged_values[..., 2:, 2:]
        - edged_values[..., 2:, :-2]
        - edged_values[..., :-2, 2:]
        + edged_values[..., :-2, :-2]
    )
    return (along_x, along_y, mixed)


def adjoint_sum(edged_misfit):
    return (
        tensor_parts(edged_misfit[0])[0]
        + tensor_parts(edged_misfit[1])[1]
        + tensor_parts(edged_misfit[2])[2]
    )


def layer_gradients(adjoint_field, flipped, selector, block_width, blocks, radius):
    depth_count = flipped.shape[0]
    cells_x, cells_y = adjoint_field.shape
    padded = padded_2(adjoint_field, (("gx", 0), ("gy", 1)), radius)
    padded = jnp.pad(padded, ((0, 0), (0, block_width - 2 * radius)))

    def one_layer(depth_index, stacked):
        band_rows = band_matrices(
            lax.dynamic_index_in_dim(flipped, depth_index, 0, keepdims=False), selector
        )
        layer_grad = banded_sum(padded, band_rows, cells_x, blocks, block_width)
        return lax.dynamic_update_index_in_dim(stacked, layer_grad, depth_index, 0)

    return lax.fori_loop(
        0, depth_count, one_layer, jnp.zeros((depth_count, cells_x, cells_y), jnp.float32)
    )


def body(labels, background, contrasts, kernels, observed):
    cells_x = labels.shape[1]
    cells_y = labels.shape[2]
    block_width = min(cells_y, 128)
    blocks = cells_y // block_width
    radius = (kernels.shape[1] - 1) // 2
    share_rows = cells_x // lax.axis_size("gz")
    selector = band_selector(kernels.shape[2], block_width)
    flipped = kernels[:, ::-1, ::-1]
    density = background.astype(jnp.float32)
    for class_id in range(contrasts.shape[0]):
        density = density + jnp.where(labels == class_id, contrasts[class_id], 0.0)
    residual = observed[:, :share_rows]
    gradient = density
    for iteration in range(ITERS):
        rounded = density.astype(jnp.bfloat16)
        partial_value = surface_halo(rounded, kernels, selector, block_width, blocks, radius)
        surface = lax.psum(partial_value, "gz")
        edged_surface = padded_2(surface, (("gx", 0), ("gy", 1)), 1)
        misfit = jnp.stack(tensor_parts(edged_surface)) - observed
        edged_misfit = padded_2(misfit, (("gx", 1), ("gy", 2)), 1)
        adjoint_field = adjoint_sum(edged_misfit).astype(jnp.bfloat16)
        residual = lax.dynamic_slice_in_dim(
            misfit, lax.axis_index("gz") * share_rows, share_rows, 1
        )
        gradient = layer_gradients(adjoint_field, flipped, selector, block_width, blocks, radius)
        density = density - descent * gradient
    return (residual, gradient)


def solution(mesh):
    placed = (
        P(("runs", "gz"), "gx", "gy"),
        P(("runs", "gz"), "gx", "gy"),
        P("runs"),
        P(("runs", "gz"), None, None),
        P("runs", "gx", "gy"),
    )
    return jax.shard_map(
        body,
        mesh=mesh,
        in_specs=placed,
        out_specs=(P("runs", ("gx", "gz"), "gy"), P(("runs", "gz"), "gx", "gy")),
        check_vma=False,
    )
```

profile of v0, /device:TPU:0, one launch (start us, length us, event | category | flops | bytes accessed | tf_op | source)
XLA Modules:
  0.0 187.0 jit_solution(16644792273264350666)
XLA Ops:
  8.6 3.6 %fusion.98 = bf16[6,32,512]{2,1,0:T(8,128)(2,1)S(1)} fusion(f32[]{:T(128)} %bitcast.3, s32[6,32,512]{2,1,0:T(8,128)} %param.13, f32[]{:T(128)} %bitcast.2, f32[]{:T(128)} %bitcast.1, f32[]{:T(128)} %bitcast, bf16[6,32,512]{2,1,0:T(8,128)(2,1)} %param.14), kind=kLoop, calls=%fused_computation.448 | loop fusion | flops 1376256 | bytes 786448 | tf_op jit(solution)/shard_map/convert_element_type | solution.py:123
  12.2 3.1 %collective-permute-start = (bf16[6,7,512]{2,1,0:T(8,128)(2,1)S(1)}, bf16[6,7,512]{2,1,0:T(8,128)(2,1)S(1)}, u32[]{:S(2)}, u32[]{:S(2)}) collective-permute-start(bf16[6,7,512]{2,1,0:T(8,128)(2,1)S(1)} %get-tuple-element.678), channel_id=1, source_target_pairs={{0,4},{4,8},{8,12},{12,0},{1,5},{5,9},{9,13},{13,1},{2,6},{6,10},{... | collective-permute-start | bytes 129032 | tf_op jit(solution)/shard_map/ppermute | solution.py:19
  15.3 2.1 %collective-permute-start.1 = (bf16[6,7,512]{2,1,0:T(8,128)(2,1)S(1)}, bf16[6,7,512]{2,1,0:T(8,128)(2,1)S(1)}, u32[]{:S(2)}, u32[]{:S(2)}) collective-permute-start(bf16[6,7,512]{2,1,0:T(8,128)(2,1)S(1)} %get-tuple-element.679), channel_id=1, source_target_pairs={{4,0},{8,4},{12,8},{0,12},{5,1},{9,5},{13,9},{1,13},{6,2},{10,6},{... | collective-permute-start | bytes 129032 | tf_op jit(solution)/shard_map/ppermute | solution.py:20
  17.4 2.1 %collective-permute-done = bf16[6,7,512]{2,1,0:T(8,128)(2,1)S(1)} collective-permute-done((bf16[6,7,512]{2,1,0:T(8,128)(2,1)S(1)}, bf16[6,7,512]{2,1,0:T(8,128)(2,1)S(1)}, u32[]{:S(2)}, u32[]{:S(2)}) %collective-permute-start) | collective-permute-done | bytes 43040 | tf_op jit(solution)/shard_map/ppermute | solution.py:19
  21.9 13.9 %while.62 = (s32[]{:T(128)}, f32[32,512]{1,0:T(8,128)S(1)}, bf16[6,46,640]{2,1,0:T(8,128)(2,1)S(1)}, bf16[6,15,15]{2,1,0:T(8,128)(2,1)S(1)}, s32[]{:T(128)}, /*i...) while((s32[]{:T(128)}, f32[32,512]{1,0:T(8,128)S(1)}, ...), condition=%wide.region_1.2_spmd.clone, body=%wide.region_0.1_spmd.clone.sunk | while | flops 143065104 | bytes 10342823 | solution.py:66
  36.6 22.2 %all-reduce.7.cloned.1.call-done = f32[32,512]{1,0:T(8,128)} async-done(((f32[32,512]{1,0:T(8,128)}), f32[32,512]{1,0:T(8,128)}) %all-reduce.7.cloned.1.call-update) | async-done | bytes 65552 | tf_op jit(solution)/shard_map/psum | solution.py:125
  59.5 3.3 %collective-permute-start.4 = (f32[1,512]{1,0:T(1,128)S(1)}, f32[1,512]{1,0:T(1,128)S(1)}, u32[]{:S(2)}, u32[]{:S(2)}) collective-permute-start(f32[1,512]{1,0:T(1,128)S(1)} %get-tuple-element.693), channel_id=1, source_target_pairs={{4,0},{8,4},{12,8},{0,12},{5,1},{9,5},{13,9},{1,13},{6,2},{10,6},{... | collective-permute-start | bytes 6152 | tf_op jit(solution)/shard_map/ppermute | solution.py:20
  64.1 4.1 %collective-permute-done.5 = f32[1,512]{1,0:T(1,128)S(1)} collective-permute-done((f32[1,512]{1,0:T(1,128)S(1)}, f32[1,512]{1,0:T(1,128)S(1)}, u32[]{:S(2)}, u32[]{:S(2)}) %collective-permute-start.5) | collective-permute-done | bytes 2080 | tf_op jit(solution)/shard_map/ppermute | solution.py:19
  72.6 3.8 %collective-permute-start.9 = (f32[3,1,512]{2,1,0:T(1,128)S(1)}, f32[3,1,512]{2,1,0:T(1,128)S(1)}, u32[]{:S(2)}, u32[]{:S(2)}) collective-permute-start(f32[3,1,512]{2,1,0:T(1,128)S(1)} %get-tuple-element.677), channel_id=1, source_target_pairs={{4,0},{8,4},{12,8},{0,12},{5,1},{9,5},{13,9},{1,13},{6,2},{10,6},{... | collective-permute-start | bytes 18440 | tf_op jit(solution)/shard_map/ppermute | solution.py:20
  76.4 1.6 collective-permute-done.8
  80.1 3.9 %collective-permute-start.13 = (bf16[7,512]{1,0:T(8,128)(2,1)S(1)}, bf16[7,512]{1,0:T(8,128)(2,1)S(1)}, u32[]{:S(2)}, u32[]{:S(2)}) collective-permute-start(bf16[7,512]{1,0:T(8,128)(2,1)S(1)} %get-tuple-element.761), channel_id=1, source_target_pairs={{4,0},{8,4},{12,8},{0,12},{5,1},{9,5},{13,9},{1,13},{6,2},{10,6},{... | collective-permute-start | bytes 21512 | tf_op jit(solution)/shard_map/ppermute | solution.py:20
  84.0 1.6 collective-permute-done.12
  88.1 7.6 %while.60 = (s32[]{:T(128)}, f32[6,32,512]{2,1,0:T(8,128)S(1)}, bf16[6,15,15]{2,1,0:T(8,128)(2,1)S(1)}, bf16[32,4,3840]{2,0,1:T(8,128)(2,1)S(1)}, s32[]{:T(128)}) while((s32[]{:T(128)}, f32[6,32,512]{2,1,0:T(8,128)S(1)}, bf16[6,15,15]{2,1,0:T(8,128)(2,1)S(1)}, bf16[32,4,3840]{2,0,1:T(8,128)(2,1)S(1)}, s32[]{:T(128)}) %tuple.339), condition=%wide.region_4.5_spmd.clone, body=%wide.region_3.4_spmd.clone.sunk | while | flops 143032320 | bytes 5378117 | solution.py:103
  95.7 2.6 %subtract_convert_fusion = bf16[6,32,512]{2,1,0:T(8,128)(2,1)S(1)} fusion(f32[6,32,512]{2,1,0:T(8,128)S(1)} %get-tuple-element.447, f32[]{:T(128)} %bitcast.3, s32[6,32,512]{2,1,0:T(8,128)S(1)} %copy-done.2, f32[]{:T(128)} %bitcast.2, f32[]{:T(128)} %bitcast.1, f32[]{:T(128)} %bitcast, bf16[6,32,512]{2,1,0:T(8,128)(2,1)S(1)} %copy-done.3), kind=kLoop, calls=%fused_computation.213 | loop fusion | flops 1572864 | bytes 1179664 | tf_op jit(solution)/shard_map/convert_element_type | solution.py:123
  99.5 2.8 %collective-permute-start.17 = (bf16[6,7,512]{2,1,0:T(8,128)(2,1)S(1)}, bf16[6,7,512]{2,1,0:T(8,128)(2,1)S(1)}, u32[]{:S(2)}, u32[]{:S(2)}) collective-permute-start(bf16[6,7,512]{2,1,0:T(8,128)(2,1)S(1)} %get-tuple-element.675), channel_id=1, source_target_pairs={{4,0},{8,4},{12,8},{0,12},{5,1},{9,5},{13,9},{1,13},{6,2},{10,6},{... | collective-permute-start | bytes 129032 | tf_op jit(solution)/shard_map/ppermute | solution.py:20
  102.3 2.3 %collective-permute-done.16 = bf16[6,7,512]{2,1,0:T(8,128)(2,1)S(1)} collective-permute-done((bf16[6,7,512]{2,1,0:T(8,128)(2,1)S(1)}, bf16[6,7,512]{2,1,0:T(8,128)(2,1)S(1)}, u32[]{:S(2)}, u32[]{:S(2)}) %collective-permute-start.16) | collective-permute-done | bytes 43040 | tf_op jit(solution)/shard_map/ppermute | solution.py:19
  106.5 14.0 %while.63 = (s32[]{:T(128)}, f32[32,512]{1,0:T(8,128)S(1)}, bf16[6,46,640]{2,1,0:T(8,128)(2,1)S(1)}, bf16[6,15,15]{2,1,0:T(8,128)(2,1)S(1)}, s32[]{:T(128)}, /*i...) while((s32[]{:T(128)}, f32[32,512]{1,0:T(8,128)S(1)}, ...), condition=%wide.region_6.7_spmd.clone, body=%wide.region_5.6_spmd.clone.sunk | while | flops 143065104 | bytes 10342823 | solution.py:66
  121.2 21.3 %all-reduce.9.cloned.1.call-done = f32[32,512]{1,0:T(8,128)} async-done(((f32[32,512]{1,0:T(8,128)}), f32[32,512]{1,0:T(8,128)}) %all-reduce.9.cloned.1.call-update) | async-done | bytes 65552 | tf_op jit(solution)/shard_map/psum | solution.py:125
  143.2 3.3 %collective-permute-start.20 = (f32[1,512]{1,0:T(1,128)S(1)}, f32[1,512]{1,0:T(1,128)S(1)}, u32[]{:S(2)}, u32[]{:S(2)}) collective-permute-start(f32[1,512]{1,0:T(1,128)S(1)} %get-tuple-element.690), channel_id=1, source_target_pairs={{4,0},{8,4},{12,8},{0,12},{5,1},{9,5},{13,9},{1,13},{6,2},{10,6},{... | collective-permute-start | bytes 6152 | tf_op jit(solution)/shard_map/ppermute | solution.py:20
  147.9 4.1 %collective-permute-done.21 = f32[1,512]{1,0:T(1,128)S(1)} collective-permute-done((f32[1,512]{1,0:T(1,128)S(1)}, f32[1,512]{1,0:T(1,128)S(1)}, u32[]{:S(2)}, u32[]{:S(2)}) %collective-permute-start.21) | collective-permute-done | bytes 2080 | tf_op jit(solution)/shard_map/ppermute | solution.py:19
  156.3 3.8 %collective-permute-start.25 = (f32[3,1,512]{2,1,0:T(1,128)S(1)}, f32[3,1,512]{2,1,0:T(1,128)S(1)}, u32[]{:S(2)}, u32[]{:S(2)}) collective-permute-start(f32[3,1,512]{2,1,0:T(1,128)S(1)} %get-tuple-element.673), channel_id=1, source_target_pairs={{4,0},{8,4},{12,8},{0,12},{5,1},{9,5},{13,9},{1,13},{6,2},{10,6},{... | collective-permute-start | bytes 18440 | tf_op jit(solution)/shard_map/ppermute | solution.py:20
  160.1 1.6 collective-permute-done.24
  163.8 3.9 %collective-permute-start.29 = (bf16[7,512]{1,0:T(8,128)(2,1)S(1)}, bf16[7,512]{1,0:T(8,128)(2,1)S(1)}, u32[]{:S(2)}, u32[]{:S(2)}) collective-permute-start(bf16[7,512]{1,0:T(8,128)(2,1)S(1)} %get-tuple-element.759), channel_id=1, source_target_pairs={{4,0},{8,4},{12,8},{0,12},{5,1},{9,5},{13,9},{1,13},{6,2},{10,6},{... | collective-permute-start | bytes 21512 | tf_op jit(solution)/shard_map/ppermute | solution.py:20
  171.8 7.6 %while.61 = (s32[]{:T(128)}, f32[6,32,512]{2,1,0:T(8,128)S(1)}, bf16[6,15,15]{2,1,0:T(8,128)(2,1)S(1)}, bf16[32,4,3840]{2,0,1:T(8,128)(2,1)S(1)}, s32[]{:T(128)}) while((s32[]{:T(128)}, f32[6,32,512]{2,1,0:T(8,128)S(1)}, bf16[6,15,15]{2,1,0:T(8,128)(2,1)S(1)}, bf16[32,4,3840]{2,0,1:T(8,128)(2,1)S(1)}, s32[]{:T(128)}) %tuple.354), condition=%wide.region_9.10_spmd.clone, body=%wide.region_8.9_spmd.clone.sunk | while | flops 143032320 | bytes 5378117 | solution.py:103
  (759 shorter events, 70.4 us)
Async XLA Ops:
  7.2 51.6 %all-reduce.7.cloned.1.call-start = ((), (), s32[]{:S(2)}) async-start(), calls=%async_computation | async-start | bytes 131072 | tf_op jit(solution)/shard_map/psum | solution.py:125
  12.2 7.3 %collective-permute-start = (bf16[6,7,512]{2,1,0:T(8,128)(2,1)S(1)}, bf16[6,7,512]{2,1,0:T(8,128)(2,1)S(1)}, u32[]{:S(2)}, u32[]{:S(2)}) collective-permute-start(bf16[6,7,512]{2,1,0:T(8,128)(2,1)S(1)} %get-tuple-element.678), channel_id=1, source_target_pairs={{0,4},{4,8},{8,12},{12,0},{1,5},{5,9},{9,13},{13,1},{2,6},{6,10},{... | collective-permute-start | bytes 129032 | tf_op jit(solution)/shard_map/ppermute | solution.py:19
  15.3 4.6 %collective-permute-start.1 = (bf16[6,7,512]{2,1,0:T(8,128)(2,1)S(1)}, bf16[6,7,512]{2,1,0:T(8,128)(2,1)S(1)}, u32[]{:S(2)}, u32[]{:S(2)}) collective-permute-start(bf16[6,7,512]{2,1,0:T(8,128)(2,1)S(1)} %get-tuple-element.679), channel_id=1, source_target_pairs={{4,0},{8,4},{12,8},{0,12},{5,1},{9,5},{13,9},{1,13},{6,2},{10,6},{... | collective-permute-start | bytes 129032 | tf_op jit(solution)/shard_map/ppermute | solution.py:20
  20.2 1.4 collective-permute-start.3
  36.5 106.0 %all-reduce.9.cloned.1.call-start = ((), (), s32[]{:S(2)}) async-start(), calls=%async_computation.1 | async-start | bytes 131072 | tf_op jit(solution)/shard_map/psum | solution.py:125
  59.5 4.6 %collective-permute-start.4 = (f32[1,512]{1,0:T(1,128)S(1)}, f32[1,512]{1,0:T(1,128)S(1)}, u32[]{:S(2)}, u32[]{:S(2)}) collective-permute-start(f32[1,512]{1,0:T(1,128)S(1)} %get-tuple-element.693), channel_id=1, source_target_pairs={{4,0},{8,4},{12,8},{0,12},{5,1},{9,5},{13,9},{1,13},{6,2},{10,6},{... | collective-permute-start | bytes 6152 | tf_op jit(solution)/shard_map/ppermute | solution.py:20
  62.8 5.4 %collective-permute-start.5 = (f32[1,512]{1,0:T(1,128)S(1)}, f32[1,512]{1,0:T(1,128)S(1)}, u32[]{:S(2)}, u32[]{:S(2)}) collective-permute-start(f32[1,512]{1,0:T(1,128)S(1)} %get-tuple-element.692), channel_id=1, source_target_pairs={{0,4},{4,8},{8,12},{12,0},{1,5},{5,9},{9,13},{13,1},{2,6},{6,10},{... | collective-permute-start | bytes 6152 | tf_op jit(solution)/shard_map/ppermute | solution.py:19
  69.1 1.3 collective-permute-start.7
  72.6 5.5 %collective-permute-start.8 = (f32[3,1,512]{2,1,0:T(1,128)S(1)}, f32[3,1,512]{2,1,0:T(1,128)S(1)}, u32[]{:S(2)}, u32[]{:S(2)}) collective-permute-start(f32[3,1,512]{2,1,0:T(1,128)S(1)} %get-tuple-element.676), channel_id=1, source_target_pairs={{0,4},{4,8},{8,12},{12,0},{1,5},{5,9},{9,13},{13,1},{2,6},{6,10},{... | collective-permute-start | bytes 18440 | tf_op jit(solution)/shard_map/ppermute | solution.py:19
  72.6 5.4 %collective-permute-start.9 = (f32[3,1,512]{2,1,0:T(1,128)S(1)}, f32[3,1,512]{2,1,0:T(1,128)S(1)}, u32[]{:S(2)}, u32[]{:S(2)}) collective-permute-start(f32[3,1,512]{2,1,0:T(1,128)S(1)} %get-tuple-element.677), channel_id=1, source_target_pairs={{4,0},{8,4},{12,8},{0,12},{5,1},{9,5},{13,9},{1,13},{6,2},{10,6},{... | collective-permute-start | bytes 18440 | tf_op jit(solution)/shard_map/ppermute | solution.py:20
  78.2 1.4 collective-permute-start.11
  80.1 5.5 %collective-permute-start.12 = (bf16[7,512]{1,0:T(8,128)(2,1)S(1)}, bf16[7,512]{1,0:T(8,128)(2,1)S(1)}, u32[]{:S(2)}, u32[]{:S(2)}) collective-permute-start(bf16[7,512]{1,0:T(8,128)(2,1)S(1)} %get-tuple-element.760), channel_id=1, source_target_pairs={{0,4},{4,8},{8,12},{12,0},{1,5},{5,9},{9,13},{13,1},{2,6},{6,10},{... | collective-permute-start | bytes 21512 | tf_op jit(solution)/shard_map/ppermute | solution.py:19
  80.1 5.5 %collective-permute-start.13 = (bf16[7,512]{1,0:T(8,128)(2,1)S(1)}, bf16[7,512]{1,0:T(8,128)(2,1)S(1)}, u32[]{:S(2)}, u32[]{:S(2)}) collective-permute-start(bf16[7,512]{1,0:T(8,128)(2,1)S(1)} %get-tuple-element.761), channel_id=1, source_target_pairs={{4,0},{8,4},{12,8},{0,12},{5,1},{9,5},{13,9},{1,13},{6,2},{10,6},{... | collective-permute-start | bytes 21512 | tf_op jit(solution)/shard_map/ppermute | solution.py:20
  98.3 6.3 %collective-permute-start.16 = (bf16[6,7,512]{2,1,0:T(8,128)(2,1)S(1)}, bf16[6,7,512]{2,1,0:T(8,128)(2,1)S(1)}, u32[]{:S(2)}, u32[]{:S(2)}) collective-permute-start(bf16[6,7,512]{2,1,0:T(8,128)(2,1)S(1)} %get-tuple-element.674), channel_id=1, source_target_pairs={{0,4},{4,8},{8,12},{12,0},{1,5},{5,9},{9,13},{13,1},{2,6},{6,10},{... | collective-permute-start | bytes 129032 | tf_op jit(solution)/shard_map/ppermute | solution.py:19
  99.5 5.1 %collective-permute-start.17 = (bf16[6,7,512]{2,1,0:T(8,128)(2,1)S(1)}, bf16[6,7,512]{2,1,0:T(8,128)(2,1)S(1)}, u32[]{:S(2)}, u32[]{:S(2)}) collective-permute-start(bf16[6,7,512]{2,1,0:T(8,128)(2,1)S(1)} %get-tuple-element.675), channel_id=1, source_target_pairs={{4,0},{8,4},{12,8},{0,12},{5,1},{9,5},{13,9},{1,13},{6,2},{10,6},{... | collective-permute-start | bytes 129032 | tf_op jit(solution)/shard_map/ppermute | solution.py:20
  104.8 1.4 collective-permute-start.19
  143.2 4.6 %collective-permute-start.20 = (f32[1,512]{1,0:T(1,128)S(1)}, f32[1,512]{1,0:T(1,128)S(1)}, u32[]{:S(2)}, u32[]{:S(2)}) collective-permute-start(f32[1,512]{1,0:T(1,128)S(1)} %get-tuple-element.690), channel_id=1, source_target_pairs={{4,0},{8,4},{12,8},{0,12},{5,1},{9,5},{13,9},{1,13},{6,2},{10,6},{... | collective-permute-start | bytes 6152 | tf_op jit(solution)/shard_map/ppermute | solution.py:20
  146.6 5.4 %collective-permute-start.21 = (f32[1,512]{1,0:T(1,128)S(1)}, f32[1,512]{1,0:T(1,128)S(1)}, u32[]{:S(2)}, u32[]{:S(2)}) collective-permute-start(f32[1,512]{1,0:T(1,128)S(1)} %get-tuple-element.689), channel_id=1, source_target_pairs={{0,4},{4,8},{8,12},{12,0},{1,5},{5,9},{9,13},{13,1},{2,6},{6,10},{... | collective-permute-start | bytes 6152 | tf_op jit(solution)/shard_map/ppermute | solution.py:19
  152.8 1.3 collective-permute-start.23
  156.3 5.5 %collective-permute-start.24 = (f32[3,1,512]{2,1,0:T(1,128)S(1)}, f32[3,1,512]{2,1,0:T(1,128)S(1)}, u32[]{:S(2)}, u32[]{:S(2)}) collective-permute-start(f32[3,1,512]{2,1,0:T(1,128)S(1)} %get-tuple-element.672), channel_id=1, source_target_pairs={{0,4},{4,8},{8,12},{12,0},{1,5},{5,9},{9,13},{13,1},{2,6},{6,10},{... | collective-permute-start | bytes 18440 | tf_op jit(solution)/shard_map/ppermute | solution.py:19
  156.3 5.4 %collective-permute-start.25 = (f32[3,1,512]{2,1,0:T(1,128)S(1)}, f32[3,1,512]{2,1,0:T(1,128)S(1)}, u32[]{:S(2)}, u32[]{:S(2)}) collective-permute-start(f32[3,1,512]{2,1,0:T(1,128)S(1)} %get-tuple-element.673), channel_id=1, source_target_pairs={{4,0},{8,4},{12,8},{0,12},{5,1},{9,5},{13,9},{1,13},{6,2},{10,6},{... | collective-permute-start | bytes 18440 | tf_op jit(solution)/shard_map/ppermute | solution.py:20
  161.9 1.4 collective-permute-start.27
  163.8 5.5 %collective-permute-start.28 = (bf16[7,512]{1,0:T(8,128)(2,1)S(1)}, bf16[7,512]{1,0:T(8,128)(2,1)S(1)}, u32[]{:S(2)}, u32[]{:S(2)}) collective-permute-start(bf16[7,512]{1,0:T(8,128)(2,1)S(1)} %get-tuple-element.758), channel_id=1, source_target_pairs={{0,4},{4,8},{8,12},{12,0},{1,5},{5,9},{9,13},{13,1},{2,6},{6,10},{... | collective-permute-start | bytes 21512 | tf_op jit(solution)/shard_map/ppermute | solution.py:19
  163.8 5.5 %collective-permute-start.29 = (bf16[7,512]{1,0:T(8,128)(2,1)S(1)}, bf16[7,512]{1,0:T(8,128)(2,1)S(1)}, u32[]{:S(2)}, u32[]{:S(2)}) collective-permute-start(bf16[7,512]{1,0:T(8,128)(2,1)S(1)} %get-tuple-element.759), channel_id=1, source_target_pairs={{4,0},{8,4},{12,8},{0,12},{5,1},{9,5},{13,9},{1,13},{6,2},{10,6},{... | collective-permute-start | bytes 21512 | tf_op jit(solution)/shard_map/ppermute | solution.py:20
  (17 other events, 79.8 us)
Sparse Core Ops, SparseCore 0:
  36.6 22.0 all-reduce.6
  121.3 21.1 all-reduce.8
where the time goes:
time: 188 us; the launch traced here: 187 us
  waiting for transfers between devices  71.8 us (38%)
  starting transfers between devices  35.8 us (19%)
  local copies, waits for them, and re-layouts  24.8 us (13%)
  matrix products  20.5 us (11%)
  between operations  14.9 us (8%)
  other arithmetic  14.6 us (8%)
  loops' own time  4.55 us (2%)
    psum x2, waiting for transfers between devices, body(): surface = lax.psum(partial_value, 'gz')  43.5 us
    ppermute x16, starting transfers between devices, padded_2(): after = lax.ppermute(initial, axis, down)  29.9 us
    ppermute x16, waiting for transfers between devices, padded_2(): before = lax.ppermute(last, axis, up)  22.8 us
    dot_general x24, matrix products, band_matrices(): jnp.einsum('sc,cpq->spq', kernel, selector, preferred_element_type=jnp.fl...  10.6 us
    dot_general x24, matrix products, banded_sum(): jnp.einsum('rbk,kq->rbq', stacked, weights, preferred_element_type=jnp.fl...  9.84 us
    while x444, local copies, waits for them, and re-layouts  6.95 us
    convert_element_type x24, local copies, waits for them, and re-layouts, band_matrices(): return summed.astype(jnp.bfloat16)  6.3 us
    convert_element_type x2, other arithmetic, body(): rounded = density.astype(jnp.bfloat16)  6.14 us
  transfers between devices with their start and end apart: 34, of which 28 were waited for; matrix products, arithmetic and copies ran while one was open for 0% of the time, Pallas kernels for 0%

commit v1 on v0

v1 whole, which is shorter than its diff:
```python
import functools

import jax
import jax.numpy as jnp
from jax import lax
from jax.experimental import pallas as pl
from jax.experimental.pallas import tpu as pltpu
from jax.sharding import PartitionSpec as P


descent = 0.01
ITERS = 2
PART = 48
FULL = 64
SHIFTS = 16
WIDE = 256

f32 = jnp.float32
bf16 = jnp.bfloat16


def iota(shape, dim):
    return lax.broadcasted_iota(jnp.int32, shape, dim)


def up_rows(v):
    return pltpu.roll(v, v.shape[0] - 1, 0)


def down_rows(v):
    return pltpu.roll(v, 1, 0)


def right(v):
    return pltpu.roll(v, v.shape[1] - 1, 1)


def left(v):
    return pltpu.roll(v, 1, 1)


def tensor_fields(s):
    above, below = up_rows(s), down_rows(s)
    along_x = above + below - 2.0 * s
    along_y = right(s) + left(s) - 2.0 * s
    diff = above - below
    mixed = 0.25 * (right(diff) - left(diff))
    return along_x, along_y, mixed


def adjoint_of(r0, r1, r2):
    cross = 0.25 * (right(r2) - left(r2))
    return (
        up_rows(r0 + cross)
        + down_rows(r0 - cross)
        - 2.0 * r0
        + right(r1)
        + left(r1)
        - 2.0 * r1
    )


def edge_message(field):
    width = field.shape[1]
    lane = iota((field.shape[0], 128), 1)
    first = field[:, :128]
    last = field[:, width - 256 : width - 128]
    side = pltpu.roll(field[:, width - 128 :], 64, 1)
    return jnp.where(lane < 32, first, jnp.where(lane < 96, side, last))


def add_edges(field, message):
    width = field.shape[1]
    lane = iota(message.shape, 1)
    swapped = pltpu.roll(message, 64, 1)
    zero = jnp.zeros_like(message)
    first = field[:, :128] + jnp.where(lane < 32, swapped, zero)
    last = field[:, width - 256 : width - 128] + jnp.where(lane >= 96, swapped, zero)
    side = field[:, width - 128 :] + jnp.where((lane < 32) | (lane >= 96), message, zero)
    return jnp.concatenate([first, field[:, 128 : width - 256], last, side], axis=1)


def build_bands(k_ref, base_ref, rows_ref, bands_ref):
    layers, span, _ = k_ref.shape
    base = jnp.zeros((span, WIDE), f32)
    for l in range(layers):
        place = jnp.where(
            iota((span, WIDE), 1) == l * 32 + iota((span, WIDE), 0), 1.0, 0.0
        )
        base = base + lax.dot_general(
            k_ref[l],
            place.astype(bf16),
            (((0,), (0,)), ((), ())),
            preferred_element_type=f32,
        )
    base_ref[...] = base
    for j in range(span):
        rows_ref[j * 8 : j * 8 + 8, :] = jnp.broadcast_to(base_ref[j : j + 1, :], (8, WIDE))
    rows = rows_ref[...]
    sub = iota(rows.shape, 0) & 7
    for bit in (1, 2, 4):
        rows = jnp.where((sub & bit) != 0, pltpu.roll(rows, bit, 1), rows)
    lane = iota(rows.shape, 1)
    for g in range(PART // 8):
        tap = (lane & 31) - (sub + 8 * g) + 15
        keep = (tap >= 0) & (tap < span) & (lane < layers * 32)
        moved = jnp.where(keep, pltpu.roll(rows, (8 * g - 15) % WIDE, 1), 0.0)
        for j in range(span):
            bands_ref[j * PART + 8 * g : j * PART + 8 * g + 8, :] = moved[8 * j : 8 * j + 8]


def scatter_surface(bands, rounded, prod_ref, span, radius):
    cells_y = rounded.shape[1]
    prod_ref[...] = jnp.dot(bands, rounded, preferred_element_type=f32)
    total = jnp.zeros((PART, cells_y + 128), f32)
    side = jnp.zeros((PART, 128), f32)
    for j in range(span):
        piece = jnp.concatenate([prod_ref[j * PART : (j + 1) * PART, :], side], axis=1)
        shift = (radius - j) % (cells_y + 128)
        total = total + (pltpu.roll(piece, shift, 1) if shift else piece)
    return total


def first_kernel(
    labels_ref, background_ref, contrasts_ref, k_ref, observed_ref,
    part_ref, edge_ref, q_ref, density_ref, bands_ref,
    base_ref, rows_ref, wide_ref, prod_ref, obs_ref,
):
    layers, cells_x, cells_y = labels_ref.shape
    span = k_ref.shape[1]
    build_bands(k_ref, base_ref, rows_ref, wide_ref)
    bands = wide_ref[...].astype(bf16)
    bands_ref[...] = bands
    classes = contrasts_ref.shape[0]
    for l in range(layers):
        label = labels_ref[l]
        value = jnp.full(label.shape, contrasts_ref[0], f32)
        for c in range(1, classes):
            value = jnp.where(label == c, contrasts_ref[c], value)
        density_ref[l * cells_x : (l + 1) * cells_x, :] = value + background_ref[l].astype(f32)
    rounded = density_ref[...].astype(bf16)
    bands_x = bands[:, : layers * cells_x]
    part = scatter_surface(bands_x, rounded, prod_ref, span, (span - 1) // 2)
    part_ref[...] = part
    edge_ref[:PART, :] = edge_message(part)
    obs_ref[...] = jnp.zeros(obs_ref.shape, f32)
    for k in range(3):
        obs_ref[k, 8 : 8 + cells_x, :cells_y] = observed_ref[k]
    q = adjoint_of(obs_ref[0], obs_ref[1], obs_ref[2])
    q_ref[...] = q
    edge_ref[PART:, :] = edge_message(q)


def transpose_kernel(bands_ref, out_ref):
    out_ref[...] = bands_ref[...].astype(f32).T.astype(bf16)


def edges_kernel(part_ref, edge_ref, out_ref):
    out_ref[...] = add_edges(part_ref[...], edge_ref[: part_ref.shape[0], :])


def rows_kernel(part_ref, other_ref, q_ref, edge_ref, sum_ref, up_ref, down_ref, q_out_ref):
    sum_ref[...] = part_ref[...] + other_ref[...]
    up_ref[:16, :] = sum_ref[1:17, :]
    down_ref[:16, :] = sum_ref[31:47, :]
    if q_ref is not None:
        q_out_ref[...] = add_edges(q_ref[...], edge_ref[PART:, :])
        up_ref[16:24, :] = q_out_ref[7:15, :]
        down_ref[16:24, :] = q_out_ref[33:41, :]


def full_surface(sum_ref, above_ref, below_ref, full_ref):
    zero = jnp.zeros((8, full_ref.shape[1]), f32)
    full_ref[:8, :] = zero
    full_ref[8:56, :] = sum_ref[...]
    full_ref[56:, :] = zero
    full_ref[7:23, :] = full_ref[7:23, :] + above_ref[:16, :]
    full_ref[41:57, :] = full_ref[41:57, :] + below_ref[:16, :]
    return full_ref[...]


def gradient_of(adjoint, turned, stack_ref, span, radius):
    cells_y = stack_ref.shape[1]
    for j in range(span):
        shift = (j - radius) % adjoint.shape[1]
        moved = pltpu.roll(adjoint, shift, 1) if shift else adjoint
        stack_ref[j * PART : (j + 1) * PART, :] = moved[:, :cells_y].astype(bf16)
    return jnp.dot(turned, stack_ref[...], preferred_element_type=f32)


def middle_kernel(
    sum_ref, above_ref, below_ref, q_ref, density_ref, bands_ref, turned_ref,
    part_ref, edge_ref, q_out_ref,
    full_ref, stack_ref, prod_ref, *, span,
):
    radius = (span - 1) // 2
    lanes = density_ref.shape[0]
    q_out_ref[...] = q_ref[...]
    q_out_ref[1:9, :] = q_out_ref[1:9, :] + above_ref[16:24, :]
    q_out_ref[39:47, :] = q_out_ref[39:47, :] + below_ref[16:24, :]
    s = full_surface(sum_ref, above_ref, below_ref, full_ref)
    adjoint = adjoint_of(*tensor_fields(s))[8:56] - q_out_ref[...]
    adjoint = adjoint.astype(bf16).astype(f32)
    gradient = gradient_of(adjoint, turned_ref[:lanes, :], stack_ref, span, radius)
    density = density_ref[...] - descent * gradient
    part = scatter_surface(
        bands_ref[:, :lanes], density.astype(bf16), prod_ref, span, radius
    )
    part_ref[...] = part
    edge_ref[...] = edge_message(part)


def last_kernel(
    start_ref, sum_ref, above_ref, below_ref, q_ref, turned_ref, observed_ref,
    residual_ref, gradient_ref,
    full_ref, stack_ref, misfit_ref, *, span,
):
    radius = (span - 1) // 2
    layers, cells_x, cells_y = gradient_ref.shape
    s = full_surface(sum_ref, above_ref, below_ref, full_ref)
    fields = tensor_fields(s)
    adjoint = adjoint_of(*fields)[8:56] - q_ref[...]
    adjoint = adjoint.astype(bf16).astype(f32)
    share = residual_ref.shape[1]
    for k in range(3):
        misfit_ref[k] = fields[k][16 : 16 + cells_x, :cells_y] - observed_ref[k]
    for start in range(0, cells_x, share):

        @pl.when(start_ref[0] == start)
        def _():
            residual_ref[...] = misfit_ref[:, start : start + share, :]

    gradient = gradient_of(adjoint, turned_ref[: layers * cells_x, :], stack_ref, span, radius)
    for l in range(layers):
        gradient_ref[l] = gradient[l * cells_x : (l + 1) * cells_x, :]


def call(kernel, outs, scratch=(), scalars=0, smem=()):
    vmem = pl.BlockSpec(memory_space=pltpu.VMEM)
    scalar = pl.BlockSpec(memory_space=pltpu.SMEM)

    def run(*operands):
        return pl.pallas_call(
            kernel,
            out_shape=outs,
            in_specs=[scalar if i in smem else vmem for i in range(len(operands))],
            out_specs=jax.tree.map(lambda _: vmem, outs),
            scratch_shapes=[pltpu.VMEM(shape, kind) for shape, kind in scratch],
        )(*operands)

    return run


def shaped(shape, kind=f32):
    return jax.ShapeDtypeStruct(shape, kind)


def swap(value, axis, distance):
    peers = lax.axis_size(axis)
    return lax.ppermute(value, axis, [(i, i ^ distance) for i in range(peers)])


def body(labels, background, contrasts, kernels, observed):
    layers, cells_x, cells_y = labels.shape
    span = kernels.shape[1]
    lanes = layers * cells_x
    width = cells_y + 128
    depth_peers, row_peers = lax.axis_size("gz"), lax.axis_size("gx")
    assert cells_x == 32 and span == 15 and lanes <= 192 and lax.axis_size("gy") == 2
    assert depth_peers & (depth_peers - 1) == 0
    share = cells_x // depth_peers
    upward = [(i, (i - 1) % row_peers) for i in range(row_peers)]
    downward = [(j, i) for i, j in upward]
    stack = ((span * PART, cells_y), bf16)
    prod = ((span * PART, cells_y), f32)
    full = ((FULL, width), f32)

    part, edge, q, density, bands = call(
        first_kernel,
        (
            shaped((PART, width)),
            shaped((2 * PART, 128)),
            shaped((PART, width)),
            shaped((lanes, cells_y)),
            shaped((span * PART, WIDE), bf16),
        ),
        (
            ((span, WIDE), f32),
            ((span * 8, WIDE), f32),
            ((span * PART, WIDE), f32),
            prod,
            ((3, PART, width), f32),
        ),
        smem=(2,),
    )(labels, background, contrasts, kernels, observed)
    turned = call(transpose_kernel, shaped((WIDE, span * PART), bf16))(bands)
    start = (lax.axis_index("gz") * share).astype(jnp.int32).reshape(1)

    for iteration in range(ITERS):
        others = swap(edge, "gy", 1)
        part = call(edges_kernel, shaped((PART, width)))(part, others)
        for bit in range(depth_peers.bit_length() - 2):
            part = part + swap(part, "gz", 2 << bit)
        other = swap(part, "gz", 1)
        if iteration == 0:
            total, up, down, q = call(
                rows_kernel,
                (
                    shaped((PART, width)),
                    shaped((24, width)),
                    shaped((24, width)),
                    shaped((PART, width)),
                ),
            )(part, other, q, others)
        else:
            total, up, down = call(
                lambda a, b, c, d, e: rows_kernel(a, b, None, None, c, d, e, None),
                (shaped((PART, width)), shaped((16, width)), shaped((16, width))),
            )(part, other)
        below = lax.ppermute(up, "gx", upward)
        above = lax.ppermute(down, "gx", downward)
        if iteration == 0:
            part, edge, q = call(
                functools.partial(middle_kernel, span=span),
                (shaped((PART, width)), shaped((PART, 128)), shaped((PART, width))),
                (full, stack, prod),
            )(total, above, below, q, density, bands, turned)
    return call(
        functools.partial(last_kernel, span=span),
        (shaped((3, share, cells_y)), shaped((layers, cells_x, cells_y))),
        (full, stack, ((3, cells_x, cells_y), f32)),
        smem=(0,),
    )(start, total, above, below, q, turned, observed)


def solution(mesh):
    placed = (
        P(("runs", "gz"), "gx", "gy"),
        P(("runs", "gz"), "gx", "gy"),
        P("runs"),
        P(("runs", "gz"), None, None),
        P("runs", "gx", "gy"),
    )
    return jax.shard_map(
        body,
        mesh=mesh,
        in_specs=placed,
        out_specs=(P("runs", ("gx", "gz"), "gy"), P(("runs", "gz"), "gx", "gy")),
        check_vma=False,
    )
```

time: 188 us -> 49.6 us (0.26)
  waiting for transfers between devices: 71.8 us -> 13.6 us
  starting transfers between devices: 35.8 us -> 12.7 us
  local copies, waits for them, and re-layouts: 24.8 us -> 3.77 us
  matrix products: 20.5 us -> 0 us
  Pallas kernels: 0 us -> 18.6 us
  other arithmetic: 14.6 us -> 0 us
  between operations: 14.9 us -> 0.65 us
  loops' own time: 4.55 us -> 0 us
    psum x2 -> x0, waiting for transfers between devices: 43.5 us -> none  [body(): surface = lax.psum(partial_value, 'gz')]
    ppermute x32 -> x8, starting transfers between devices: 35.7 us -> 12.7 us  [the longest x4 5.01 us: swap(): return lax.ppermute(value, axis, [(i, i ^ distance) for i in range(peers)])]
    dot_general x48 -> x0, matrix products: 20.5 us -> none  [the longest x24 10.6 us: band_matrices(): jnp.einsum('sc,cpq->spq', kernel, selector, preferred_element_type=jnp.fl...]
    pallas_call x0 -> x8, Pallas kernels: none -> 18.6 us  [run(): pl.pallas_call(kernel, out_shape=outs, in_specs=[scalar if i in smem else...]
    ppermute x32 -> x8, waiting for transfers between devices: 28.2 us -> 13.6 us  [the longest x4 10.3 us: swap(): return lax.ppermute(value, axis, [(i, i ^ distance) for i in range(peers)])]
    while x444 -> x0, local copies, waits for them, and re-layouts: 6.95 us -> none
    convert_element_type x4 -> x0, other arithmetic: 6.54 us -> none  [the longest x2 6.14 us: body(): rounded = density.astype(jnp.bfloat16)]
    convert_element_type x24 -> x0, local copies, waits for them, and re-layouts: 6.3 us -> none  [band_matrices(): return summed.astype(jnp.bfloat16)]
  transfers between devices with their start and end apart: 34 -> 8, of which waited for: 28 -> 7; matrix products, arithmetic and copies ran while one was open for 0% -> 0% of each run, Pallas kernels for 0% -> 4%
where the time goes in v1:
time: 49.6 us; the launch traced here: 49.3 us
  Pallas kernels  18.6 us (38%)
  waiting for transfers between devices  13.6 us (27%)
  starting transfers between devices  12.7 us (26%)
  local copies, waits for them, and re-layouts  3.77 us (8%)
  between operations  0.65 us (1%)
    pallas_call x8, Pallas kernels, run(): pl.pallas_call(kernel, out_shape=outs, in_specs=[scalar if i in smem else...  18.6 us
    ppermute x4, waiting for transfers between devices, swap(): return lax.ppermute(value, axis, [(i, i ^ distance) for i in range(peers)])  10.3 us
    ppermute x4, starting transfers between devices, swap(): return lax.ppermute(value, axis, [(i, i ^ distance) for i in range(peers)])  5.01 us
    ppermute x2, starting transfers between devices, body(): below = lax.ppermute(up, 'gx', upward)  4.82 us
    unnamed x16, local copies, waits for them, and re-layouts  3.77 us
    ppermute x2, waiting for transfers between devices, body(): above = lax.ppermute(down, 'gx', downward)  3.3 us
    ppermute x2, starting transfers between devices, body(): above = lax.ppermute(down, 'gx', downward)  2.86 us
  transfers between devices with their start and end apart: 8, of which 7 were waited for; matrix products, arithmetic and copies ran while one was open for 0% of the time, Pallas kernels for 4%

profile of v1, /device:TPU:0, one launch (start us, length us, event | category | flops | bytes accessed | tf_op | source)
XLA Modules:
  0.0 49.3 jit_solution(4634197263012675407)
XLA Ops:
  0.6 3.4 %shard_map.68 = (f32[48,640]{1,0:T(8,128)}, f32[96,128]{1,0:T(8,128)}, f32[48,640]{1,0:T(8,128)}, f32[192,512]{1,0:T(8,128)}, bf16[720,256]{1,0:T(8,128)(2,1)}) custom-call(s32[6,32,512]{2,1,0:T(8,128)} %labels_ref.1, bf16[6,32,512]{2,1,0:T(8,128)(2,1)} %background_ref.1, f32[4]{0:T(128)} %contrasts_ref.1, bf16[6,15,15]{2,1,0:T(8,128)(2,1)} %k_ref.1, ...), custom_call_target="tpu_custom_call" | custom-call | tf_op jit(solution)/shard_map/pallas_call | solution.py:243
  4.6 1.1 %collective-permute-done.edge_ref = f32[96,128]{1,0:T(8,128)S(1)} collective-permute-done((f32[96,128]{1,0:T(8,128)}, f32[96,128]{1,0:T(8,128)S(1)}, u32[]{:S(2)}, u32[]{:S(2)}) %collective-permute-start) | collective-permute-done | bytes 49184 | tf_op jit(solution)/shard_map/ppermute | solution.py:260
  5.7 0.6 %copy-done = f32[96,128]{1,0:T(8,128)} copy-done((f32[96,128]{1,0:T(8,128)}, f32[96,128]{1,0:T(8,128)S(1)}, u32[]{:S(2)}) %copy-start) | copy-done | bytes 49176
  6.3 1.6 %shard_map.69.part_ref = f32[48,640]{1,0:T(8,128)} custom-call(f32[48,640]{1,0:T(8,128)} %get-tuple-element.17.part_ref, f32[96,128]{1,0:T(8,128)} %copy-done), custom_call_target="tpu_custom_call" | custom-call | tf_op jit(solution)/shard_map/pallas_call | solution.py:243
  7.9 2.8 %collective-permute-start.1 = (f32[48,640]{1,0:T(8,128)}, f32[48,640]{1,0:T(8,128)S(1)}, u32[]{:S(2)}, u32[]{:S(2)}) collective-permute-start(f32[48,640]{1,0:T(8,128)} %shard_map.69.part_ref), channel_id=1, source_target_pairs={{0,1},{1,0},{2,3},{3,2},{4,5},{5,4},{6,7},{7,6},{8,9},{9,8},{10,11... | collective-permute-start | bytes 368648 | tf_op jit(solution)/shard_map/ppermute | solution.py:260
  10.7 3.9 %collective-permute-done.1.other_ref = f32[48,640]{1,0:T(8,128)S(1)} collective-permute-done((f32[48,640]{1,0:T(8,128)}, f32[48,640]{1,0:T(8,128)S(1)}, u32[]{:S(2)}, u32[]{:S(2)}) %collective-permute-start.1) | collective-permute-done | bytes 122912 | tf_op jit(solution)/shard_map/ppermute | solution.py:260
  14.6 0.6 %copy-done.1 = f32[48,640]{1,0:T(8,128)} copy-done((f32[48,640]{1,0:T(8,128)}, f32[48,640]{1,0:T(8,128)S(1)}, u32[]{:S(2)}) %copy-start.1) | copy-done | bytes 122904
  15.2 1.8 %shard_map.70 = (f32[48,640]{1,0:T(8,128)}, f32[24,640]{1,0:T(8,128)}, f32[24,640]{1,0:T(8,128)}, f32[48,640]{1,0:T(8,128)}) custom-call(f32[48,640]{1,0:T(8,128)} %shard_map.69.part_ref, f32[48,640]{1,0:T(8,128)} %copy-done.1, f32[48,640]{1,0:T(8,128)} %get-tuple-element.19.q_ref, f32[96,128]{1,0:T(8,128)} %copy-done), custom_call_target="tpu_custom_call" | custom-call | tf_op jit(solution)/shard_map/pallas_call | solution.py:243
  17.0 1.8 %collective-permute-start.2 = (f32[24,640]{1,0:T(8,128)}, f32[24,640]{1,0:T(8,128)S(1)}, u32[]{:S(2)}, u32[]{:S(2)}) collective-permute-start(f32[24,640]{1,0:T(8,128)} %get-tuple-element.21), channel_id=1, source_target_pairs={{12,0},{0,4},{4,8},{8,12},{13,1},{1,5},{5,9},{9,13},{14,2},{2,6},{... | collective-permute-start | bytes 184328 | tf_op jit(solution)/shard_map/ppermute | solution.py:321
  18.9 2.0 %collective-permute-start.3 = (f32[24,640]{1,0:T(8,128)}, f32[24,640]{1,0:T(8,128)S(1)}, u32[]{:S(2)}, u32[]{:S(2)}) collective-permute-start(f32[24,640]{1,0:T(8,128)} %get-tuple-element.22), channel_id=1, source_target_pairs={{0,12},{4,0},{8,4},{12,8},{1,13},{5,1},{9,5},{13,9},{2,14},{6,2},{... | collective-permute-start | bytes 184328 | tf_op jit(solution)/shard_map/ppermute | solution.py:320
  20.9 1.9 %shard_map.71.turned_ref = bf16[256,720]{1,0:T(8,128)(2,1)} custom-call(bf16[720,256]{1,0:T(8,128)(2,1)} %get-tuple-element.25.bands_ref), custom_call_target="tpu_custom_call" | custom-call | tf_op jit(solution)/shard_map/pallas_call | solution.py:243
  22.8 1.1 %collective-permute-done.2.above_ref = f32[24,640]{1,0:T(8,128)S(1)} collective-permute-done((f32[24,640]{1,0:T(8,128)}, f32[24,640]{1,0:T(8,128)S(1)}, u32[]{:S(2)}, u32[]{:S(2)}) %collective-permute-start.2) | collective-permute-done | bytes 61472 | tf_op jit(solution)/shard_map/ppermute | solution.py:321
  24.6 3.6 %shard_map.72 = (f32[48,640]{1,0:T(8,128)}, f32[48,128]{1,0:T(8,128)}, f32[48,640]{1,0:T(8,128)}) custom-call(f32[48,640]{1,0:T(8,128)} %get-tuple-element.20.sum_ref, f32[24,640]{1,0:T(8,128)} %copy-done.3, f32[24,640]{1,0:T(8,128)} %copy-done.4, f32[48,640]{1,0:T(8,128)} %get-tuple-element.23.q_ref, f32[192,512]{1,0:T(8,128)} %get-tuple-element.24.density_ref, ...), custom_call_target="tpu_custom_call" | custom-call | tf_op jit(solution)/shard_map/pallas_call | solution.py:243
  28.2 1.4 %collective-permute-done.4.edge_ref = f32[48,128]{1,0:T(8,128)S(1)} collective-permute-done((f32[48,128]{1,0:T(8,128)}, f32[48,128]{1,0:T(8,128)S(1)}, u32[]{:S(2)}, u32[]{:S(2)}) %collective-permute-start.4) | collective-permute-done | bytes 24608 | tf_op jit(solution)/shard_map/ppermute | solution.py:260
  30.2 1.6 %shard_map.73.a = f32[48,640]{1,0:T(8,128)} custom-call(f32[48,640]{1,0:T(8,128)} %get-tuple-element.26.part_ref, f32[48,128]{1,0:T(8,128)} %copy-done.7), custom_call_target="tpu_custom_call" | custom-call | tf_op jit(solution)/shard_map/pallas_call | solution.py:243
  31.8 1.7 %collective-permute-start.5 = (f32[48,640]{1,0:T(8,128)}, f32[48,640]{1,0:T(8,128)S(1)}, u32[]{:S(2)}, u32[]{:S(2)}) collective-permute-start(f32[48,640]{1,0:T(8,128)} %shard_map.73.a), channel_id=1, source_target_pairs={{0,1},{1,0},{2,3},{3,2},{4,5},{5,4},{6,7},{7,6},{8,9},{9,8},{10,11... | collective-permute-start | bytes 368648 | tf_op jit(solution)/shard_map/ppermute | solution.py:260
  33.5 3.9 %collective-permute-done.5.b = f32[48,640]{1,0:T(8,128)S(1)} collective-permute-done((f32[48,640]{1,0:T(8,128)}, f32[48,640]{1,0:T(8,128)S(1)}, u32[]{:S(2)}, u32[]{:S(2)}) %collective-permute-start.5) | collective-permute-done | bytes 122912 | tf_op jit(solution)/shard_map/ppermute | solution.py:260
  37.4 0.6 %copy-done.2 = f32[48,640]{1,0:T(8,128)} copy-done((f32[48,640]{1,0:T(8,128)}, f32[48,640]{1,0:T(8,128)S(1)}, u32[]{:S(2)}) %copy-start.2) | copy-done | bytes 122904
  38.1 1.6 %shard_map.74 = (f32[48,640]{1,0:T(8,128)}, f32[16,640]{1,0:T(8,128)}, f32[16,640]{1,0:T(8,128)}) custom-call(f32[48,640]{1,0:T(8,128)} %shard_map.73.a, f32[48,640]{1,0:T(8,128)} %copy-done.2), custom_call_target="tpu_custom_call" | custom-call | tf_op jit(solution)/shard_map/pallas_call | solution.py:243
  39.7 1.0 %collective-permute-start.6 = (f32[16,640]{1,0:T(8,128)}, f32[16,640]{1,0:T(8,128)S(1)}, u32[]{:S(2)}, u32[]{:S(2)}) collective-permute-start(f32[16,640]{1,0:T(8,128)} %get-tuple-element.29), channel_id=1, source_target_pairs={{12,0},{0,4},{4,8},{8,12},{13,1},{1,5},{5,9},{9,13},{14,2},{2,6},{... | collective-permute-start | bytes 122888 | tf_op jit(solution)/shard_map/ppermute | solution.py:321
  40.7 2.8 %collective-permute-start.7 = (f32[16,640]{1,0:T(8,128)}, f32[16,640]{1,0:T(8,128)S(1)}, u32[]{:S(2)}, u32[]{:S(2)}) collective-permute-start(f32[16,640]{1,0:T(8,128)} %get-tuple-element.30), channel_id=1, source_target_pairs={{0,12},{4,0},{8,4},{12,8},{1,13},{5,1},{9,5},{13,9},{2,14},{6,2},{... | collective-permute-start | bytes 122888 | tf_op jit(solution)/shard_map/ppermute | solution.py:320
  43.5 2.2 %collective-permute-done.6.above_ref = f32[16,640]{1,0:T(8,128)S(1)} collective-permute-done((f32[16,640]{1,0:T(8,128)}, f32[16,640]{1,0:T(8,128)S(1)}, u32[]{:S(2)}, u32[]{:S(2)}) %collective-permute-start.6) | collective-permute-done | bytes 40992 | tf_op jit(solution)/shard_map/ppermute | solution.py:321
  45.8 0.6 %copy-done.5 = f32[16,640]{1,0:T(8,128)} copy-done((f32[16,640]{1,0:T(8,128)}, f32[16,640]{1,0:T(8,128)S(1)}, u32[]{:S(2)}) %copy-start.5) | copy-done | bytes 40984
  46.4 2.9 %shard_map.75 = (f32[3,16,512]{2,1,0:T(8,128)}, f32[6,32,512]{2,1,0:T(8,128)}) custom-call(s32[1]{0:T(128)} %bitcast.start_ref, f32[48,640]{1,0:T(8,128)} %get-tuple-element.28.sum_ref, f32[16,640]{1,0:T(8,128)} %copy-done.5, f32[16,640]{1,0:T(8,128)} %copy-done.6, f32[48,640]{1,0:T(8,128)} %get-tuple-element.31.q_ref, ...), custom_call_target="tpu_custom_call" | custom-call | tf_op jit(solution)/shard_map/pallas_call | solution.py:243
  (16 shorter events, 1.8 us)
Async XLA Ops:
  4.1 1.6 %collective-permute-start = (f32[96,128]{1,0:T(8,128)}, f32[96,128]{1,0:T(8,128)S(1)}, u32[]{:S(2)}, u32[]{:S(2)}) collective-permute-start(f32[96,128]{1,0:T(8,128)} %get-tuple-element.18), channel_id=1, source_target_pairs={{0,2},{2,0},{1,3},{3,1},{4,6},{6,4},{5,7},{7,5},{8,10},{10,8},{9,1... | collective-permute-start | bytes 147464 | tf_op jit(solution)/shard_map/ppermute | solution.py:260
  5.7 0.6 %copy-start = (f32[96,128]{1,0:T(8,128)}, f32[96,128]{1,0:T(8,128)S(1)}, u32[]{:S(2)}) copy-start(f32[96,128]{1,0:T(8,128)S(1)} %collective-permute-done.edge_ref) | copy-start | bytes 147460
  7.9 6.7 %collective-permute-start.1 = (f32[48,640]{1,0:T(8,128)}, f32[48,640]{1,0:T(8,128)S(1)}, u32[]{:S(2)}, u32[]{:S(2)}) collective-permute-start(f32[48,640]{1,0:T(8,128)} %shard_map.69.part_ref), channel_id=1, source_target_pairs={{0,1},{1,0},{2,3},{3,2},{4,5},{5,4},{6,7},{7,6},{8,9},{9,8},{10,11... | collective-permute-start | bytes 368648 | tf_op jit(solution)/shard_map/ppermute | solution.py:260
  14.6 0.6 %copy-start.1 = (f32[48,640]{1,0:T(8,128)}, f32[48,640]{1,0:T(8,128)S(1)}, u32[]{:S(2)}) copy-start(f32[48,640]{1,0:T(8,128)S(1)} %collective-permute-done.1.other_ref) | copy-start | bytes 368644
  17.0 6.8 %collective-permute-start.2 = (f32[24,640]{1,0:T(8,128)}, f32[24,640]{1,0:T(8,128)S(1)}, u32[]{:S(2)}, u32[]{:S(2)}) collective-permute-start(f32[24,640]{1,0:T(8,128)} %get-tuple-element.21), channel_id=1, source_target_pairs={{12,0},{0,4},{4,8},{8,12},{13,1},{1,5},{5,9},{9,13},{14,2},{2,6},{... | collective-permute-start | bytes 184328 | tf_op jit(solution)/shard_map/ppermute | solution.py:321
  18.9 5.1 %collective-permute-start.3 = (f32[24,640]{1,0:T(8,128)}, f32[24,640]{1,0:T(8,128)S(1)}, u32[]{:S(2)}, u32[]{:S(2)}) collective-permute-start(f32[24,640]{1,0:T(8,128)} %get-tuple-element.22), channel_id=1, source_target_pairs={{0,12},{4,0},{8,4},{12,8},{1,13},{5,1},{9,5},{13,9},{2,14},{6,2},{... | collective-permute-start | bytes 184328 | tf_op jit(solution)/shard_map/ppermute | solution.py:320
  23.9 0.6 %copy-start.3 = (f32[24,640]{1,0:T(8,128)}, f32[24,640]{1,0:T(8,128)S(1)}, u32[]{:S(2)}) copy-start(f32[24,640]{1,0:T(8,128)S(1)} %collective-permute-done.2.above_ref) | copy-start | bytes 184324
  24.0 0.6 %copy-start.4 = (f32[24,640]{1,0:T(8,128)}, f32[24,640]{1,0:T(8,128)S(1)}, u32[]{:S(2)}) copy-start(f32[24,640]{1,0:T(8,128)S(1)} %collective-permute-done.3.below_ref) | copy-start | bytes 184324
  28.2 1.4 %collective-permute-start.4 = (f32[48,128]{1,0:T(8,128)}, f32[48,128]{1,0:T(8,128)S(1)}, u32[]{:S(2)}, u32[]{:S(2)}) collective-permute-start(f32[48,128]{1,0:T(8,128)} %get-tuple-element.27), channel_id=1, source_target_pairs={{0,2},{2,0},{1,3},{3,1},{4,6},{6,4},{5,7},{7,5},{8,10},{10,8},{9,1... | collective-permute-start | bytes 73736 | tf_op jit(solution)/shard_map/ppermute | solution.py:260
  29.6 0.6 %copy-start.7 = (f32[48,128]{1,0:T(8,128)}, f32[48,128]{1,0:T(8,128)S(1)}, u32[]{:S(2)}) copy-start(f32[48,128]{1,0:T(8,128)S(1)} %collective-permute-done.4.edge_ref) | copy-start | bytes 73732
  31.8 5.6 %collective-permute-start.5 = (f32[48,640]{1,0:T(8,128)}, f32[48,640]{1,0:T(8,128)S(1)}, u32[]{:S(2)}, u32[]{:S(2)}) collective-permute-start(f32[48,640]{1,0:T(8,128)} %shard_map.73.a), channel_id=1, source_target_pairs={{0,1},{1,0},{2,3},{3,2},{4,5},{5,4},{6,7},{7,6},{8,9},{9,8},{10,11... | collective-permute-start | bytes 368648 | tf_op jit(solution)/shard_map/ppermute | solution.py:260
  37.4 0.6 %copy-start.2 = (f32[48,640]{1,0:T(8,128)}, f32[48,640]{1,0:T(8,128)S(1)}, u32[]{:S(2)}) copy-start(f32[48,640]{1,0:T(8,128)S(1)} %collective-permute-done.5.b) | copy-start | bytes 368644
  39.7 6.0 %collective-permute-start.6 = (f32[16,640]{1,0:T(8,128)}, f32[16,640]{1,0:T(8,128)S(1)}, u32[]{:S(2)}, u32[]{:S(2)}) collective-permute-start(f32[16,640]{1,0:T(8,128)} %get-tuple-element.29), channel_id=1, source_target_pairs={{12,0},{0,4},{4,8},{8,12},{13,1},{1,5},{5,9},{9,13},{14,2},{2,6},{... | collective-permute-start | bytes 122888 | tf_op jit(solution)/shard_map/ppermute | solution.py:321
  40.7 5.0 %collective-permute-start.7 = (f32[16,640]{1,0:T(8,128)}, f32[16,640]{1,0:T(8,128)S(1)}, u32[]{:S(2)}, u32[]{:S(2)}) collective-permute-start(f32[16,640]{1,0:T(8,128)} %get-tuple-element.30), channel_id=1, source_target_pairs={{0,12},{4,0},{8,4},{12,8},{1,13},{5,1},{9,5},{13,9},{2,14},{6,2},{... | collective-permute-start | bytes 122888 | tf_op jit(solution)/shard_map/ppermute | solution.py:320
  45.8 0.6 %copy-start.5 = (f32[16,640]{1,0:T(8,128)}, f32[16,640]{1,0:T(8,128)S(1)}, u32[]{:S(2)}) copy-start(f32[16,640]{1,0:T(8,128)S(1)} %collective-permute-done.6.above_ref) | copy-start | bytes 122884
  45.8 0.6 %copy-start.6 = (f32[16,640]{1,0:T(8,128)}, f32[16,640]{1,0:T(8,128)S(1)}, u32[]{:S(2)}) copy-start(f32[16,640]{1,0:T(8,128)S(1)} %collective-permute-done.7.below_ref) | copy-start | bytes 122884

commit v2 on v1

--- a/solution.py
+++ b/solution.py
@@ -14,6 +14,7 @@
 FULL = 64
 SHIFTS = 16
 WIDE = 256
+GRANT = 16 * 2**20
 
 f32 = jnp.float32
 bf16 = jnp.bfloat16
@@ -122,15 +123,33 @@
 
 
 def first_kernel(
-    labels_ref, background_ref, contrasts_ref, k_ref, observed_ref,
+    labels_hbm, background_hbm, contrasts_hbm, k_hbm, observed_hbm,
     part_ref, edge_ref, q_ref, density_ref, bands_ref,
+    labels_ref, background_ref, contrasts_ref, k_ref, observed_ref, sems,
     base_ref, rows_ref, wide_ref, prod_ref, obs_ref,
 ):
     layers, cells_x, cells_y = labels_ref.shape
     span = k_ref.shape[1]
+    copies = [
+        pltpu.make_async_copy(source, target, sems.at[n])
+        for n, (source, target) in enumerate(
+            (
+                (k_hbm, k_ref),
+                (labels_hbm, labels_ref),
+                (background_hbm, background_ref),
+                (contrasts_hbm, contrasts_ref),
+                (observed_hbm, observed_ref),
+            )
+        )
+    ]
+    for copy in copies:
+        copy.start()
+    copies[0].wait()
     build_bands(k_ref, base_ref, rows_ref, wide_ref)
     bands = wide_ref[...].astype(bf16)
     bands_ref[...] = bands
+    for copy in copies[1:]:
+        copy.wait()
     classes = contrasts_ref.shape[0]
     for l in range(layers):
         label = labels_ref[l]
@@ -235,17 +254,23 @@
         gradient_ref[l] = gradient[l * cells_x : (l + 1) * cells_x, :]
 
 
-def call(kernel, outs, scratch=(), scalars=0, smem=()):
+def call(kernel, outs, scratch=(), inputs=pltpu.VMEM, smem=()):
     vmem = pl.BlockSpec(memory_space=pltpu.VMEM)
+    given = pl.BlockSpec(memory_space=inputs)
     scalar = pl.BlockSpec(memory_space=pltpu.SMEM)
 
     def run(*operands):
+        if inputs is pltpu.HBM:
+            operands = [pltpu.with_memory_space_constraint(v, pltpu.HBM) for v in operands]
         return pl.pallas_call(
             kernel,
             out_shape=outs,
-            in_specs=[scalar if i in smem else vmem for i in range(len(operands))],
+            in_specs=[scalar if i in smem else given for i in range(len(operands))],
             out_specs=jax.tree.map(lambda _: vmem, outs),
-            scratch_shapes=[pltpu.VMEM(shape, kind) for shape, kind in scratch],
+            scratch_shapes=[
+                item if not isinstance(item, tuple) else pltpu.VMEM(*item) for item in scratch
+            ],
+            compiler_params=pltpu.CompilerParams(vmem_limit_bytes=GRANT),
         )(*operands)
 
     return run
@@ -285,13 +310,19 @@
             shaped((span * PART, WIDE), bf16),
         ),
         (
+            (labels.shape, labels.dtype),
+            (background.shape, background.dtype),
+            pltpu.SMEM(contrasts.shape, contrasts.dtype),
+            (kernels.shape, kernels.dtype),
+            (observed.shape, observed.dtype),
+            pltpu.SemaphoreType.DMA((5,)),
             ((span, WIDE), f32),
             ((span * 8, WIDE), f32),
             ((span * PART, WIDE), f32),
             prod,
             ((3, PART, width), f32),
         ),
-        smem=(2,),
+        inputs=pltpu.HBM,
     )(labels, background, contrasts, kernels, observed)
     turned = call(transpose_kernel, shaped((WIDE, span * PART), bf16))(bands)
     start = (lax.axis_index("gz") * share).astype(jnp.int32).reshape(1)

time: 49.6 us -> 34 us (0.69)
  Pallas kernels: 18.6 us -> 6.14 us
  local copies, waits for them, and re-layouts: 3.77 us -> 0.01 us
    pallas_call x8, Pallas kernels: 18.6 us -> 6.14 us  [run(): pl.pallas_call(kernel, out_shape=outs, in_specs=[scalar if i in smem else...]
    unnamed x16 -> x2, local copies, waits for them, and re-layouts: 3.77 us -> 0.01 us
    ppermute x2, waiting for transfers between devices: 3.3 us -> 4.55 us  [body(): above = lax.ppermute(down, 'gx', downward)]
    ppermute x4, waiting for transfers between devices: 10.3 us -> 9.43 us  [swap(): return lax.ppermute(value, axis, [(i, i ^ distance) for i in range(peers)])]
  transfers between devices with their start and end apart: 8 -> 8, of which waited for: 7 -> 7; matrix products, arithmetic and copies ran while one was open for 0% -> 0% of each run, Pallas kernels for 4% -> 0%
where the time goes in v2:
time: 34 us; the launch traced here: 33.9 us
  waiting for transfers between devices  14 us (41%)
  starting transfers between devices  13 us (38%)
  Pallas kernels  6.14 us (18%)
  between operations  0.66 us (2%)
    ppermute x4, waiting for transfers between devices, swap(): return lax.ppermute(value, axis, [(i, i ^ distance) for i in range(peers)])  9.43 us
    pallas_call x8, Pallas kernels, run(): pl.pallas_call(kernel, out_shape=outs, in_specs=[scalar if i in smem else...  6.14 us
    ppermute x4, starting transfers between devices, swap(): return lax.ppermute(value, axis, [(i, i ^ distance) for i in range(peers)])  5.18 us
    ppermute x2, starting transfers between devices, body(): below = lax.ppermute(up, 'gx', upward)  4.88 us
    ppermute x2, waiting for transfers between devices, body(): above = lax.ppermute(down, 'gx', downward)  4.55 us
    ppermute x2, starting transfers between devices, body(): above = lax.ppermute(down, 'gx', downward)  2.96 us
  transfers between devices with their start and end apart: 8, of which 7 were waited for; matrix products, arithmetic and copies ran while one was open for 0% of the time, Pallas kernels for 0%

profile of v2, /device:TPU:0, one launch (start us, length us, event | category | flops | bytes accessed | tf_op | source)
XLA Modules:
  0.0 33.9 jit_solution(16451778891159988904)
XLA Ops:
  0.6 2.4 %shard_map.68 = (f32[48,640]{1,0:T(8,128)S(1)}, f32[96,128]{1,0:T(8,128)S(1)}, f32[48,640]{1,0:T(8,128)S(1)}, f32[192,512]{1,0:T(8,128)S(1)}, bf16[720,256]{1,0:T(8,128)(2,1)S(1)}) custom-call(s32[6,32,512]{2,1,0:T(8,128)} %labels_hbm.1, bf16[6,32,512]{2,1,0:T(8,128)(2,1)} %background_hbm.1, f32[4]{0:T(128)} %contrasts_hbm.1, bf16[6,15,15]{2,1,0:T(8,128)(2,1)} %k_hbm.1, ...), custom_call_target="tpu_custom_call" | custom-call | tf_op jit(solution)/shard_map/pallas_call | solution.py:265
  3.1 0.6 %collective-permute-start = (f32[96,128]{1,0:T(8,128)S(1)}, f32[96,128]{1,0:T(8,128)S(1)}, u32[]{:S(2)}, u32[]{:S(2)}) collective-permute-start(f32[96,128]{1,0:T(8,128)S(1)} %get-tuple-element.18), channel_id=1, source_target_pairs={{0,2},{2,0},{1,3},{3,1},{4,6},{6,4},{5,7},{7,5},{8,10},{10,8},{9,1... | collective-permute-start | bytes 147464 | tf_op jit(solution)/shard_map/ppermute | solution.py:285
  3.6 0.9 %collective-permute-done.edge_ref = f32[96,128]{1,0:T(8,128)S(1)} collective-permute-done((f32[96,128]{1,0:T(8,128)S(1)}, f32[96,128]{1,0:T(8,128)S(1)}, u32[]{:S(2)}, u32[]{:S(2)}) %collective-permute-start) | collective-permute-done | bytes 49184 | tf_op jit(solution)/shard_map/ppermute | solution.py:285
  4.5 0.1 shard_map.69.part_ref
  4.6 2.8 %collective-permute-start.1 = (f32[48,640]{1,0:T(8,128)S(1)}, f32[48,640]{1,0:T(8,128)S(1)}, u32[]{:S(2)}, u32[]{:S(2)}) collective-permute-start(f32[48,640]{1,0:T(8,128)S(1)} %shard_map.69.part_ref), channel_id=1, source_target_pairs={{0,1},{1,0},{2,3},{3,2},{4,5},{5,4},{6,7},{7,6},{8,9},{9,8},{10,11... | collective-permute-start | bytes 368648 | tf_op jit(solution)/shard_map/ppermute | solution.py:285
  7.4 3.6 %collective-permute-done.1.other_ref = f32[48,640]{1,0:T(8,128)S(1)} collective-permute-done((f32[48,640]{1,0:T(8,128)S(1)}, f32[48,640]{1,0:T(8,128)S(1)}, u32[]{:S(2)}, u32[]{:S(2)}) %collective-permute-start.1) | collective-permute-done | bytes 122912 | tf_op jit(solution)/shard_map/ppermute | solution.py:285
  11.1 0.1 shard_map.70
  11.2 1.9 %collective-permute-start.2 = (f32[24,640]{1,0:T(8,128)S(1)}, f32[24,640]{1,0:T(8,128)S(1)}, u32[]{:S(2)}, u32[]{:S(2)}) collective-permute-start(f32[24,640]{1,0:T(8,128)S(1)} %get-tuple-element.21), channel_id=1, source_target_pairs={{12,0},{0,4},{4,8},{8,12},{13,1},{1,5},{5,9},{9,13},{14,2},{2,6},{... | collective-permute-start | bytes 184328 | tf_op jit(solution)/shard_map/ppermute | solution.py:352
  13.0 2.1 %collective-permute-start.3 = (f32[24,640]{1,0:T(8,128)S(1)}, f32[24,640]{1,0:T(8,128)S(1)}, u32[]{:S(2)}, u32[]{:S(2)}) collective-permute-start(f32[24,640]{1,0:T(8,128)S(1)} %get-tuple-element.22), channel_id=1, source_target_pairs={{0,12},{4,0},{8,4},{12,8},{1,13},{5,1},{9,5},{13,9},{2,14},{6,2},{... | collective-permute-start | bytes 184328 | tf_op jit(solution)/shard_map/ppermute | solution.py:351
  15.1 0.2 shard_map.71.turned_ref
  15.3 2.5 %collective-permute-done.2.above_ref = f32[24,640]{1,0:T(8,128)S(1)} collective-permute-done((f32[24,640]{1,0:T(8,128)S(1)}, f32[24,640]{1,0:T(8,128)S(1)}, u32[]{:S(2)}, u32[]{:S(2)}) %collective-permute-start.2) | collective-permute-done | bytes 61472 | tf_op jit(solution)/shard_map/ppermute | solution.py:352
  17.9 0.1 collective-permute-done.3.below_ref
  17.9 1.5 %shard_map.72 = (f32[48,640]{1,0:T(8,128)S(1)}, f32[48,128]{1,0:T(8,128)S(1)}, f32[48,640]{1,0:T(8,128)S(1)}) custom-call(f32[48,640]{1,0:T(8,128)S(1)} %get-tuple-element.20.sum_ref, f32[24,640]{1,0:T(8,128)S(1)} %collective-permute-done.2.above_ref, f32[24,640]{1,0:T(8,128)S(1)} %collective-permute-done.3.below_ref, ...), custom_call_target="tpu_custom_call" | custom-call | tf_op jit(solution)/shard_map/pallas_call | solution.py:265
  19.4 0.1 collective-permute-start.4
  19.5 1.2 %collective-permute-done.4.edge_ref = f32[48,128]{1,0:T(8,128)S(1)} collective-permute-done((f32[48,128]{1,0:T(8,128)S(1)}, f32[48,128]{1,0:T(8,128)S(1)}, u32[]{:S(2)}, u32[]{:S(2)}) %collective-permute-start.4) | collective-permute-done | bytes 24608 | tf_op jit(solution)/shard_map/ppermute | solution.py:285
  20.7 0.1 shard_map.73.a
  20.8 1.7 %collective-permute-start.5 = (f32[48,640]{1,0:T(8,128)S(1)}, f32[48,640]{1,0:T(8,128)S(1)}, u32[]{:S(2)}, u32[]{:S(2)}) collective-permute-start(f32[48,640]{1,0:T(8,128)S(1)} %shard_map.73.a), channel_id=1, source_target_pairs={{0,1},{1,0},{2,3},{3,2},{4,5},{5,4},{6,7},{7,6},{8,9},{9,8},{10,11... | collective-permute-start | bytes 368648 | tf_op jit(solution)/shard_map/ppermute | solution.py:285
  22.5 3.7 %collective-permute-done.5.b = f32[48,640]{1,0:T(8,128)S(1)} collective-permute-done((f32[48,640]{1,0:T(8,128)S(1)}, f32[48,640]{1,0:T(8,128)S(1)}, u32[]{:S(2)}, u32[]{:S(2)}) %collective-permute-start.5) | collective-permute-done | bytes 122912 | tf_op jit(solution)/shard_map/ppermute | solution.py:285
  26.3 1.1 %collective-permute-start.6 = (f32[16,640]{1,0:T(8,128)S(1)}, f32[16,640]{1,0:T(8,128)S(1)}, u32[]{:S(2)}, u32[]{:S(2)}) collective-permute-start(f32[16,640]{1,0:T(8,128)S(1)} %get-tuple-element.29), channel_id=1, source_target_pairs={{12,0},{0,4},{4,8},{8,12},{13,1},{1,5},{5,9},{9,13},{14,2},{2,6},{... | collective-permute-start | bytes 122888 | tf_op jit(solution)/shard_map/ppermute | solution.py:352
  27.3 2.8 %collective-permute-start.7 = (f32[16,640]{1,0:T(8,128)S(1)}, f32[16,640]{1,0:T(8,128)S(1)}, u32[]{:S(2)}, u32[]{:S(2)}) collective-permute-start(f32[16,640]{1,0:T(8,128)S(1)} %get-tuple-element.30), channel_id=1, source_target_pairs={{0,12},{4,0},{8,4},{12,8},{1,13},{5,1},{9,5},{13,9},{2,14},{6,2},{... | collective-permute-start | bytes 122888 | tf_op jit(solution)/shard_map/ppermute | solution.py:351
  30.1 2.0 %collective-permute-done.6.above_ref = f32[16,640]{1,0:T(8,128)S(1)} collective-permute-done((f32[16,640]{1,0:T(8,128)S(1)}, f32[16,640]{1,0:T(8,128)S(1)}, u32[]{:S(2)}, u32[]{:S(2)}) %collective-permute-start.6) | collective-permute-done | bytes 40992 | tf_op jit(solution)/shard_map/ppermute | solution.py:352
  32.1 0.0 collective-permute-done.7.below_ref
  32.1 0.0 copy-done
  32.1 1.7 %shard_map.75 = (f32[3,16,512]{2,1,0:T(8,128)}, f32[6,32,512]{2,1,0:T(8,128)}) custom-call(s32[1]{0:T(128)} %bitcast.start_ref, f32[48,640]{1,0:T(8,128)S(1)} %get-tuple-element.28.sum_ref, f32[16,640]{1,0:T(8,128)S(1)} %collective-permute-done.6.above_ref, f32[16,640]{1,0:T(8,128)S(1)} %collective-permute-done.7.below_ref, ...), custom_call_target="tpu_custom_call" | custom-call | tf_op jit(solution)/shard_map/pallas_call | solution.py:265
  (2 shorter events, 0.0 us)
Async XLA Ops:
  3.1 1.4 %collective-permute-start = (f32[96,128]{1,0:T(8,128)S(1)}, f32[96,128]{1,0:T(8,128)S(1)}, u32[]{:S(2)}, u32[]{:S(2)}) collective-permute-start(f32[96,128]{1,0:T(8,128)S(1)} %get-tuple-element.18), channel_id=1, source_target_pairs={{0,2},{2,0},{1,3},{3,1},{4,6},{6,4},{5,7},{7,5},{8,10},{10,8},{9,1... | collective-permute-start | bytes 147464 | tf_op jit(solution)/shard_map/ppermute | solution.py:285
  4.6 6.5 %collective-permute-start.1 = (f32[48,640]{1,0:T(8,128)S(1)}, f32[48,640]{1,0:T(8,128)S(1)}, u32[]{:S(2)}, u32[]{:S(2)}) collective-permute-start(f32[48,640]{1,0:T(8,128)S(1)} %shard_map.69.part_ref), channel_id=1, source_target_pairs={{0,1},{1,0},{2,3},{3,2},{4,5},{5,4},{6,7},{7,6},{8,9},{9,8},{10,11... | collective-permute-start | bytes 368648 | tf_op jit(solution)/shard_map/ppermute | solution.py:285
  11.2 6.7 %collective-permute-start.2 = (f32[24,640]{1,0:T(8,128)S(1)}, f32[24,640]{1,0:T(8,128)S(1)}, u32[]{:S(2)}, u32[]{:S(2)}) collective-permute-start(f32[24,640]{1,0:T(8,128)S(1)} %get-tuple-element.21), channel_id=1, source_target_pairs={{12,0},{0,4},{4,8},{8,12},{13,1},{1,5},{5,9},{9,13},{14,2},{2,6},{... | collective-permute-start | bytes 184328 | tf_op jit(solution)/shard_map/ppermute | solution.py:352
  13.0 4.9 %collective-permute-start.3 = (f32[24,640]{1,0:T(8,128)S(1)}, f32[24,640]{1,0:T(8,128)S(1)}, u32[]{:S(2)}, u32[]{:S(2)}) collective-permute-start(f32[24,640]{1,0:T(8,128)S(1)} %get-tuple-element.22), channel_id=1, source_target_pairs={{0,12},{4,0},{8,4},{12,8},{1,13},{5,1},{9,5},{13,9},{2,14},{6,2},{... | collective-permute-start | bytes 184328 | tf_op jit(solution)/shard_map/ppermute | solution.py:351
  19.4 1.3 %collective-permute-start.4 = (f32[48,128]{1,0:T(8,128)S(1)}, f32[48,128]{1,0:T(8,128)S(1)}, u32[]{:S(2)}, u32[]{:S(2)}) collective-permute-start(f32[48,128]{1,0:T(8,128)S(1)} %get-tuple-element.27), channel_id=1, source_target_pairs={{0,2},{2,0},{1,3},{3,1},{4,6},{6,4},{5,7},{7,5},{8,10},{10,8},{9,1... | collective-permute-start | bytes 73736 | tf_op jit(solution)/shard_map/ppermute | solution.py:285
  20.8 11.4 %copy-start = (f32[3,32,512]{2,1,0:T(8,128)S(1)}, f32[3,32,512]{2,1,0:T(8,128)}, u32[]{:S(2)}) copy-start(f32[3,32,512]{2,1,0:T(8,128)} %observed_ref.1) | copy-start | bytes 589828
  20.8 5.4 %collective-permute-start.5 = (f32[48,640]{1,0:T(8,128)S(1)}, f32[48,640]{1,0:T(8,128)S(1)}, u32[]{:S(2)}, u32[]{:S(2)}) collective-permute-start(f32[48,640]{1,0:T(8,128)S(1)} %shard_map.73.a), channel_id=1, source_target_pairs={{0,1},{1,0},{2,3},{3,2},{4,5},{5,4},{6,7},{7,6},{8,9},{9,8},{10,11... | collective-permute-start | bytes 368648 | tf_op jit(solution)/shard_map/ppermute | solution.py:285
  26.3 5.9 %collective-permute-start.6 = (f32[16,640]{1,0:T(8,128)S(1)}, f32[16,640]{1,0:T(8,128)S(1)}, u32[]{:S(2)}, u32[]{:S(2)}) collective-permute-start(f32[16,640]{1,0:T(8,128)S(1)} %get-tuple-element.29), channel_id=1, source_target_pairs={{12,0},{0,4},{4,8},{8,12},{13,1},{1,5},{5,9},{9,13},{14,2},{2,6},{... | collective-permute-start | bytes 122888 | tf_op jit(solution)/shard_map/ppermute | solution.py:352
  27.3 4.8 %collective-permute-start.7 = (f32[16,640]{1,0:T(8,128)S(1)}, f32[16,640]{1,0:T(8,128)S(1)}, u32[]{:S(2)}, u32[]{:S(2)}) collective-permute-start(f32[16,640]{1,0:T(8,128)S(1)} %get-tuple-element.30), channel_id=1, source_target_pairs={{0,12},{4,0},{8,4},{12,8},{1,13},{5,1},{9,5},{13,9},{2,14},{6,2},{... | collective-permute-start | bytes 122888 | tf_op jit(solution)/shard_map/ppermute | solution.py:351

commit v3 on v2

--- a/solution.py
+++ b/solution.py
@@ -11,8 +11,8 @@
 descent = 0.01
 ITERS = 2
 PART = 48
+EDGE = 9
 FULL = 64
-SHIFTS = 16
 WIDE = 256
 GRANT = 16 * 2**20
 
@@ -110,23 +110,62 @@
             bands_ref[j * PART + 8 * g : j * PART + 8 * g + 8, :] = moved[8 * j : 8 * j + 8]
 
 
-def scatter_surface(bands, rounded, prod_ref, span, radius):
-    cells_y = rounded.shape[1]
-    prod_ref[...] = jnp.dot(bands, rounded, preferred_element_type=f32)
-    total = jnp.zeros((PART, cells_y + 128), f32)
+def outer_columns(v):
+    return jnp.concatenate([v[:, :128], v[:, v.shape[1] - 128 :]], axis=1)
+
+
+def edge_product(outer_ref, span, radius):
+    total = jnp.zeros((PART, 384), f32)
     side = jnp.zeros((PART, 128), f32)
     for j in range(span):
-        piece = jnp.concatenate([prod_ref[j * PART : (j + 1) * PART, :], side], axis=1)
-        shift = (radius - j) % (cells_y + 128)
+        rows = outer_ref[j * PART : (j + 1) * PART, :]
+        piece = jnp.concatenate([rows[:, 128:], side, rows[:, :128]], axis=1)
+        shift = (radius - j) % 384
+        total = total + (pltpu.roll(piece, shift, 1) if shift else piece)
+    return edge_message(
+        jnp.concatenate([total[:, 256:], total[:, :128], total[:, 128:256]], axis=1)
+    )
+
+
+def scatter_surface(bands, inner, outer_ref, prod_ref, span, radius):
+    prod_ref[...] = jnp.dot(bands, inner, preferred_element_type=f32)
+    width = inner.shape[1] + 384
+    total = jnp.zeros((PART, width), f32)
+    side = jnp.zeros((PART, 128), f32)
+    for j in range(span):
+        rows = slice(j * PART, (j + 1) * PART)
+        piece = jnp.concatenate(
+            [outer_ref[rows, :128], prod_ref[rows, :], outer_ref[rows, 128:], side], axis=1
+        )
+        shift = (radius - j) % width
         total = total + (pltpu.roll(piece, shift, 1) if shift else piece)
     return total
 
 
+def fold_side(side):
+    lane = iota((8, 128), 1)
+    turned = pltpu.roll(side, EDGE, 1)
+    folded = jnp.zeros((8, 128), f32)
+    for g in range(PART // 8):
+        piece = jnp.where(lane < 2 * EDGE, turned[8 * g : 8 * g + 8], 0.0)
+        folded = folded + (pltpu.roll(piece, 2 * EDGE * g, 1) if g else piece)
+    return folded
+
+
+def unfold_side(folded):
+    lane = iota((8, 128), 1)
+    pieces = []
+    for g in range(PART // 8):
+        piece = pltpu.roll(folded, 128 - 2 * EDGE * g, 1) if g else folded
+        pieces.append(jnp.where(lane < 2 * EDGE, piece, 0.0))
+    return pltpu.roll(jnp.concatenate(pieces, axis=0), 128 - EDGE, 1)
+
+
 def first_kernel(
     labels_hbm, background_hbm, contrasts_hbm, k_hbm, observed_hbm,
-    part_ref, edge_ref, q_ref, density_ref, bands_ref,
+    edge_ref, q_ref, density_ref, bands_ref, outer_ref,
     labels_ref, background_ref, contrasts_ref, k_ref, observed_ref, sems,
-    base_ref, rows_ref, wide_ref, prod_ref, obs_ref,
+    base_ref, rows_ref, wide_ref, obs_ref,
 ):
     layers, cells_x, cells_y = labels_ref.shape
     span = k_ref.shape[1]
@@ -157,11 +196,11 @@
         for c in range(1, classes):
             value = jnp.where(label == c, contrasts_ref[c], value)
         density_ref[l * cells_x : (l + 1) * cells_x, :] = value + background_ref[l].astype(f32)
-    rounded = density_ref[...].astype(bf16)
-    bands_x = bands[:, : layers * cells_x]
-    part = scatter_surface(bands_x, rounded, prod_ref, span, (span - 1) // 2)
-    part_ref[...] = part
-    edge_ref[:PART, :] = edge_message(part)
+    rounded = outer_columns(density_ref[...]).astype(bf16)
+    outer_ref[...] = jnp.dot(
+        bands[:, : layers * cells_x], rounded, preferred_element_type=f32
+    )
+    edge_ref[:PART, :] = edge_product(outer_ref, span, (span - 1) // 2)
     obs_ref[...] = jnp.zeros(obs_ref.shape, f32)
     for k in range(3):
         obs_ref[k, 8 : 8 + cells_x, :cells_y] = observed_ref[k]
@@ -174,12 +213,36 @@
     out_ref[...] = bands_ref[...].astype(f32).T.astype(bf16)
 
 
+def inner_kernel(density_ref, bands_ref, outer_ref, part_ref, prod_ref, *, span):
+    lanes, cells_y = density_ref.shape
+    rounded = density_ref[:, 128 : cells_y - 128].astype(bf16)
+    part_ref[...] = scatter_surface(
+        bands_ref[:, :lanes], rounded, outer_ref, prod_ref, span, (span - 1) // 2
+    )
+
+
 def edges_kernel(part_ref, edge_ref, out_ref):
-    out_ref[...] = add_edges(part_ref[...], edge_ref[: part_ref.shape[0], :])
-
-
-def rows_kernel(part_ref, other_ref, q_ref, edge_ref, sum_ref, up_ref, down_ref, q_out_ref):
-    sum_ref[...] = part_ref[...] + other_ref[...]
+    cells_y = out_ref.shape[1]
+    part = add_edges(part_ref[...], edge_ref[:PART, :])
+    out_ref[...] = part[:, :cells_y]
+    folded = fold_side(part[:, cells_y:])
+    for n in range(8):
+        row = (PART - 1) * (n // 4)
+        out_ref[row : row + 1, 128 * (n % 4) : 128 * (n % 4 + 1)] = folded[n : n + 1]
+
+
+def rows_kernel(
+    part_ref, other_ref, q_ref, edge_ref, sum_ref, up_ref, down_ref, q_out_ref, fold_ref
+):
+    cells_y = part_ref.shape[1]
+    sum_ref[:, :cells_y] = part_ref[...] + other_ref[...]
+    for n in range(8):
+        row = (PART - 1) * (n // 4)
+        fold_ref[n : n + 1, :] = sum_ref[row : row + 1, 128 * (n % 4) : 128 * (n % 4 + 1)]
+    sum_ref[:, cells_y:] = unfold_side(fold_ref[...])
+    zero = jnp.zeros((1, cells_y), f32)
+    sum_ref[:1, :cells_y] = zero
+    sum_ref[PART - 1 :, :cells_y] = zero
     up_ref[:16, :] = sum_ref[1:17, :]
     down_ref[:16, :] = sum_ref[31:47, :]
     if q_ref is not None:
@@ -198,41 +261,62 @@
     return full_ref[...]
 
 
-def gradient_of(adjoint, turned, stack_ref, span, radius):
-    cells_y = stack_ref.shape[1]
+def stack_shifts(adjoint, stack_ref, columns, span, radius):
     for j in range(span):
         shift = (j - radius) % adjoint.shape[1]
         moved = pltpu.roll(adjoint, shift, 1) if shift else adjoint
-        stack_ref[j * PART : (j + 1) * PART, :] = moved[:, :cells_y].astype(bf16)
-    return jnp.dot(turned, stack_ref[...], preferred_element_type=f32)
+        stack_ref[j * PART : (j + 1) * PART, :] = columns(moved).astype(bf16)
 
 
 def middle_kernel(
     sum_ref, above_ref, below_ref, q_ref, density_ref, bands_ref, turned_ref,
-    part_ref, edge_ref, q_out_ref,
-    full_ref, stack_ref, prod_ref, *, span,
+    edge_ref, q_out_ref, adjoint_ref, outer_ref,
+    full_ref, stack_ref, *, span,
 ):
     radius = (span - 1) // 2
-    lanes = density_ref.shape[0]
+    lanes, cells_y = density_ref.shape
     q_out_ref[...] = q_ref[...]
     q_out_ref[1:9, :] = q_out_ref[1:9, :] + above_ref[16:24, :]
     q_out_ref[39:47, :] = q_out_ref[39:47, :] + below_ref[16:24, :]
     s = full_surface(sum_ref, above_ref, below_ref, full_ref)
     adjoint = adjoint_of(*tensor_fields(s))[8:56] - q_out_ref[...]
-    adjoint = adjoint.astype(bf16).astype(f32)
-    gradient = gradient_of(adjoint, turned_ref[:lanes, :], stack_ref, span, radius)
-    density = density_ref[...] - descent * gradient
-    part = scatter_surface(
-        bands_ref[:, :lanes], density.astype(bf16), prod_ref, span, radius
-    )
-    part_ref[...] = part
-    edge_ref[...] = edge_message(part)
+    adjoint_ref[...] = adjoint.astype(bf16).astype(f32)
+    stack_shifts(
+        adjoint_ref[...], stack_ref, lambda v: outer_columns(v[:, :cells_y]), span, radius
+    )
+    gradient = jnp.dot(turned_ref[:lanes, :], stack_ref[...], preferred_element_type=f32)
+    density = outer_columns(density_ref[...]) - descent * gradient
+    outer_ref[...] = jnp.dot(
+        bands_ref[:, :lanes], density.astype(bf16), preferred_element_type=f32
+    )
+    edge_ref[...] = edge_product(outer_ref, span, radius)
+
+
+def middle_inner_kernel(
+    adjoint_ref, density_ref, bands_ref, turned_ref, outer_ref,
+    part_ref,
+    stack_ref, prod_ref, *, span,
+):
+    radius = (span - 1) // 2
+    lanes, cells_y = density_ref.shape
+    stack_shifts(
+        adjoint_ref[:, :cells_y],
+        stack_ref,
+        lambda v: v[:, 128 : cells_y - 128],
+        span,
+        radius,
+    )
+    gradient = jnp.dot(turned_ref[:lanes, :], stack_ref[...], preferred_element_type=f32)
+    density = density_ref[:, 128 : cells_y - 128] - descent * gradient
+    part_ref[...] = scatter_surface(
+        bands_ref[:, :lanes], density.astype(bf16), outer_ref, prod_ref, span, radius
+    )
 
 
 def last_kernel(
     start_ref, sum_ref, above_ref, below_ref, q_ref, turned_ref, observed_ref,
-    residual_ref, gradient_ref,
-    full_ref, stack_ref, misfit_ref, *, span,
+    residual_hbm, gradient_hbm,
+    residual_ref, gradient_ref, sems, full_ref, stack_ref, misfit_ref, *, span,
 ):
     radius = (span - 1) // 2
     layers, cells_x, cells_y = gradient_ref.shape
@@ -249,13 +333,27 @@
         def _():
             residual_ref[...] = misfit_ref[:, start : start + share, :]
 
-    gradient = gradient_of(adjoint, turned_ref[: layers * cells_x, :], stack_ref, span, radius)
-    for l in range(layers):
-        gradient_ref[l] = gradient[l * cells_x : (l + 1) * cells_x, :]
-
-
-def call(kernel, outs, scratch=(), inputs=pltpu.VMEM, smem=()):
-    vmem = pl.BlockSpec(memory_space=pltpu.VMEM)
+    copies = [pltpu.make_async_copy(residual_ref, residual_hbm, sems.at[0])]
+    copies[0].start()
+    stack_shifts(adjoint, stack_ref, lambda v: v[:, :cells_y], span, radius)
+    turned = turned_ref[: layers * cells_x, :]
+    half = cells_y // 2
+    for n in range(2):
+        columns = slice(n * half, (n + 1) * half)
+        gradient = jnp.dot(turned, stack_ref[:, columns], preferred_element_type=f32)
+        for l in range(layers):
+            gradient_ref[l, :, columns] = gradient[l * cells_x : (l + 1) * cells_x, :]
+        copy = pltpu.make_async_copy(
+            gradient_ref.at[:, :, columns], gradient_hbm.at[:, :, columns], sems.at[1 + n]
+        )
+        copy.start()
+        copies.append(copy)
+    for copy in copies:
+        copy.wait()
+
+
+def call(kernel, outs, scratch=(), inputs=pltpu.VMEM, smem=(), results=pltpu.VMEM):
+    made = pl.BlockSpec(memory_space=results)
     given = pl.BlockSpec(memory_space=inputs)
     scalar = pl.BlockSpec(memory_space=pltpu.SMEM)
 
@@ -266,7 +364,7 @@
             kernel,
             out_shape=outs,
             in_specs=[scalar if i in smem else given for i in range(len(operands))],
-            out_specs=jax.tree.map(lambda _: vmem, outs),
+            out_specs=jax.tree.map(lambda _: made, outs),
             scratch_shapes=[
                 item if not isinstance(item, tuple) else pltpu.VMEM(*item) for item in scratch
             ],
@@ -291,23 +389,28 @@
     lanes = layers * cells_x
     width = cells_y + 128
     depth_peers, row_peers = lax.axis_size("gz"), lax.axis_size("gx")
-    assert cells_x == 32 and span == 15 and lanes <= 192 and lax.axis_size("gy") == 2
+    assert cells_x == 32 and span == 15 and lanes <= 192 and cells_y == 512 and lax.axis_size("gy") == 2
     assert depth_peers & (depth_peers - 1) == 0
     share = cells_x // depth_peers
     upward = [(i, (i - 1) % row_peers) for i in range(row_peers)]
     downward = [(j, i) for i, j in upward]
-    stack = ((span * PART, cells_y), bf16)
-    prod = ((span * PART, cells_y), f32)
+    half = cells_y - 256
     full = ((FULL, width), f32)
-
-    part, edge, q, density, bands = call(
+    outer = shaped((span * PART, 256))
+    inner = ((span * PART, half), f32)
+    field = shaped((PART, width))
+
+    def kernel_of(body_of):
+        return functools.partial(body_of, span=span)
+
+    edge, q, density, bands, outer_product = call(
         first_kernel,
         (
-            shaped((PART, width)),
             shaped((2 * PART, 128)),
-            shaped((PART, width)),
+            field,
             shaped((lanes, cells_y)),
             shaped((span * PART, WIDE), bf16),
+            outer,
         ),
         (
             (labels.shape, labels.dtype),
@@ -319,48 +422,57 @@
             ((span, WIDE), f32),
             ((span * 8, WIDE), f32),
             ((span * PART, WIDE), f32),
-            prod,
             ((3, PART, width), f32),
         ),
         inputs=pltpu.HBM,
     )(labels, background, contrasts, kernels, observed)
+    part = call(kernel_of(inner_kernel), field, (inner,))(density, bands, outer_product)
     turned = call(transpose_kernel, shaped((WIDE, span * PART), bf16))(bands)
     start = (lax.axis_index("gz") * share).astype(jnp.int32).reshape(1)
 
     for iteration in range(ITERS):
         others = swap(edge, "gy", 1)
-        part = call(edges_kernel, shaped((PART, width)))(part, others)
+        part = call(edges_kernel, shaped((PART, cells_y)))(part, others)
         for bit in range(depth_peers.bit_length() - 2):
             part = part + swap(part, "gz", 2 << bit)
         other = swap(part, "gz", 1)
+        fold = (((8, 128), f32),)
         if iteration == 0:
             total, up, down, q = call(
-                rows_kernel,
-                (
-                    shaped((PART, width)),
-                    shaped((24, width)),
-                    shaped((24, width)),
-                    shaped((PART, width)),
-                ),
+                rows_kernel, (field, shaped((24, width)), shaped((24, width)), field), fold
             )(part, other, q, others)
         else:
             total, up, down = call(
-                lambda a, b, c, d, e: rows_kernel(a, b, None, None, c, d, e, None),
-                (shaped((PART, width)), shaped((16, width)), shaped((16, width))),
+                lambda a, b, c, d, e, g: rows_kernel(a, b, None, None, c, d, e, None, g),
+                (field, shaped((16, width)), shaped((16, width))),
+                fold,
             )(part, other)
         below = lax.ppermute(up, "gx", upward)
         above = lax.ppermute(down, "gx", downward)
         if iteration == 0:
-            part, edge, q = call(
-                functools.partial(middle_kernel, span=span),
-                (shaped((PART, width)), shaped((PART, 128)), shaped((PART, width))),
-                (full, stack, prod),
+            edge, q, adjoint, outer_product = call(
+                kernel_of(middle_kernel),
+                (shaped((PART, 128)), field, field, outer),
+                (full, ((span * PART, 256), bf16)),
             )(total, above, below, q, density, bands, turned)
+            part = call(
+                kernel_of(middle_inner_kernel),
+                field,
+                (((span * PART, half), bf16), inner),
+            )(adjoint, density, bands, turned, outer_product)
     return call(
-        functools.partial(last_kernel, span=span),
+        kernel_of(last_kernel),
         (shaped((3, share, cells_y)), shaped((layers, cells_x, cells_y))),
-        (full, stack, ((3, cells_x, cells_y), f32)),
+        (
+            ((3, share, cells_y), f32),
+            ((layers, cells_x, cells_y), f32),
+            pltpu.SemaphoreType.DMA((3,)),
+            full,
+            ((span * PART, cells_y), bf16),
+            ((3, cells_x, cells_y), f32),
+        ),
         smem=(0,),
+        results=pltpu.HBM,
     )(start, total, above, below, q, turned, observed)
 
 

time: 34 us -> 32.8 us (0.965)
  waiting for transfers between devices: 14 us -> 11.7 us
  Pallas kernels: 6.14 us -> 7.24 us
    ppermute x4, waiting for transfers between devices: 9.43 us -> 7.08 us  [swap(): return lax.ppermute(value, axis, [(i, i ^ distance) for i in range(peers)])]
    pallas_call x8 -> x10, Pallas kernels: 6.14 us -> 7.24 us  [run(): pl.pallas_call(kernel, out_shape=outs, in_specs=[scalar if i in smem else...]
  transfers between devices with their start and end apart: 8 -> 8, of which waited for: 7 -> 7; matrix products, arithmetic and copies ran while one was open for 0% -> 0% of each run, Pallas kernels for 0% -> 4%
where the time goes in v3:
time: 32.8 us; the launch traced here: 32.6 us
  starting transfers between devices  13 us (40%)
  waiting for transfers between devices  11.7 us (36%)
  Pallas kernels  7.24 us (22%)
  between operations  0.69 us (2%)
    pallas_call x10, Pallas kernels, run(): pl.pallas_call(kernel, out_shape=outs, in_specs=[scalar if i in smem else...  7.24 us
    ppermute x4, waiting for transfers between devices, swap(): return lax.ppermute(value, axis, [(i, i ^ distance) for i in range(peers)])  7.08 us
    ppermute x4, starting transfers between devices, swap(): return lax.ppermute(value, axis, [(i, i ^ distance) for i in range(peers)])  5.22 us
    ppermute x2, starting transfers between devices, body(): below = lax.ppermute(up, 'gx', upward)  4.88 us
    ppermute x2, waiting for transfers between devices, body(): above = lax.ppermute(down, 'gx', downward)  4.55 us
    ppermute x2, starting transfers between devices, body(): above = lax.ppermute(down, 'gx', downward)  2.91 us
  transfers between devices with their start and end apart: 8, of which 7 were waited for; matrix products, arithmetic and copies ran while one was open for 0% of the time, Pallas kernels for 4%

profile of v3, /device:TPU:0, one launch (start us, length us, event | category | flops | bytes accessed | tf_op | source)
XLA Modules:
  0.0 32.6 jit_solution(16191129688703598309)
XLA Ops:
  0.6 2.2 %shard_map.68 = (f32[96,128]{1,0:T(8,128)S(1)}, f32[48,640]{1,0:T(8,128)S(1)}, f32[192,512]{1,0:T(8,128)S(1)}, bf16[720,256]{1,0:T(8,128)(2,1)S(1)}, f32[720,256]{1,0:T(8,128)S(1)}) custom-call(s32[6,32,512]{2,1,0:T(8,128)} %labels_hbm.1, bf16[6,32,512]{2,1,0:T(8,128)(2,1)} %background_hbm.1, f32[4]{0:T(128)} %contrasts_hbm.1, bf16[6,15,15]{2,1,0:T(8,128)(2,1)} %k_hbm.1, ...), custom_call_target="tpu_custom_call" | custom-call | tf_op jit(solution)/shard_map/pallas_call | solution.py:363
  2.8 0.6 %collective-permute-start = (f32[96,128]{1,0:T(8,128)S(1)}, f32[96,128]{1,0:T(8,128)S(1)}, u32[]{:S(2)}, u32[]{:S(2)}) collective-permute-start(f32[96,128]{1,0:T(8,128)S(1)} %get-tuple-element.21), channel_id=1, source_target_pairs={{0,2},{2,0},{1,3},{3,1},{4,6},{6,4},{5,7},{7,5},{8,10},{10,8},{9,1... | collective-permute-start | bytes 147464 | tf_op jit(solution)/shard_map/ppermute | solution.py:383
  3.4 0.5 %shard_map.69.part_ref = f32[48,640]{1,0:T(8,128)S(1)} custom-call(f32[192,512]{1,0:T(8,128)S(1)} %get-tuple-element.18.density_ref, bf16[720,256]{1,0:T(8,128)(2,1)S(1)} %get-tuple-element.19.bands_ref, f32[720,256]{1,0:T(8,128)S(1)} %get-tuple-element.20.outer_ref), custom_call_target="tpu_custom_call" | custom-call | tf_op jit(solution)/shard_map/pallas_call | solution.py:363
  3.9 0.4 %collective-permute-done.edge_ref = f32[96,128]{1,0:T(8,128)S(1)} collective-permute-done((f32[96,128]{1,0:T(8,128)S(1)}, f32[96,128]{1,0:T(8,128)S(1)}, u32[]{:S(2)}, u32[]{:S(2)}) %collective-permute-start) | collective-permute-done | bytes 49184 | tf_op jit(solution)/shard_map/ppermute | solution.py:383
  4.2 0.1 shard_map.70.part_ref
  4.4 2.9 %collective-permute-start.1 = (f32[48,512]{1,0:T(8,128)S(1)}, f32[48,512]{1,0:T(8,128)S(1)}, u32[]{:S(2)}, u32[]{:S(2)}) collective-permute-start(f32[48,512]{1,0:T(8,128)S(1)} %shard_map.70.part_ref), channel_id=1, source_target_pairs={{0,1},{1,0},{2,3},{3,2},{4,5},{5,4},{6,7},{7,6},{8,9},{9,8},{10,11... | collective-permute-start | bytes 294920 | tf_op jit(solution)/shard_map/ppermute | solution.py:383
  7.3 3.1 %collective-permute-done.1.other_ref = f32[48,512]{1,0:T(8,128)S(1)} collective-permute-done((f32[48,512]{1,0:T(8,128)S(1)}, f32[48,512]{1,0:T(8,128)S(1)}, u32[]{:S(2)}, u32[]{:S(2)}) %collective-permute-start.1) | collective-permute-done | bytes 98336 | tf_op jit(solution)/shard_map/ppermute | solution.py:383
  10.4 0.2 shard_map.71
  10.5 1.9 %collective-permute-start.2 = (f32[24,640]{1,0:T(8,128)S(1)}, f32[24,640]{1,0:T(8,128)S(1)}, u32[]{:S(2)}, u32[]{:S(2)}) collective-permute-start(f32[24,640]{1,0:T(8,128)S(1)} %get-tuple-element.24), channel_id=1, source_target_pairs={{12,0},{0,4},{4,8},{8,12},{13,1},{1,5},{5,9},{9,13},{14,2},{2,6},{... | collective-permute-start | bytes 184328 | tf_op jit(solution)/shard_map/ppermute | solution.py:451
  12.4 2.1 %collective-permute-start.3 = (f32[24,640]{1,0:T(8,128)S(1)}, f32[24,640]{1,0:T(8,128)S(1)}, u32[]{:S(2)}, u32[]{:S(2)}) collective-permute-start(f32[24,640]{1,0:T(8,128)S(1)} %get-tuple-element.25), channel_id=1, source_target_pairs={{0,12},{4,0},{8,4},{12,8},{1,13},{5,1},{9,5},{13,9},{2,14},{6,2},{... | collective-permute-start | bytes 184328 | tf_op jit(solution)/shard_map/ppermute | solution.py:450
  14.5 0.2 shard_map.72.turned_ref
  14.7 2.5 %collective-permute-done.2.above_ref = f32[24,640]{1,0:T(8,128)S(1)} collective-permute-done((f32[24,640]{1,0:T(8,128)S(1)}, f32[24,640]{1,0:T(8,128)S(1)}, u32[]{:S(2)}, u32[]{:S(2)}) %collective-permute-start.2) | collective-permute-done | bytes 61472 | tf_op jit(solution)/shard_map/ppermute | solution.py:451
  17.3 1.3 %shard_map.73 = (f32[48,128]{1,0:T(8,128)S(1)}, f32[48,640]{1,0:T(8,128)S(1)}, f32[48,640]{1,0:T(8,128)S(1)}, f32[720,256]{1,0:T(8,128)S(1)}) custom-call(f32[48,640]{1,0:T(8,128)S(1)} %get-tuple-element.23.sum_ref, f32[24,640]{1,0:T(8,128)S(1)} %collective-permute-done.2.above_ref, f32[24,640]{1,0:T(8,128)S(1)} %collective-permute-done.3.below_ref, ...), custom_call_target="tpu_custom_call" | custom-call | tf_op jit(solution)/shard_map/pallas_call | solution.py:363
  18.6 0.1 collective-permute-start.4
  18.7 0.8 %shard_map.74.part_ref = f32[48,640]{1,0:T(8,128)S(1)} custom-call(f32[48,640]{1,0:T(8,128)S(1)} %get-tuple-element.27.adjoint_ref, f32[192,512]{1,0:T(8,128)S(1)} %get-tuple-element.18.density_ref, bf16[720,256]{1,0:T(8,128)(2,1)S(1)} %get-tuple-element.19.bands_ref, bf16[256,720]{1,0:T(8,128)(2,1)S(1)} %shard_map.72.turned_ref, ...), custom_call_target="tpu_custom_call" | custom-call | tf_op jit(solution)/shard_map/pallas_call | solution.py:363
  19.4 0.4 %collective-permute-done.4.edge_ref = f32[48,128]{1,0:T(8,128)S(1)} collective-permute-done((f32[48,128]{1,0:T(8,128)S(1)}, f32[48,128]{1,0:T(8,128)S(1)}, u32[]{:S(2)}, u32[]{:S(2)}) %collective-permute-start.4) | collective-permute-done | bytes 24608 | tf_op jit(solution)/shard_map/ppermute | solution.py:383
  19.8 0.1 shard_map.75.a
  20.0 1.7 %collective-permute-start.5 = (f32[48,512]{1,0:T(8,128)S(1)}, f32[48,512]{1,0:T(8,128)S(1)}, u32[]{:S(2)}, u32[]{:S(2)}) collective-permute-start(f32[48,512]{1,0:T(8,128)S(1)} %shard_map.75.a), channel_id=1, source_target_pairs={{0,1},{1,0},{2,3},{3,2},{4,5},{5,4},{6,7},{7,6},{8,9},{9,8},{10,11... | collective-permute-start | bytes 294920 | tf_op jit(solution)/shard_map/ppermute | solution.py:383
  21.7 3.2 %collective-permute-done.5.b = f32[48,512]{1,0:T(8,128)S(1)} collective-permute-done((f32[48,512]{1,0:T(8,128)S(1)}, f32[48,512]{1,0:T(8,128)S(1)}, u32[]{:S(2)}, u32[]{:S(2)}) %collective-permute-start.5) | collective-permute-done | bytes 98336 | tf_op jit(solution)/shard_map/ppermute | solution.py:383
  24.9 0.2 shard_map.76
  25.1 1.0 %collective-permute-start.6 = (f32[16,640]{1,0:T(8,128)S(1)}, f32[16,640]{1,0:T(8,128)S(1)}, u32[]{:S(2)}, u32[]{:S(2)}) collective-permute-start(f32[16,640]{1,0:T(8,128)S(1)} %get-tuple-element.31), channel_id=1, source_target_pairs={{12,0},{0,4},{4,8},{8,12},{13,1},{1,5},{5,9},{9,13},{14,2},{2,6},{... | collective-permute-start | bytes 122888 | tf_op jit(solution)/shard_map/ppermute | solution.py:451
  26.1 2.8 %collective-permute-start.7 = (f32[16,640]{1,0:T(8,128)S(1)}, f32[16,640]{1,0:T(8,128)S(1)}, u32[]{:S(2)}, u32[]{:S(2)}) collective-permute-start(f32[16,640]{1,0:T(8,128)S(1)} %get-tuple-element.32), channel_id=1, source_target_pairs={{0,12},{4,0},{8,4},{12,8},{1,13},{5,1},{9,5},{13,9},{2,14},{6,2},{... | collective-permute-start | bytes 122888 | tf_op jit(solution)/shard_map/ppermute | solution.py:450
  28.9 2.0 %collective-permute-done.6.above_ref = f32[16,640]{1,0:T(8,128)S(1)} collective-permute-done((f32[16,640]{1,0:T(8,128)S(1)}, f32[16,640]{1,0:T(8,128)S(1)}, u32[]{:S(2)}, u32[]{:S(2)}) %collective-permute-start.6) | collective-permute-done | bytes 40992 | tf_op jit(solution)/shard_map/ppermute | solution.py:451
  30.9 1.7 %shard_map.77 = (f32[3,16,512]{2,1,0:T(8,128)}, f32[6,32,512]{2,1,0:T(8,128)}) custom-call(s32[1]{0:T(128)} %bitcast.start_ref, f32[48,640]{1,0:T(8,128)S(1)} %get-tuple-element.30.sum_ref, f32[16,640]{1,0:T(8,128)S(1)} %collective-permute-done.6.above_ref, f32[16,640]{1,0:T(8,128)S(1)} %collective-permute-done.7.below_ref, ...), custom_call_target="tpu_custom_call" | custom-call | tf_op jit(solution)/shard_map/pallas_call | solution.py:363
  (4 shorter events, 0.1 us)
Async XLA Ops:
  2.8 1.4 %collective-permute-start = (f32[96,128]{1,0:T(8,128)S(1)}, f32[96,128]{1,0:T(8,128)S(1)}, u32[]{:S(2)}, u32[]{:S(2)}) collective-permute-start(f32[96,128]{1,0:T(8,128)S(1)} %get-tuple-element.21), channel_id=1, source_target_pairs={{0,2},{2,0},{1,3},{3,1},{4,6},{6,4},{5,7},{7,5},{8,10},{10,8},{9,1... | collective-permute-start | bytes 147464 | tf_op jit(solution)/shard_map/ppermute | solution.py:383
  4.4 6.0 %collective-permute-start.1 = (f32[48,512]{1,0:T(8,128)S(1)}, f32[48,512]{1,0:T(8,128)S(1)}, u32[]{:S(2)}, u32[]{:S(2)}) collective-permute-start(f32[48,512]{1,0:T(8,128)S(1)} %shard_map.70.part_ref), channel_id=1, source_target_pairs={{0,1},{1,0},{2,3},{3,2},{4,5},{5,4},{6,7},{7,6},{8,9},{9,8},{10,11... | collective-permute-start | bytes 294920 | tf_op jit(solution)/shard_map/ppermute | solution.py:383
  10.5 6.7 %collective-permute-start.2 = (f32[24,640]{1,0:T(8,128)S(1)}, f32[24,640]{1,0:T(8,128)S(1)}, u32[]{:S(2)}, u32[]{:S(2)}) collective-permute-start(f32[24,640]{1,0:T(8,128)S(1)} %get-tuple-element.24), channel_id=1, source_target_pairs={{12,0},{0,4},{4,8},{8,12},{13,1},{1,5},{5,9},{9,13},{14,2},{2,6},{... | collective-permute-start | bytes 184328 | tf_op jit(solution)/shard_map/ppermute | solution.py:451
  12.4 4.9 %collective-permute-start.3 = (f32[24,640]{1,0:T(8,128)S(1)}, f32[24,640]{1,0:T(8,128)S(1)}, u32[]{:S(2)}, u32[]{:S(2)}) collective-permute-start(f32[24,640]{1,0:T(8,128)S(1)} %get-tuple-element.25), channel_id=1, source_target_pairs={{0,12},{4,0},{8,4},{12,8},{1,13},{5,1},{9,5},{13,9},{2,14},{6,2},{... | collective-permute-start | bytes 184328 | tf_op jit(solution)/shard_map/ppermute | solution.py:450
  18.6 1.3 %collective-permute-start.4 = (f32[48,128]{1,0:T(8,128)S(1)}, f32[48,128]{1,0:T(8,128)S(1)}, u32[]{:S(2)}, u32[]{:S(2)}) collective-permute-start(f32[48,128]{1,0:T(8,128)S(1)} %get-tuple-element.29), channel_id=1, source_target_pairs={{0,2},{2,0},{1,3},{3,1},{4,6},{6,4},{5,7},{7,5},{8,10},{10,8},{9,1... | collective-permute-start | bytes 73736 | tf_op jit(solution)/shard_map/ppermute | solution.py:383
  19.4 11.5 %copy-start = (f32[3,32,512]{2,1,0:T(8,128)S(1)}, f32[3,32,512]{2,1,0:T(8,128)}, u32[]{:S(2)}) copy-start(f32[3,32,512]{2,1,0:T(8,128)} %observed_ref.1) | copy-start | bytes 589828
  20.0 4.9 %collective-permute-start.5 = (f32[48,512]{1,0:T(8,128)S(1)}, f32[48,512]{1,0:T(8,128)S(1)}, u32[]{:S(2)}, u32[]{:S(2)}) collective-permute-start(f32[48,512]{1,0:T(8,128)S(1)} %shard_map.75.a), channel_id=1, source_target_pairs={{0,1},{1,0},{2,3},{3,2},{4,5},{5,4},{6,7},{7,6},{8,9},{9,8},{10,11... | collective-permute-start | bytes 294920 | tf_op jit(solution)/shard_map/ppermute | solution.py:383
  25.1 5.8 %collective-permute-start.6 = (f32[16,640]{1,0:T(8,128)S(1)}, f32[16,640]{1,0:T(8,128)S(1)}, u32[]{:S(2)}, u32[]{:S(2)}) collective-permute-start(f32[16,640]{1,0:T(8,128)S(1)} %get-tuple-element.31), channel_id=1, source_target_pairs={{12,0},{0,4},{4,8},{8,12},{13,1},{1,5},{5,9},{9,13},{14,2},{2,6},{... | collective-permute-start | bytes 122888 | tf_op jit(solution)/shard_map/ppermute | solution.py:451
  26.1 4.8 %collective-permute-start.7 = (f32[16,640]{1,0:T(8,128)S(1)}, f32[16,640]{1,0:T(8,128)S(1)}, u32[]{:S(2)}, u32[]{:S(2)}) collective-permute-start(f32[16,640]{1,0:T(8,128)S(1)} %get-tuple-element.32), channel_id=1, source_target_pairs={{0,12},{4,0},{8,4},{12,8},{1,13},{5,1},{9,5},{13,9},{2,14},{6,2},{... | collective-permute-start | bytes 122888 | tf_op jit(solution)/shard_map/ppermute | solution.py:450

commit v4 on v3

v4 whole, which is shorter than its diff:
```python
import functools

import jax
import jax.numpy as jnp
from jax import lax
from jax.experimental import pallas as pl
from jax.experimental.pallas import tpu as pltpu
from jax.sharding import PartitionSpec as P


descent = 0.01
ITERS = 2
PART = 48
EDGE = 9
FULL = 64
WIDE = 256
GRANT = 16 * 2**20

f32 = jnp.float32
bf16 = jnp.bfloat16


def iota(shape, dim):
    return lax.broadcasted_iota(jnp.int32, shape, dim)


def up_rows(v):
    return pltpu.roll(v, v.shape[0] - 1, 0)


def down_rows(v):
    return pltpu.roll(v, 1, 0)


def right(v):
    return pltpu.roll(v, v.shape[1] - 1, 1)


def left(v):
    return pltpu.roll(v, 1, 1)


def tensor_fields(s):
    above, below = up_rows(s), down_rows(s)
    along_x = above + below - 2.0 * s
    along_y = right(s) + left(s) - 2.0 * s
    diff = above - below
    mixed = 0.25 * (right(diff) - left(diff))
    return along_x, along_y, mixed


def adjoint_of(r0, r1, r2):
    cross = 0.25 * (right(r2) - left(r2))
    return (
        up_rows(r0 + cross)
        + down_rows(r0 - cross)
        - 2.0 * r0
        + right(r1)
        + left(r1)
        - 2.0 * r1
    )


def adjoint_square(s):
    def row(k):
        return pltpu.roll(s, -k % FULL, 0)[8 : 8 + PART]

    def column(v, k):
        return pltpu.roll(v, -k % v.shape[1], 1)

    centre = s[8 : 8 + PART]
    near, far = row(1) + row(-1), row(2) + row(-2)
    mixed = 0.0625 * (far - 2.0 * centre)
    both = centre + mixed
    return (
        (far - 4.0 * near + 12.0 * centre - 2.0 * mixed)
        + (column(both, 2) + column(both, -2))
        - 4.0 * (column(centre, 1) + column(centre, -1))
    )


def edge_columns(first, last, side=None):
    lane = iota(first.shape, 1)
    inside = jnp.where(lane < 64, pltpu.roll(first, 32, 1), last)
    if side is None:
        return jnp.where(lane < 32, jnp.zeros_like(first), inside)
    outside = jnp.where(lane < 16, side, pltpu.roll(side, 32, 1))
    return jnp.where(lane < 32, outside, inside)


def edges_of(v):
    width = v.shape[1]
    return edge_columns(v[:, :128], v[:, width - 256 : width - 128], v[:, width - 128 :])


def add_edges(field, message):
    width = field.shape[1]
    lane = iota(message.shape, 1)
    turned = pltpu.roll(message, 96, 1)
    zero = jnp.zeros_like(message)
    first = field[:, :128] + jnp.where(lane < EDGE, message, zero)
    last = field[:, width - 256 : width - 128] + jnp.where(lane >= 128 - EDGE, turned, zero)
    side = field[:, width - 128 :] + jnp.where(
        lane < EDGE, turned, jnp.where(lane >= 128 - EDGE, message, zero)
    )
    return jnp.concatenate([first, field[:, 128 : width - 256], last, side], axis=1)


def build_bands(k_ref, taps_ref, base_ref, bands_ref):
    layers, span, _ = k_ref.shape
    taps_ref[...] = jnp.zeros(taps_ref.shape, f32)
    for l in range(layers):
        taps_ref[16 * l : 16 * l + span, :span] = k_ref[l].astype(f32)
    shape = (taps_ref.shape[0], WIDE)
    source = iota(shape, 0)
    place = jnp.where(32 * (source >> 4) + (source & 15) == iota(shape, 1), 1.0, 0.0)
    base_ref[...] = lax.dot_general(
        taps_ref[...].astype(bf16),
        place.astype(bf16),
        (((0,), (0,)), ((), ())),
        preferred_element_type=f32,
    )
    tap = (iota((8, 128), 1) & 31) - iota((8, 128), 0) + 15
    keep = [(tap - 8 * g >= 0) & (tap - 8 * g < span) for g in range(PART // 8)]
    for block in range(WIDE // 128):
        columns = slice(128 * block, 128 * block + 128)
        for j in range(span):
            row = jnp.broadcast_to(base_ref[j : j + 1, columns], (8, 128))
            moved = [
                jnp.where(
                    keep[g],
                    pltpu.roll(row, (8 * g - 15) % 128, 1, stride=1, stride_axis=0),
                    0.0,
                )
                for g in range(PART // 8)
            ]
            bands_ref[j * PART : (j + 1) * PART, columns] = jnp.concatenate(
                moved, axis=0
            ).astype(bf16)


def edge_message(bands, rounded, prod_ref, span, radius):
    prod_ref[...] = jnp.dot(bands, rounded, preferred_element_type=f32)
    total = prod_ref[radius * PART : (radius + 1) * PART, :]
    for j in range(span):
        if j != radius:
            piece = prod_ref[j * PART : (j + 1) * PART, :]
            total = total + pltpu.roll(piece, (radius - j) % 128, 1)
    return total


def scatter_surface(bands, rounded, prod_ref, span, radius):
    width = rounded.shape[1] + 128
    prod_ref[...] = jnp.dot(bands, rounded, preferred_element_type=f32)
    total = jnp.zeros((PART, width), f32)
    side = jnp.zeros((PART, 128), f32)
    for j in range(span):
        piece = jnp.concatenate([prod_ref[j * PART : (j + 1) * PART, :], side], axis=1)
        shift = (radius - j) % width
        total = total + (pltpu.roll(piece, shift, 1) if shift else piece)
    return total


def fold_side(side):
    lane = iota((8, 128), 1)
    turned = pltpu.roll(side, EDGE, 1)
    folded = jnp.zeros((8, 128), f32)
    for g in range(PART // 8):
        piece = jnp.where(lane < 2 * EDGE, turned[8 * g : 8 * g + 8], 0.0)
        folded = folded + (pltpu.roll(piece, 2 * EDGE * g, 1) if g else piece)
    return folded


def unfold_side(folded):
    lane = iota((8, 128), 1)
    pieces = []
    for g in range(PART // 8):
        piece = pltpu.roll(folded, 128 - 2 * EDGE * g, 1) if g else folded
        pieces.append(jnp.where(lane < 2 * EDGE, piece, 0.0))
    return pltpu.roll(jnp.concatenate(pieces, axis=0), 128 - EDGE, 1)


def first_kernel(
    labels_hbm, background_hbm, contrasts_hbm, k_hbm, observed_hbm,
    edge_ref, density_edge_ref, density_ref, bands_ref, observed_ref,
    labels_ref, background_ref, contrasts_ref, k_ref, sems,
    taps_ref, base_ref, prod_ref,
):
    layers, cells_x, cells_y = labels_ref.shape
    span = k_ref.shape[1]
    copies = [
        pltpu.make_async_copy(source, target, sems.at[n])
        for n, (source, target) in enumerate(
            (
                (k_hbm, k_ref),
                (contrasts_hbm, contrasts_ref),
                (labels_hbm, labels_ref),
                (background_hbm, background_ref),
                (observed_hbm, observed_ref),
            )
        )
    ]
    for copy in copies:
        copy.start()
    copies[0].wait()
    build_bands(k_ref, taps_ref, base_ref, bands_ref)
    for copy in copies[1:]:
        copy.wait()
    classes = contrasts_ref.shape[0]
    for l in range(layers):
        label = labels_ref[l]
        value = jnp.full(label.shape, contrasts_ref[0], f32)
        for c in range(1, classes):
            value = jnp.where(label == c, contrasts_ref[c], value)
        density = value + background_ref[l].astype(f32)
        rows = slice(l * cells_x, (l + 1) * cells_x)
        density_ref[rows, :] = density
        density_edge_ref[rows, :] = edge_columns(density[:, :128], density[:, cells_y - 128 :])
    edge_ref[:PART, :] = edge_message(
        bands_ref[:, : layers * cells_x],
        density_edge_ref[...].astype(bf16),
        prod_ref,
        span,
        (span - 1) // 2,
    )
    empty = jnp.zeros((8, 128), f32)
    edge_ref[PART:, :] = adjoint_of(
        *(
            jnp.concatenate(
                [
                    empty,
                    edge_columns(observed_ref[k, :, :128], observed_ref[k, :, cells_y - 128 :]),
                    empty,
                ],
                axis=0,
            )
            for k in range(3)
        )
    )


def first_field_kernel(
    density_ref, bands_ref, observed_ref, part_ref, q_ref, prod_ref, obs_ref, *, span
):
    lanes, cells_y = density_ref.shape
    part_ref[...] = scatter_surface(
        bands_ref[:, :lanes], density_ref[...].astype(bf16), prod_ref, span, (span - 1) // 2
    )
    obs_ref[...] = jnp.zeros(obs_ref.shape, f32)
    for k in range(3):
        obs_ref[k, 8 : PART - 8, :cells_y] = observed_ref[k]
    q_ref[...] = adjoint_of(obs_ref[0], obs_ref[1], obs_ref[2])


def transpose_kernel(bands_ref, out_ref):
    out_ref[...] = bands_ref[...].astype(f32).T.astype(bf16)


def edges_kernel(part_ref, edge_ref, out_ref):
    cells_y = out_ref.shape[1]
    part = add_edges(part_ref[...], edge_ref[:PART, :])
    out_ref[...] = part[:, :cells_y]
    folded = fold_side(part[:, cells_y:])
    for n in range(8):
        row = (PART - 1) * (n // 4)
        out_ref[row : row + 1, 128 * (n % 4) : 128 * (n % 4 + 1)] = folded[n : n + 1]


def rows_kernel(
    part_ref, other_ref, q_ref, edge_ref, sum_ref, up_ref, down_ref, q_out_ref, fold_ref
):
    cells_y = part_ref.shape[1]
    sum_ref[:, :cells_y] = part_ref[...] + other_ref[...]
    for n in range(8):
        row = (PART - 1) * (n // 4)
        fold_ref[n : n + 1, :] = sum_ref[row : row + 1, 128 * (n % 4) : 128 * (n % 4 + 1)]
    sum_ref[:, cells_y:] = unfold_side(fold_ref[...])
    zero = jnp.zeros((1, cells_y), f32)
    sum_ref[:1, :cells_y] = zero
    sum_ref[PART - 1 :, :cells_y] = zero
    sub = iota((8, sum_ref.shape[1]), 0)
    up_ref[:8, :] = sum_ref[8:16, :]
    up_ref[8:16, :] = jnp.where(sub >= 1, sum_ref[:8, :], sum_ref[16:24, :])
    down_ref[:8, :] = sum_ref[32:40, :]
    down_ref[8:16, :] = jnp.where(sub < 7, sum_ref[40:48, :], sum_ref[24:32, :])
    if q_ref is not None:
        q_out_ref[...] = add_edges(q_ref[...], edge_ref[PART:, :])
        up_ref[16:24, :] = jnp.where(sub < 7, q_out_ref[8:16, :], q_out_ref[:8, :])
        down_ref[16:24, :] = jnp.where(sub >= 1, q_out_ref[32:40, :], q_out_ref[40:48, :])


def full_surface(total, above, below):
    shape = (8, total.shape[1])
    sub = iota(shape, 0)
    zero = jnp.zeros(shape, f32)
    return jnp.concatenate(
        [
            jnp.where(sub == 7, above[8:16], zero),
            total[:8] + above[:8],
            total[8:16] + jnp.where(sub < 7, above[8:16], zero),
            total[16:32],
            total[32:40] + jnp.where(sub >= 1, below[8:16], zero),
            total[40:48] + below[:8],
            jnp.where(sub == 0, below[8:16], zero),
        ],
        axis=0,
    )


def full_q(q, above, below):
    shape = (8, q.shape[1])
    sub = iota(shape, 0)
    zero = jnp.zeros(shape, f32)
    return jnp.concatenate(
        [
            q[:8] + jnp.where(sub >= 1, above[16:24], zero),
            q[8:16] + jnp.where(sub == 0, above[16:24], zero),
            q[16:32],
            q[32:40] + jnp.where(sub == 7, below[16:24], zero),
            q[40:48] + jnp.where(sub < 7, below[16:24], zero),
        ],
        axis=0,
    )


def stack_shifts(adjoint, stack_ref, columns, span, radius):
    for j in range(span):
        shift = (j - radius) % adjoint.shape[1]
        moved = pltpu.roll(adjoint, shift, 1) if shift else adjoint
        stack_ref[j * PART : (j + 1) * PART, columns] = moved[:, columns].astype(bf16)


def rounded_adjoint(s, q):
    return (adjoint_square(s) - q).astype(bf16).astype(f32)


def middle_kernel(
    sum_ref, above_ref, below_ref, q_ref, density_edge_ref, bands_ref, turned_ref,
    edge_ref,
    stack_ref, prod_ref, *, span,
):
    radius = (span - 1) // 2
    lanes = density_edge_ref.shape[0]
    total, q = edges_of(sum_ref[...]), edges_of(q_ref[...])
    above, below = edges_of(above_ref[...]), edges_of(below_ref[...])
    adjoint = rounded_adjoint(full_surface(total, above, below), full_q(q, above, below))
    stack_shifts(adjoint, stack_ref, slice(0, 128), span, radius)
    gradient = jnp.dot(turned_ref[:lanes, :], stack_ref[...], preferred_element_type=f32)
    density = density_edge_ref[...] - descent * gradient
    lane = iota(density.shape, 1)
    keep = ((lane >= 32) & (lane < 48)) | (lane >= 112)
    density = jnp.where(keep, density, 0.0)
    edge_ref[...] = edge_message(
        bands_ref[:, :lanes], density.astype(bf16), prod_ref, span, radius
    )


def middle_field_kernel(
    sum_ref, above_ref, below_ref, q_ref, density_ref, bands_ref, turned_ref,
    part_ref, q_out_ref,
    stack_ref, prod_ref, *, span,
):
    radius = (span - 1) // 2
    lanes, cells_y = density_ref.shape
    above, below = above_ref[...], below_ref[...]
    q = full_q(q_ref[...], above, below)
    q_out_ref[...] = q
    adjoint = rounded_adjoint(full_surface(sum_ref[...], above, below), q)
    stack_shifts(adjoint, stack_ref, slice(0, cells_y), span, radius)
    gradient = jnp.dot(turned_ref[:lanes, :], stack_ref[...], preferred_element_type=f32)
    density = density_ref[...] - descent * gradient
    part_ref[...] = scatter_surface(
        bands_ref[:, :lanes], density.astype(bf16), prod_ref, span, radius
    )


def last_kernel(
    start_ref, sum_ref, above_ref, below_ref, q_ref, turned_ref, observed_ref,
    residual_hbm, gradient_hbm,
    residual_ref, gradient_ref, sems, full_ref, stack_ref, misfit_ref, *, span,
):
    radius = (span - 1) // 2
    layers, cells_x, cells_y = gradient_ref.shape
    s = full_surface(sum_ref[...], above_ref[...], below_ref[...])
    full_ref[...] = s
    adjoint = rounded_adjoint(s, q_ref[...])
    turned = turned_ref[: layers * cells_x, :]
    half = cells_y // 2
    copies = []
    for n in range(2):
        columns = slice(n * half, (n + 1) * half)
        stack_shifts(adjoint, stack_ref, columns, span, radius)
        gradient = jnp.dot(turned, stack_ref[:, columns], preferred_element_type=f32)
        for l in range(layers):
            gradient_ref[l, :, columns] = gradient[l * cells_x : (l + 1) * cells_x, :]
        copies.append(
            pltpu.make_async_copy(
                gradient_ref.at[:, :, columns], gradient_hbm.at[:, :, columns], sems.at[n]
            )
        )
        copies[-1].start()
    share = residual_ref.shape[1]
    for start in range(0, cells_x, share):

        @pl.when(start_ref[0] == start)
        def _():
            top = 16 + start
            low, high = (top - 1) // 8 * 8, -(-(top + share + 1) // 8) * 8
            fields = tensor_fields(full_ref[low:high, :])
            for k in range(3):
                misfit_ref[k, : high - low, :] = fields[k][:, :cells_y]
                residual_ref[k] = (
                    misfit_ref[k, top - low : top - low + share, :]
                    - observed_ref[k, start : start + share, :]
                )

    copies.append(pltpu.make_async_copy(residual_ref, residual_hbm, sems.at[2]))
    copies[-1].start()
    for copy in copies:
        copy.wait()


def call(kernel, outs, scratch=(), inputs=pltpu.VMEM, smem=(), results=pltpu.VMEM):
    made = pl.BlockSpec(memory_space=results)
    given = pl.BlockSpec(memory_space=inputs)
    scalar = pl.BlockSpec(memory_space=pltpu.SMEM)

    def run(*operands):
        if inputs is pltpu.HBM:
            operands = [pltpu.with_memory_space_constraint(v, pltpu.HBM) for v in operands]
        return pl.pallas_call(
            kernel,
            out_shape=outs,
            in_specs=[scalar if i in smem else given for i in range(len(operands))],
            out_specs=jax.tree.map(lambda _: made, outs),
            scratch_shapes=[
                item if not isinstance(item, tuple) else pltpu.VMEM(*item) for item in scratch
            ],
            compiler_params=pltpu.CompilerParams(vmem_limit_bytes=GRANT),
        )(*operands)

    return run


def shaped(shape, kind=f32):
    return jax.ShapeDtypeStruct(shape, kind)


def swap(value, axis, distance):
    peers = lax.axis_size(axis)
    return lax.ppermute(value, axis, [(i, i ^ distance) for i in range(peers)])


def body(labels, background, contrasts, kernels, observed):
    layers, cells_x, cells_y = labels.shape
    span = kernels.shape[1]
    lanes = layers * cells_x
    width = cells_y + 128
    depth_peers, row_peers = lax.axis_size("gz"), lax.axis_size("gx")
    assert cells_x == 32 and span == 15 and lanes <= 192 and cells_y == 512 and lax.axis_size("gy") == 2
    assert depth_peers & (depth_peers - 1) == 0
    share = cells_x // depth_peers
    upward = [(i, (i - 1) % row_peers) for i in range(row_peers)]
    downward = [(j, i) for i, j in upward]
    full = ((FULL, width), f32)
    prod = ((span * PART, cells_y), f32)
    stack = ((span * PART, cells_y), bf16)
    edge_prod = ((span * PART, 128), f32)
    edge_stack = ((span * PART, 128), bf16)
    field = shaped((PART, width))

    def kernel_of(body_of):
        return functools.partial(body_of, span=span)

    edge, density_edge, density, bands, observed = call(
        first_kernel,
        (
            shaped((2 * PART, 128)),
            shaped((lanes, 128)),
            shaped((lanes, cells_y)),
            shaped((span * PART, WIDE), bf16),
            shaped(observed.shape),
        ),
        (
            (labels.shape, labels.dtype),
            (background.shape, background.dtype),
            pltpu.SMEM(contrasts.shape, contrasts.dtype),
            (kernels.shape, kernels.dtype),
            pltpu.SemaphoreType.DMA((5,)),
            ((16 * layers, 16), f32),
            ((16, WIDE), f32),
            edge_prod,
        ),
        inputs=pltpu.HBM,
    )(labels, background, contrasts, kernels, observed)
    part, q = call(
        kernel_of(first_field_kernel), (field, field), (prod, ((3, PART, width), f32))
    )(density, bands, observed)
    turned = call(transpose_kernel, shaped((WIDE, span * PART), bf16))(bands)
    start = (lax.axis_index("gz") * share).astype(jnp.int32).reshape(1)

    for iteration in range(ITERS):
        others = swap(edge, "gy", 1)
        part = call(edges_kernel, shaped((PART, cells_y)))(part, others)
        for bit in range(depth_peers.bit_length() - 2):
            part = part + swap(part, "gz", 2 << bit)
        other = swap(part, "gz", 1)
        fold = (((8, 128), f32),)
        if iteration == 0:
            total, up, down, q = call(
                rows_kernel, (field, shaped((24, width)), shaped((24, width)), field), fold
            )(part, other, q, others)
        else:
            total, up, down = call(
                lambda a, b, c, d, e, g: rows_kernel(a, b, None, None, c, d, e, None, g),
                (field, shaped((16, width)), shaped((16, width))),
                fold,
            )(part, other)
        below = lax.ppermute(up, "gx", upward)
        above = lax.ppermute(down, "gx", downward)
        if iteration == 0:
            edge = call(
                kernel_of(middle_kernel), shaped((PART, 128)), (edge_stack, edge_prod)
            )(total, above, below, q, density_edge, bands, turned)
            part, q = call(kernel_of(middle_field_kernel), (field, field), (stack, prod))(
                total, above, below, q, density, bands, turned
            )
    return call(
        kernel_of(last_kernel),
        (shaped((3, share, cells_y)), shaped((layers, cells_x, cells_y))),
        (
            ((3, share, cells_y), f32),
            ((layers, cells_x, cells_y), f32),
            pltpu.SemaphoreType.DMA((3,)),
            full,
            ((span * PART, cells_y), bf16),
            ((3, cells_x, cells_y), f32),
        ),
        smem=(0,),
        results=pltpu.HBM,
    )(start, total, above, below, q, turned, observed)


def solution(mesh):
    placed = (
        P(("runs", "gz"), "gx", "gy"),
        P(("runs", "gz"), "gx", "gy"),
        P("runs"),
        P(("runs", "gz"), None, None),
        P("runs", "gx", "gy"),
    )
    return jax.shard_map(
        body,
        mesh=mesh,
        in_specs=placed,
        out_specs=(P("runs", ("gx", "gz"), "gy"), P(("runs", "gz"), "gx", "gy")),
        check_vma=False,
    )
```

time: 32.8 us -> 32.5 us (level)
    ppermute x2, waiting for transfers between devices: 4.55 us -> 4.88 us  [body(): above = lax.ppermute(down, 'gx', downward)]
  transfers between devices with their start and end apart: 8 -> 8, of which waited for: 7 -> 6; matrix products, arithmetic and copies ran while one was open for 0% -> 0% of each run, Pallas kernels for 4% -> 7%
where the time goes in v4:
time: 32.5 us; the launch traced here: 32.3 us
  starting transfers between devices  12.9 us (40%)
  waiting for transfers between devices  11.8 us (36%)
  Pallas kernels  6.95 us (21%)
  between operations  0.69 us (2%)
    pallas_call x10, Pallas kernels, run(): pl.pallas_call(kernel, out_shape=outs, in_specs=[scalar if i in smem else...  6.95 us
    ppermute x4, waiting for transfers between devices, swap(): return lax.ppermute(value, axis, [(i, i ^ distance) for i in range(peers)])  6.82 us
    ppermute x4, starting transfers between devices, swap(): return lax.ppermute(value, axis, [(i, i ^ distance) for i in range(peers)])  5.17 us
    ppermute x2, waiting for transfers between devices, body(): above = lax.ppermute(down, 'gx', downward)  4.88 us
    ppermute x2, starting transfers between devices, body(): below = lax.ppermute(up, 'gx', upward)  4.88 us
    ppermute x2, starting transfers between devices, body(): above = lax.ppermute(down, 'gx', downward)  2.88 us
  transfers between devices with their start and end apart: 8, of which 6 were waited for; matrix products, arithmetic and copies ran while one was open for 0% of the time, Pallas kernels for 7%

profile of v4, /device:TPU:0, one launch (start us, length us, event | category | flops | bytes accessed | tf_op | source)
XLA Modules:
  0.0 32.3 jit_solution(14853206500854567222)
XLA Ops:
  0.6 1.6 %shard_map.68 = (f32[96,128]{1,0:T(8,128)S(1)}, f32[192,128]{1,0:T(8,128)S(1)}, f32[192,512]{1,0:T(8,128)S(1)}, bf16[720,256]{1,0:T(8,128)(2,1)S(1)}, f32[3,32,512]{2,1,0:T(8,128)S(1)}) custom-call(s32[6,32,512]{2,1,0:T(8,128)} %labels_hbm.1, bf16[6,32,512]{2,1,0:T(8,128)(2,1)} %background_hbm.1, f32[4]{0:T(128)} %contrasts_hbm.1, bf16[6,15,15]{2,1,0:T(8,128)(2,1)} %k_hbm.1, ...), custom_call_target="tpu_custom_call" | custom-call | tf_op jit(solution)/shard_map/pallas_call | solution.py:431
  2.3 0.6 %collective-permute-start = (f32[96,128]{1,0:T(8,128)S(1)}, f32[96,128]{1,0:T(8,128)S(1)}, u32[]{:S(2)}, u32[]{:S(2)}) collective-permute-start(f32[96,128]{1,0:T(8,128)S(1)} %get-tuple-element.22), channel_id=1, source_target_pairs={{0,2},{2,0},{1,3},{3,1},{4,6},{6,4},{5,7},{7,5},{8,10},{10,8},{9,1... | collective-permute-start | bytes 147464 | tf_op jit(solution)/shard_map/ppermute | solution.py:451
  2.8 0.7 %shard_map.69 = (f32[48,640]{1,0:T(8,128)S(1)}, f32[48,640]{1,0:T(8,128)S(1)}) custom-call(f32[192,512]{1,0:T(8,128)S(1)} %get-tuple-element.18.density_ref, bf16[720,256]{1,0:T(8,128)(2,1)S(1)} %get-tuple-element.19.bands_ref, f32[3,32,512]{2,1,0:T(8,128)S(1)} %get-tuple-element.20.observed_ref), custom_call_target="tpu_custom_call" | custom-call | tf_op jit(solution)/shard_map/pallas_call | solution.py:431
  3.5 0.2 collective-permute-done.edge_ref
  3.7 0.2 shard_map.70.part_ref
  3.9 2.8 %collective-permute-start.1 = (f32[48,512]{1,0:T(8,128)S(1)}, f32[48,512]{1,0:T(8,128)S(1)}, u32[]{:S(2)}, u32[]{:S(2)}) collective-permute-start(f32[48,512]{1,0:T(8,128)S(1)} %shard_map.70.part_ref), channel_id=1, source_target_pairs={{0,1},{1,0},{2,3},{3,2},{4,5},{5,4},{6,7},{7,6},{8,9},{9,8},{10,11... | collective-permute-start | bytes 294920 | tf_op jit(solution)/shard_map/ppermute | solution.py:451
  6.8 3.1 %collective-permute-done.1.other_ref = f32[48,512]{1,0:T(8,128)S(1)} collective-permute-done((f32[48,512]{1,0:T(8,128)S(1)}, f32[48,512]{1,0:T(8,128)S(1)}, u32[]{:S(2)}, u32[]{:S(2)}) %collective-permute-start.1) | collective-permute-done | bytes 98336 | tf_op jit(solution)/shard_map/ppermute | solution.py:451
  9.9 0.2 shard_map.71
  10.1 1.8 %collective-permute-start.2 = (f32[24,640]{1,0:T(8,128)S(1)}, f32[24,640]{1,0:T(8,128)S(1)}, u32[]{:S(2)}, u32[]{:S(2)}) collective-permute-start(f32[24,640]{1,0:T(8,128)S(1)} %get-tuple-element.25), channel_id=1, source_target_pairs={{12,0},{0,4},{4,8},{8,12},{13,1},{1,5},{5,9},{9,13},{14,2},{2,6},{... | collective-permute-start | bytes 184328 | tf_op jit(solution)/shard_map/ppermute | solution.py:520
  11.9 2.1 %collective-permute-start.3 = (f32[24,640]{1,0:T(8,128)S(1)}, f32[24,640]{1,0:T(8,128)S(1)}, u32[]{:S(2)}, u32[]{:S(2)}) collective-permute-start(f32[24,640]{1,0:T(8,128)S(1)} %get-tuple-element.26), channel_id=1, source_target_pairs={{0,12},{4,0},{8,4},{12,8},{1,13},{5,1},{9,5},{13,9},{2,14},{6,2},{... | collective-permute-start | bytes 184328 | tf_op jit(solution)/shard_map/ppermute | solution.py:519
  14.0 0.2 shard_map.72.turned_ref
  14.2 2.5 %collective-permute-done.2.above_ref = f32[24,640]{1,0:T(8,128)S(1)} collective-permute-done((f32[24,640]{1,0:T(8,128)S(1)}, f32[24,640]{1,0:T(8,128)S(1)}, u32[]{:S(2)}, u32[]{:S(2)}) %collective-permute-start.2) | collective-permute-done | bytes 61472 | tf_op jit(solution)/shard_map/ppermute | solution.py:520
  16.7 0.1 collective-permute-done.3.below_ref
  16.8 0.8 %shard_map.74 = f32[48,128]{1,0:T(8,128)S(1)} custom-call(f32[48,640]{1,0:T(8,128)S(1)} %get-tuple-element.24.sum_ref, f32[24,640]{1,0:T(8,128)S(1)} %collective-permute-done.2.above_ref, f32[24,640]{1,0:T(8,128)S(1)} %collective-permute-done.3.below_ref, f32[48,640]{1,0:T(8,128)S(1)} %get-tuple-element.27.q_ref, ...), custom_call_target="tpu_custom_call" | custom-call | tf_op jit(solution)/shard_map/pallas_call | solution.py:431
  17.6 0.1 collective-permute-start.4
  17.7 1.3 %shard_map.73 = (f32[48,640]{1,0:T(8,128)S(1)}, f32[48,640]{1,0:T(8,128)S(1)}) custom-call(f32[48,640]{1,0:T(8,128)S(1)} %get-tuple-element.24.sum_ref, f32[24,640]{1,0:T(8,128)S(1)} %collective-permute-done.2.above_ref, f32[24,640]{1,0:T(8,128)S(1)} %collective-permute-done.3.below_ref, f32[48,640]{1,0:T(8,128)S(1)} %get-tuple-element.27.q_ref, ...), custom_call_target="tpu_custom_call" | custom-call | tf_op jit(solution)/shard_map/pallas_call | solution.py:431
  19.0 0.2 shard_map.75.a
  19.2 1.7 %collective-permute-start.5 = (f32[48,512]{1,0:T(8,128)S(1)}, f32[48,512]{1,0:T(8,128)S(1)}, u32[]{:S(2)}, u32[]{:S(2)}) collective-permute-start(f32[48,512]{1,0:T(8,128)S(1)} %shard_map.75.a), channel_id=1, source_target_pairs={{0,1},{1,0},{2,3},{3,2},{4,5},{5,4},{6,7},{7,6},{8,9},{9,8},{10,11... | collective-permute-start | bytes 294920 | tf_op jit(solution)/shard_map/ppermute | solution.py:451
  20.9 3.5 %collective-permute-done.5.b = f32[48,512]{1,0:T(8,128)S(1)} collective-permute-done((f32[48,512]{1,0:T(8,128)S(1)}, f32[48,512]{1,0:T(8,128)S(1)}, u32[]{:S(2)}, u32[]{:S(2)}) %collective-permute-start.5) | collective-permute-done | bytes 98336 | tf_op jit(solution)/shard_map/ppermute | solution.py:451
  24.4 0.2 shard_map.76
  24.6 1.0 %collective-permute-start.6 = (f32[16,640]{1,0:T(8,128)S(1)}, f32[16,640]{1,0:T(8,128)S(1)}, u32[]{:S(2)}, u32[]{:S(2)}) collective-permute-start(f32[16,640]{1,0:T(8,128)S(1)} %get-tuple-element.31), channel_id=1, source_target_pairs={{12,0},{0,4},{4,8},{8,12},{13,1},{1,5},{5,9},{9,13},{14,2},{2,6},{... | collective-permute-start | bytes 122888 | tf_op jit(solution)/shard_map/ppermute | solution.py:520
  25.6 2.8 %collective-permute-start.7 = (f32[16,640]{1,0:T(8,128)S(1)}, f32[16,640]{1,0:T(8,128)S(1)}, u32[]{:S(2)}, u32[]{:S(2)}) collective-permute-start(f32[16,640]{1,0:T(8,128)S(1)} %get-tuple-element.32), channel_id=1, source_target_pairs={{0,12},{4,0},{8,4},{12,8},{1,13},{5,1},{9,5},{13,9},{2,14},{6,2},{... | collective-permute-start | bytes 122888 | tf_op jit(solution)/shard_map/ppermute | solution.py:519
  28.4 2.3 %collective-permute-done.6.above_ref = f32[16,640]{1,0:T(8,128)S(1)} collective-permute-done((f32[16,640]{1,0:T(8,128)S(1)}, f32[16,640]{1,0:T(8,128)S(1)}, u32[]{:S(2)}, u32[]{:S(2)}) %collective-permute-start.6) | collective-permute-done | bytes 40992 | tf_op jit(solution)/shard_map/ppermute | solution.py:520
  30.8 1.6 %shard_map.77 = (f32[3,16,512]{2,1,0:T(8,128)}, f32[6,32,512]{2,1,0:T(8,128)}) custom-call(s32[1]{0:T(128)} %bitcast.start_ref, f32[48,640]{1,0:T(8,128)S(1)} %get-tuple-element.30.sum_ref, f32[16,640]{1,0:T(8,128)S(1)} %collective-permute-done.6.above_ref, f32[16,640]{1,0:T(8,128)S(1)} %collective-permute-done.7.below_ref, ...), custom_call_target="tpu_custom_call" | custom-call | tf_op jit(solution)/shard_map/pallas_call | solution.py:431
  (2 shorter events, 0.0 us)
Async XLA Ops:
  2.3 1.4 %collective-permute-start = (f32[96,128]{1,0:T(8,128)S(1)}, f32[96,128]{1,0:T(8,128)S(1)}, u32[]{:S(2)}, u32[]{:S(2)}) collective-permute-start(f32[96,128]{1,0:T(8,128)S(1)} %get-tuple-element.22), channel_id=1, source_target_pairs={{0,2},{2,0},{1,3},{3,1},{4,6},{6,4},{5,7},{7,5},{8,10},{10,8},{9,1... | collective-permute-start | bytes 147464 | tf_op jit(solution)/shard_map/ppermute | solution.py:451
  3.9 6.0 %collective-permute-start.1 = (f32[48,512]{1,0:T(8,128)S(1)}, f32[48,512]{1,0:T(8,128)S(1)}, u32[]{:S(2)}, u32[]{:S(2)}) collective-permute-start(f32[48,512]{1,0:T(8,128)S(1)} %shard_map.70.part_ref), channel_id=1, source_target_pairs={{0,1},{1,0},{2,3},{3,2},{4,5},{5,4},{6,7},{7,6},{8,9},{9,8},{10,11... | collective-permute-start | bytes 294920 | tf_op jit(solution)/shard_map/ppermute | solution.py:451
  10.1 6.7 %collective-permute-start.2 = (f32[24,640]{1,0:T(8,128)S(1)}, f32[24,640]{1,0:T(8,128)S(1)}, u32[]{:S(2)}, u32[]{:S(2)}) collective-permute-start(f32[24,640]{1,0:T(8,128)S(1)} %get-tuple-element.25), channel_id=1, source_target_pairs={{12,0},{0,4},{4,8},{8,12},{13,1},{1,5},{5,9},{9,13},{14,2},{2,6},{... | collective-permute-start | bytes 184328 | tf_op jit(solution)/shard_map/ppermute | solution.py:520
  11.9 4.9 %collective-permute-start.3 = (f32[24,640]{1,0:T(8,128)S(1)}, f32[24,640]{1,0:T(8,128)S(1)}, u32[]{:S(2)}, u32[]{:S(2)}) collective-permute-start(f32[24,640]{1,0:T(8,128)S(1)} %get-tuple-element.26), channel_id=1, source_target_pairs={{0,12},{4,0},{8,4},{12,8},{1,13},{5,1},{9,5},{13,9},{2,14},{6,2},{... | collective-permute-start | bytes 184328 | tf_op jit(solution)/shard_map/ppermute | solution.py:519
  17.6 1.4 %collective-permute-start.4 = (f32[48,128]{1,0:T(8,128)S(1)}, f32[48,128]{1,0:T(8,128)S(1)}, u32[]{:S(2)}, u32[]{:S(2)}) collective-permute-start(f32[48,128]{1,0:T(8,128)S(1)} %shard_map.74), channel_id=1, source_target_pairs={{0,2},{2,0},{1,3},{3,1},{4,6},{6,4},{5,7},{7,5},{8,10},{10,8},{9,1... | collective-permute-start | bytes 73736 | tf_op jit(solution)/shard_map/ppermute | solution.py:451
  19.2 5.2 %collective-permute-start.5 = (f32[48,512]{1,0:T(8,128)S(1)}, f32[48,512]{1,0:T(8,128)S(1)}, u32[]{:S(2)}, u32[]{:S(2)}) collective-permute-start(f32[48,512]{1,0:T(8,128)S(1)} %shard_map.75.a), channel_id=1, source_target_pairs={{0,1},{1,0},{2,3},{3,2},{4,5},{5,4},{6,7},{7,6},{8,9},{9,8},{10,11... | collective-permute-start | bytes 294920 | tf_op jit(solution)/shard_map/ppermute | solution.py:451
  24.6 6.2 %collective-permute-start.6 = (f32[16,640]{1,0:T(8,128)S(1)}, f32[16,640]{1,0:T(8,128)S(1)}, u32[]{:S(2)}, u32[]{:S(2)}) collective-permute-start(f32[16,640]{1,0:T(8,128)S(1)} %get-tuple-element.31), channel_id=1, source_target_pairs={{12,0},{0,4},{4,8},{8,12},{13,1},{1,5},{5,9},{9,13},{14,2},{2,6},{... | collective-permute-start | bytes 122888 | tf_op jit(solution)/shard_map/ppermute | solution.py:520
  25.6 5.1 %collective-permute-start.7 = (f32[16,640]{1,0:T(8,128)S(1)}, f32[16,640]{1,0:T(8,128)S(1)}, u32[]{:S(2)}, u32[]{:S(2)}) collective-permute-start(f32[16,640]{1,0:T(8,128)S(1)} %get-tuple-element.32), channel_id=1, source_target_pairs={{0,12},{4,0},{8,4},{12,8},{1,13},{5,1},{9,5},{13,9},{2,14},{6,2},{... | collective-permute-start | bytes 122888 | tf_op jit(solution)/shard_map/ppermute | solution.py:519

commit v5 on v4

--- a/solution.py
+++ b/solution.py
@@ -106,7 +106,7 @@
     return jnp.concatenate([first, field[:, 128 : width - 256], last, side], axis=1)
 
 
-def build_bands(k_ref, taps_ref, base_ref, bands_ref):
+def kernel_rows(k_ref, taps_ref):
     layers, span, _ = k_ref.shape
     taps_ref[...] = jnp.zeros(taps_ref.shape, f32)
     for l in range(layers):
@@ -114,18 +114,22 @@
     shape = (taps_ref.shape[0], WIDE)
     source = iota(shape, 0)
     place = jnp.where(32 * (source >> 4) + (source & 15) == iota(shape, 1), 1.0, 0.0)
-    base_ref[...] = lax.dot_general(
+    return lax.dot_general(
         taps_ref[...].astype(bf16),
         place.astype(bf16),
         (((0,), (0,)), ((), ())),
         preferred_element_type=f32,
     )
+
+
+def build_bands(base_ref, bands_ref, span, offset=0):
     tap = (iota((8, 128), 1) & 31) - iota((8, 128), 0) + 15
     keep = [(tap - 8 * g >= 0) & (tap - 8 * g < span) for g in range(PART // 8)]
     for block in range(WIDE // 128):
-        columns = slice(128 * block, 128 * block + 128)
         for j in range(span):
-            row = jnp.broadcast_to(base_ref[j : j + 1, columns], (8, 128))
+            row = jnp.broadcast_to(
+                base_ref[j : j + 1, 128 * block : 128 * block + 128], (8, 128)
+            )
             moved = [
                 jnp.where(
                     keep[g],
@@ -134,9 +138,10 @@
                 )
                 for g in range(PART // 8)
             ]
-            bands_ref[j * PART : (j + 1) * PART, columns] = jnp.concatenate(
-                moved, axis=0
-            ).astype(bf16)
+            bands_ref[
+                j * PART : (j + 1) * PART,
+                offset + 128 * block : offset + 128 * block + 128,
+            ] = jnp.concatenate(moved, axis=0).astype(bf16)
 
 
 def edge_message(bands, rounded, prod_ref, span, radius):
@@ -182,9 +187,9 @@
 
 def first_kernel(
     labels_hbm, background_hbm, contrasts_hbm, k_hbm, observed_hbm,
-    edge_ref, density_edge_ref, density_ref, bands_ref, observed_ref,
+    edge_ref, density_edge_ref, density_ref, base_ref, bands_ref, observed_ref,
     labels_ref, background_ref, contrasts_ref, k_ref, sems,
-    taps_ref, base_ref, prod_ref,
+    taps_ref, prod_ref,
 ):
     layers, cells_x, cells_y = labels_ref.shape
     span = k_ref.shape[1]
@@ -203,7 +208,8 @@
     for copy in copies:
         copy.start()
     copies[0].wait()
-    build_bands(k_ref, taps_ref, base_ref, bands_ref)
+    base_ref[...] = kernel_rows(k_ref, taps_ref)
+    build_bands(base_ref, bands_ref, span)
     for copy in copies[1:]:
         copy.wait()
     classes = contrasts_ref.shape[0]
@@ -252,8 +258,12 @@
     q_ref[...] = adjoint_of(obs_ref[0], obs_ref[1], obs_ref[2])
 
 
-def transpose_kernel(bands_ref, out_ref):
-    out_ref[...] = bands_ref[...].astype(f32).T.astype(bf16)
+def turn_kernel(*refs, span):
+    *base_refs, own_ref, bands_ref, turned_ref = refs
+    bands_ref[:, :WIDE] = own_ref[...]
+    for n, base_ref in enumerate(base_refs):
+        build_bands(base_ref, bands_ref, span, WIDE * (n + 1))
+    turned_ref[...] = bands_ref[...].astype(f32).T.astype(bf16)
 
 
 def edges_kernel(part_ref, edge_ref, out_ref):
@@ -264,6 +274,14 @@
     for n in range(8):
         row = (PART - 1) * (n // 4)
         out_ref[row : row + 1, 128 * (n % 4) : 128 * (n % 4 + 1)] = folded[n : n + 1]
+
+
+def send_rows(sum_ref, up_ref, down_ref):
+    sub = iota((8, sum_ref.shape[1]), 0)
+    up_ref[:8, :] = sum_ref[8:16, :]
+    up_ref[8:16, :] = jnp.where(sub >= 1, sum_ref[:8, :], sum_ref[16:24, :])
+    down_ref[:8, :] = sum_ref[32:40, :]
+    down_ref[8:16, :] = jnp.where(sub < 7, sum_ref[40:48, :], sum_ref[24:32, :])
 
 
 def rows_kernel(
@@ -278,15 +296,17 @@
     zero = jnp.zeros((1, cells_y), f32)
     sum_ref[:1, :cells_y] = zero
     sum_ref[PART - 1 :, :cells_y] = zero
-    sub = iota((8, sum_ref.shape[1]), 0)
-    up_ref[:8, :] = sum_ref[8:16, :]
-    up_ref[8:16, :] = jnp.where(sub >= 1, sum_ref[:8, :], sum_ref[16:24, :])
-    down_ref[:8, :] = sum_ref[32:40, :]
-    down_ref[8:16, :] = jnp.where(sub < 7, sum_ref[40:48, :], sum_ref[24:32, :])
+    send_rows(sum_ref, up_ref, down_ref)
     if q_ref is not None:
+        sub = iota((8, sum_ref.shape[1]), 0)
         q_out_ref[...] = add_edges(q_ref[...], edge_ref[PART:, :])
         up_ref[16:24, :] = jnp.where(sub < 7, q_out_ref[8:16, :], q_out_ref[:8, :])
         down_ref[16:24, :] = jnp.where(sub >= 1, q_out_ref[32:40, :], q_out_ref[40:48, :])
+
+
+def whole_rows_kernel(part_ref, edge_ref, sum_ref, up_ref, down_ref):
+    sum_ref[...] = add_edges(part_ref[...], edge_ref[...])
+    send_rows(sum_ref, up_ref, down_ref)
 
 
 def full_surface(total, above, below):
@@ -327,50 +347,62 @@
     for j in range(span):
         shift = (j - radius) % adjoint.shape[1]
         moved = pltpu.roll(adjoint, shift, 1) if shift else adjoint
-        stack_ref[j * PART : (j + 1) * PART, columns] = moved[:, columns].astype(bf16)
+        stack_ref[j * PART : (j + 1) * PART, columns] = moved[:, columns]
 
 
 def rounded_adjoint(s, q):
-    return (adjoint_square(s) - q).astype(bf16).astype(f32)
+    return (adjoint_square(s) - q).astype(bf16)
+
+
+def descended(densities, gradient, keep=None):
+    pieces = []
+    for n, density in enumerate(densities):
+        rows, columns = density.shape
+        moved = density - descent * gradient[n * WIDE : n * WIDE + rows]
+        if keep is not None:
+            moved = jnp.where(keep, moved, 0.0)
+        pieces.append(moved.astype(bf16))
+        pieces.append(jnp.zeros((WIDE - rows, columns), bf16))
+    return jnp.concatenate(pieces, axis=0)
 
 
 def middle_kernel(
     sum_ref, above_ref, below_ref, q_ref, density_edge_ref, bands_ref, turned_ref,
-    edge_ref,
-    stack_ref, prod_ref, *, span,
+    *rest, span,
 ):
+    *twin_refs, edge_ref, stack_ref, prod_ref = rest
     radius = (span - 1) // 2
-    lanes = density_edge_ref.shape[0]
     total, q = edges_of(sum_ref[...]), edges_of(q_ref[...])
     above, below = edges_of(above_ref[...]), edges_of(below_ref[...])
     adjoint = rounded_adjoint(full_surface(total, above, below), full_q(q, above, below))
     stack_shifts(adjoint, stack_ref, slice(0, 128), span, radius)
-    gradient = jnp.dot(turned_ref[:lanes, :], stack_ref[...], preferred_element_type=f32)
-    density = density_edge_ref[...] - descent * gradient
-    lane = iota(density.shape, 1)
+    gradient = jnp.dot(turned_ref[...], stack_ref[...], preferred_element_type=f32)
+    densities = [density_edge_ref[...]] + [
+        edge_columns(ref[:, :128], ref[:, ref.shape[1] - 128 :]) for ref in twin_refs
+    ]
+    lane = iota(densities[0].shape, 1)
     keep = ((lane >= 32) & (lane < 48)) | (lane >= 112)
-    density = jnp.where(keep, density, 0.0)
     edge_ref[...] = edge_message(
-        bands_ref[:, :lanes], density.astype(bf16), prod_ref, span, radius
+        bands_ref[...], descended(densities, gradient, keep), prod_ref, span, radius
     )
 
 
 def middle_field_kernel(
     sum_ref, above_ref, below_ref, q_ref, density_ref, bands_ref, turned_ref,
-    part_ref, q_out_ref,
-    stack_ref, prod_ref, *, span,
+    *rest, span,
 ):
+    *twin_refs, part_ref, q_out_ref, stack_ref, prod_ref = rest
     radius = (span - 1) // 2
-    lanes, cells_y = density_ref.shape
+    cells_y = density_ref.shape[1]
     above, below = above_ref[...], below_ref[...]
     q = full_q(q_ref[...], above, below)
     q_out_ref[...] = q
     adjoint = rounded_adjoint(full_surface(sum_ref[...], above, below), q)
     stack_shifts(adjoint, stack_ref, slice(0, cells_y), span, radius)
-    gradient = jnp.dot(turned_ref[:lanes, :], stack_ref[...], preferred_element_type=f32)
-    density = density_ref[...] - descent * gradient
+    gradient = jnp.dot(turned_ref[...], stack_ref[...], preferred_element_type=f32)
+    densities = [ref[...] for ref in (density_ref, *twin_refs)]
     part_ref[...] = scatter_surface(
-        bands_ref[:, :lanes], density.astype(bf16), prod_ref, span, radius
+        bands_ref[...], descended(densities, gradient), prod_ref, span, radius
     )
 
 
@@ -400,19 +432,22 @@
         )
         copies[-1].start()
     share = residual_ref.shape[1]
-    for start in range(0, cells_x, share):
-
-        @pl.when(start_ref[0] == start)
-        def _():
-            top = 16 + start
-            low, high = (top - 1) // 8 * 8, -(-(top + share + 1) // 8) * 8
-            fields = tensor_fields(full_ref[low:high, :])
-            for k in range(3):
-                misfit_ref[k, : high - low, :] = fields[k][:, :cells_y]
-                residual_ref[k] = (
-                    misfit_ref[k, top - low : top - low + share, :]
-                    - observed_ref[k, start : start + share, :]
-                )
+    if share % 8 == 0:
+        start = pl.multiple_of(start_ref[0], 8)
+        fields = tensor_fields(full_ref[pl.ds(start + 8, share + 16), :])
+        for k in range(3):
+            residual_ref[k] = (
+                fields[k][8 : 8 + share, :cells_y] - observed_ref[k, pl.ds(start, share), :]
+            )
+    else:
+        fields = tensor_fields(full_ref[...])
+        for k in range(3):
+            misfit_ref[k] = fields[k][16 : 16 + cells_x, :cells_y] - observed_ref[k]
+        for start in range(0, cells_x, share):
+
+            @pl.when(start_ref[0] == start)
+            def _():
+                residual_ref[...] = misfit_ref[:, start : start + share, :]
 
     copies.append(pltpu.make_async_copy(residual_ref, residual_hbm, sems.at[2]))
     copies[-1].start()
@@ -472,12 +507,13 @@
     def kernel_of(body_of):
         return functools.partial(body_of, span=span)
 
-    edge, density_edge, density, bands, observed = call(
+    edge, density_edge, density, base, bands, observed = call(
         first_kernel,
         (
             shaped((2 * PART, 128)),
             shaped((lanes, 128)),
             shaped((lanes, cells_y)),
+            shaped((16, WIDE)),
             shaped((span * PART, WIDE), bf16),
             shaped(observed.shape),
         ),
@@ -488,7 +524,6 @@
             (kernels.shape, kernels.dtype),
             pltpu.SemaphoreType.DMA((5,)),
             ((16 * layers, 16), f32),
-            ((16, WIDE), f32),
             edge_prod,
         ),
         inputs=pltpu.HBM,
@@ -496,34 +531,52 @@
     part, q = call(
         kernel_of(first_field_kernel), (field, field), (prod, ((3, PART, width), f32))
     )(density, bands, observed)
-    turned = call(transpose_kernel, shaped((WIDE, span * PART), bf16))(bands)
     start = (lax.axis_index("gz") * share).astype(jnp.int32).reshape(1)
 
+    twins = depth_peers == 2
+    fold = (((8, 128), f32),)
     for iteration in range(ITERS):
         others = swap(edge, "gy", 1)
-        part = call(edges_kernel, shaped((PART, cells_y)))(part, others)
-        for bit in range(depth_peers.bit_length() - 2):
-            part = part + swap(part, "gz", 2 << bit)
-        other = swap(part, "gz", 1)
-        fold = (((8, 128), f32),)
+        if iteration == 1 and twins:
+            total, up, down = call(
+                whole_rows_kernel, (field, shaped((16, width)), shaped((16, width)))
+            )(part, others)
+        else:
+            part = call(edges_kernel, shaped((PART, cells_y)))(part, others)
+            for bit in range(depth_peers.bit_length() - 2):
+                part = part + swap(part, "gz", 2 << bit)
+            other = swap(part, "gz", 1)
+            if iteration == 0:
+                total, up, down, q = call(
+                    rows_kernel,
+                    (field, shaped((24, width)), shaped((24, width)), field),
+                    fold,
+                )(part, other, q, others)
+            else:
+                total, up, down = call(
+                    lambda a, b, c, d, e, g: rows_kernel(a, b, None, None, c, d, e, None, g),
+                    (field, shaped((16, width)), shaped((16, width))),
+                    fold,
+                )(part, other)
         if iteration == 0:
-            total, up, down, q = call(
-                rows_kernel, (field, shaped((24, width)), shaped((24, width)), field), fold
-            )(part, other, q, others)
-        else:
-            total, up, down = call(
-                lambda a, b, c, d, e, g: rows_kernel(a, b, None, None, c, d, e, None, g),
-                (field, shaped((16, width)), shaped((16, width))),
-                fold,
-            )(part, other)
+            twin_base, twin_density = (), ()
+            if twins:
+                sent = lax.optimization_barrier((part, base, density))
+                twin_base = (swap(sent[1], "gz", 1),)
+                twin_density = (swap(sent[2], "gz", 1),)
+            wide = WIDE * (1 + len(twin_base))
+            bands, turned = call(
+                kernel_of(turn_kernel),
+                (shaped((span * PART, wide), bf16), shaped((wide, span * PART), bf16)),
+            )(*twin_base, bands)
         below = lax.ppermute(up, "gx", upward)
         above = lax.ppermute(down, "gx", downward)
         if iteration == 0:
             edge = call(
                 kernel_of(middle_kernel), shaped((PART, 128)), (edge_stack, edge_prod)
-            )(total, above, below, q, density_edge, bands, turned)
+            )(total, above, below, q, density_edge, bands, turned, *twin_density)
             part, q = call(kernel_of(middle_field_kernel), (field, field), (stack, prod))(
-                total, above, below, q, density, bands, turned
+                total, above, below, q, density, bands, turned, *twin_density
             )
     return call(
         kernel_of(last_kernel),

time: 32.5 us -> 37.6 us (1.16)
  waiting for transfers between devices: 11.8 us -> 16.1 us
  Pallas kernels: 6.95 us -> 7.59 us
    ppermute x4 -> x5, waiting for transfers between devices: 6.82 us -> 13.7 us  [swap(): return lax.ppermute(value, axis, [(i, i ^ distance) for i in range(peers)])]
    ppermute x2, waiting for transfers between devices: 4.88 us -> 2.38 us  [body(): above = lax.ppermute(down, 'gx', downward)]
    ppermute x2, starting transfers between devices: 4.88 us -> 5.9 us  [body(): below = lax.ppermute(up, 'gx', upward)]
    ppermute x2, starting transfers between devices: 2.88 us -> 1.9 us  [body(): above = lax.ppermute(down, 'gx', downward)]
    pallas_call x10 -> x9, Pallas kernels: 6.95 us -> 7.59 us  [run(): pl.pallas_call(kernel, out_shape=outs, in_specs=[scalar if i in smem else...]
    ppermute x4 -> x5, starting transfers between devices: 5.17 us -> 5.21 us  [swap(): return lax.ppermute(value, axis, [(i, i ^ distance) for i in range(peers)])]
  transfers between devices with their start and end apart: 8 -> 9, of which waited for: 6 -> 4; matrix products, arithmetic and copies ran while one was open for 0% -> 0% of each run, Pallas kernels for 7% -> 8%
where the time goes in v5:
time: 37.6 us; the launch traced here: 37.4 us
  waiting for transfers between devices  16.1 us (43%)
  starting transfers between devices  13 us (35%)
  Pallas kernels  7.59 us (20%)
  between operations  0.72 us (2%)
    ppermute x5, waiting for transfers between devices, swap(): return lax.ppermute(value, axis, [(i, i ^ distance) for i in range(peers)])  13.7 us
    pallas_call x9, Pallas kernels, run(): pl.pallas_call(kernel, out_shape=outs, in_specs=[scalar if i in smem else...  7.59 us
    ppermute x2, starting transfers between devices, body(): below = lax.ppermute(up, 'gx', upward)  5.9 us
    ppermute x5, starting transfers between devices, swap(): return lax.ppermute(value, axis, [(i, i ^ distance) for i in range(peers)])  5.21 us
    ppermute x2, waiting for transfers between devices, body(): above = lax.ppermute(down, 'gx', downward)  2.38 us
    ppermute x2, starting transfers between devices, body(): above = lax.ppermute(down, 'gx', downward)  1.9 us
  transfers between devices with their start and end apart: 9, of which 4 were waited for; matrix products, arithmetic and copies ran while one was open for 0% of the time, Pallas kernels for 8%

profile of v5, /device:TPU:0, one launch (start us, length us, event | category | flops | bytes accessed | tf_op | source)
XLA Modules:
  0.0 37.4 jit_solution(3360338289585940718)
XLA Ops:
  0.6 1.6 %shard_map.68 = (f32[96,128]{1,0:T(8,128)S(1)}, f32[192,128]{1,0:T(8,128)S(1)}, f32[192,512]{1,0:T(8,128)S(1)}, f32[16,256]{1,0:T(8,128)S(1)}, bf16[720,256]{1,0:T(8,128)(2,1)S(1)}, /*index=5*/f32[3,32,512]{2,1,0:T(8,128)S(1)}) custom-call(s32[6,32,512]{2,1,0:T(8,128)} %labels_hbm.1, bf16[6,32,512]{2,1,0:T(8,128)(2,1)} %background_hbm.1, f32[4]{0:T(128)} %contrasts_hbm.1, ...), custom_call_target="tpu_custom_call" | custom-call | tf_op jit(solution)/shard_map/pallas_call | solution.py:466
  2.3 0.6 %collective-permute-start = (f32[96,128]{1,0:T(8,128)S(1)}, f32[96,128]{1,0:T(8,128)S(1)}, u32[]{:S(2)}, u32[]{:S(2)}) collective-permute-start(f32[96,128]{1,0:T(8,128)S(1)} %get-tuple-element.27), channel_id=1, source_target_pairs={{0,2},{2,0},{1,3},{3,1},{4,6},{6,4},{5,7},{7,5},{8,10},{10,8},{9,1... | collective-permute-start | bytes 147464 | tf_op jit(solution)/shard_map/ppermute | solution.py:486
  2.8 0.7 %shard_map.69 = (f32[48,640]{1,0:T(8,128)S(1)}, f32[48,640]{1,0:T(8,128)S(1)}) custom-call(f32[192,512]{1,0:T(8,128)S(1)} %get-tuple-element.37.density_ref, bf16[720,256]{1,0:T(8,128)(2,1)S(1)} %get-tuple-element.24.bands_ref.refs_1_, f32[3,32,512]{2,1,0:T(8,128)S(1)} %get-tuple-element.25.observed_ref), custom_call_target="tpu_custom_call" | custom-call | tf_op jit(solution)/shard_map/pallas_call | solution.py:466
  3.5 0.2 collective-permute-done.edge_ref
  3.7 0.2 shard_map.70.part_ref
  3.9 2.8 %collective-permute-start.5 = (f32[192,512]{1,0:T(8,128)S(1)}, f32[192,512]{1,0:T(8,128)S(1)}, u32[]{:S(2)}, u32[]{:S(2)}) collective-permute-start(f32[192,512]{1,0:T(8,128)S(1)} %get-tuple-element.37.density_ref), channel_id=1, source_target_pairs={{0,1},{1,0},{2,3},{3,2},{4,5},{5,4},{6,7},{7,6},{8,9},{9,8},{10,11... | collective-permute-start | bytes 1179656 | tf_op jit(solution)/shard_map/ppermute | solution.py:486
  6.8 0.1 collective-permute-start.1
  6.8 11.5 %collective-permute-done.1.other_ref = f32[48,512]{1,0:T(8,128)S(1)} collective-permute-done((f32[48,512]{1,0:T(8,128)S(1)}, f32[48,512]{1,0:T(8,128)S(1)}, u32[]{:S(2)}, u32[]{:S(2)}) %collective-permute-start.1) | collective-permute-done | bytes 98336 | tf_op jit(solution)/shard_map/ppermute | solution.py:486
  18.3 0.2 shard_map.71
  18.5 1.8 %collective-permute-start.2 = (f32[24,640]{1,0:T(8,128)S(1)}, f32[24,640]{1,0:T(8,128)S(1)}, u32[]{:S(2)}, u32[]{:S(2)}) collective-permute-start(f32[24,640]{1,0:T(8,128)S(1)} %get-tuple-element.30), channel_id=1, source_target_pairs={{12,0},{0,4},{4,8},{8,12},{13,1},{1,5},{5,9},{9,13},{14,2},{2,6},{... | collective-permute-start | bytes 184328 | tf_op jit(solution)/shard_map/ppermute | solution.py:573
  20.3 2.1 %collective-permute-start.3 = (f32[24,640]{1,0:T(8,128)S(1)}, f32[24,640]{1,0:T(8,128)S(1)}, u32[]{:S(2)}, u32[]{:S(2)}) collective-permute-start(f32[24,640]{1,0:T(8,128)S(1)} %get-tuple-element.31), channel_id=1, source_target_pairs={{0,12},{4,0},{8,4},{12,8},{1,13},{5,1},{9,5},{13,9},{2,14},{6,2},{... | collective-permute-start | bytes 184328 | tf_op jit(solution)/shard_map/ppermute | solution.py:572
  22.4 1.7 %collective-permute-start.4 = (f32[16,256]{1,0:T(8,128)S(1)}, f32[16,256]{1,0:T(8,128)S(1)}, u32[]{:S(2)}, u32[]{:S(2)}) collective-permute-start(f32[16,256]{1,0:T(8,128)S(1)} %get-tuple-element.34), channel_id=1, source_target_pairs={{0,1},{1,0},{2,3},{3,2},{4,5},{5,4},{6,7},{7,6},{8,9},{9,8},{10,11... | collective-permute-start | bytes 49160 | tf_op jit(solution)/shard_map/ppermute | solution.py:486
  24.1 2.1 %collective-permute-done.4.refs_0_ = f32[16,256]{1,0:T(8,128)S(1)} collective-permute-done((f32[16,256]{1,0:T(8,128)S(1)}, f32[16,256]{1,0:T(8,128)S(1)}, u32[]{:S(2)}, u32[]{:S(2)}) %collective-permute-start.4) | collective-permute-done | bytes 16416 | tf_op jit(solution)/shard_map/ppermute | solution.py:486
  26.2 0.4 %shard_map.72 = (bf16[720,512]{1,0:T(8,128)(2,1)S(1)}, bf16[512,720]{1,0:T(8,128)(2,1)S(1)}) custom-call(f32[16,256]{1,0:T(8,128)S(1)} %collective-permute-done.4.refs_0_, bf16[720,256]{1,0:T(8,128)(2,1)S(1)} %get-tuple-element.24.bands_ref.refs_1_), custom_call_target="tpu_custom_call" | custom-call | tf_op jit(solution)/shard_map/pallas_call | solution.py:466
  26.6 0.0 collective-permute-done.3.below_ref
  26.6 1.3 %shard_map.74 = f32[48,128]{1,0:T(8,128)S(1)} custom-call(f32[48,640]{1,0:T(8,128)S(1)} %get-tuple-element.29.sum_ref, f32[24,640]{1,0:T(8,128)S(1)} %collective-permute-done.2.above_ref, f32[24,640]{1,0:T(8,128)S(1)} %collective-permute-done.3.below_ref, f32[48,640]{1,0:T(8,128)S(1)} %get-tuple-element.32.q_ref, ...), custom_call_target="tpu_custom_call" | custom-call | tf_op jit(solution)/shard_map/pallas_call | solution.py:466
  27.9 0.1 collective-permute-start.6
  28.0 1.6 %shard_map.73 = (f32[48,640]{1,0:T(8,128)S(1)}, f32[48,640]{1,0:T(8,128)S(1)}) custom-call(f32[48,640]{1,0:T(8,128)S(1)} %get-tuple-element.29.sum_ref, f32[24,640]{1,0:T(8,128)S(1)} %collective-permute-done.2.above_ref, f32[24,640]{1,0:T(8,128)S(1)} %collective-permute-done.3.below_ref, f32[48,640]{1,0:T(8,128)S(1)} %get-tuple-element.32.q_ref, ...), custom_call_target="tpu_custom_call" | custom-call | tf_op jit(solution)/shard_map/pallas_call | solution.py:466
  29.6 0.0 collective-permute-done.6.edge_ref
  29.6 0.1 shard_map.75
  29.7 0.1 collective-permute-start.7
  29.7 3.8 %collective-permute-start.8 = (f32[16,640]{1,0:T(8,128)S(1)}, f32[16,640]{1,0:T(8,128)S(1)}, u32[]{:S(2)}, u32[]{:S(2)}) collective-permute-start(f32[16,640]{1,0:T(8,128)S(1)} %get-tuple-element.42), channel_id=1, source_target_pairs={{0,12},{4,0},{8,4},{12,8},{1,13},{5,1},{9,5},{13,9},{2,14},{6,2},{... | collective-permute-start | bytes 122888 | tf_op jit(solution)/shard_map/ppermute | solution.py:572
  33.5 2.4 %collective-permute-done.7.above_ref = f32[16,640]{1,0:T(8,128)S(1)} collective-permute-done((f32[16,640]{1,0:T(8,128)S(1)}, f32[16,640]{1,0:T(8,128)S(1)}, u32[]{:S(2)}, u32[]{:S(2)}) %collective-permute-start.7) | collective-permute-done | bytes 40992 | tf_op jit(solution)/shard_map/ppermute | solution.py:573
  35.9 1.5 %shard_map.76 = (f32[3,16,512]{2,1,0:T(8,128)}, f32[6,32,512]{2,1,0:T(8,128)}) custom-call(s32[1]{0:T(128)} %bitcast.start_ref, f32[48,640]{1,0:T(8,128)S(1)} %get-tuple-element.40.sum_ref, f32[16,640]{1,0:T(8,128)S(1)} %collective-permute-done.7.above_ref, f32[16,640]{1,0:T(8,128)S(1)} %collective-permute-done.8.below_ref, ...), custom_call_target="tpu_custom_call" | custom-call | tf_op jit(solution)/shard_map/pallas_call | solution.py:466
  (3 shorter events, 0.0 us)
Async XLA Ops:
  2.3 1.4 %collective-permute-start = (f32[96,128]{1,0:T(8,128)S(1)}, f32[96,128]{1,0:T(8,128)S(1)}, u32[]{:S(2)}, u32[]{:S(2)}) collective-permute-start(f32[96,128]{1,0:T(8,128)S(1)} %get-tuple-element.27), channel_id=1, source_target_pairs={{0,2},{2,0},{1,3},{3,1},{4,6},{6,4},{5,7},{7,5},{8,10},{10,8},{9,1... | collective-permute-start | bytes 147464 | tf_op jit(solution)/shard_map/ppermute | solution.py:486
  3.9 22.7 %collective-permute-start.5 = (f32[192,512]{1,0:T(8,128)S(1)}, f32[192,512]{1,0:T(8,128)S(1)}, u32[]{:S(2)}, u32[]{:S(2)}) collective-permute-start(f32[192,512]{1,0:T(8,128)S(1)} %get-tuple-element.37.density_ref), channel_id=1, source_target_pairs={{0,1},{1,0},{2,3},{3,2},{4,5},{5,4},{6,7},{7,6},{8,9},{9,8},{10,11... | collective-permute-start | bytes 1179656 | tf_op jit(solution)/shard_map/ppermute | solution.py:486
  6.8 11.5 %collective-permute-start.1 = (f32[48,512]{1,0:T(8,128)S(1)}, f32[48,512]{1,0:T(8,128)S(1)}, u32[]{:S(2)}, u32[]{:S(2)}) collective-permute-start(f32[48,512]{1,0:T(8,128)S(1)} %shard_map.70.part_ref), channel_id=1, source_target_pairs={{0,1},{1,0},{2,3},{3,2},{4,5},{5,4},{6,7},{7,6},{8,9},{9,8},{10,11... | collective-permute-start | bytes 294920 | tf_op jit(solution)/shard_map/ppermute | solution.py:486
  18.5 8.1 %collective-permute-start.2 = (f32[24,640]{1,0:T(8,128)S(1)}, f32[24,640]{1,0:T(8,128)S(1)}, u32[]{:S(2)}, u32[]{:S(2)}) collective-permute-start(f32[24,640]{1,0:T(8,128)S(1)} %get-tuple-element.30), channel_id=1, source_target_pairs={{12,0},{0,4},{4,8},{8,12},{13,1},{1,5},{5,9},{9,13},{14,2},{2,6},{... | collective-permute-start | bytes 184328 | tf_op jit(solution)/shard_map/ppermute | solution.py:573
  20.3 6.2 %collective-permute-start.3 = (f32[24,640]{1,0:T(8,128)S(1)}, f32[24,640]{1,0:T(8,128)S(1)}, u32[]{:S(2)}, u32[]{:S(2)}) collective-permute-start(f32[24,640]{1,0:T(8,128)S(1)} %get-tuple-element.31), channel_id=1, source_target_pairs={{0,12},{4,0},{8,4},{12,8},{1,13},{5,1},{9,5},{13,9},{2,14},{6,2},{... | collective-permute-start | bytes 184328 | tf_op jit(solution)/shard_map/ppermute | solution.py:572
  22.4 3.7 %collective-permute-start.4 = (f32[16,256]{1,0:T(8,128)S(1)}, f32[16,256]{1,0:T(8,128)S(1)}, u32[]{:S(2)}, u32[]{:S(2)}) collective-permute-start(f32[16,256]{1,0:T(8,128)S(1)} %get-tuple-element.34), channel_id=1, source_target_pairs={{0,1},{1,0},{2,3},{3,2},{4,5},{5,4},{6,7},{7,6},{8,9},{9,8},{10,11... | collective-permute-start | bytes 49160 | tf_op jit(solution)/shard_map/ppermute | solution.py:486
  27.9 1.7 %collective-permute-start.6 = (f32[48,128]{1,0:T(8,128)S(1)}, f32[48,128]{1,0:T(8,128)S(1)}, u32[]{:S(2)}, u32[]{:S(2)}) collective-permute-start(f32[48,128]{1,0:T(8,128)S(1)} %shard_map.74), channel_id=1, source_target_pairs={{0,2},{2,0},{1,3},{3,1},{4,6},{6,4},{5,7},{7,5},{8,10},{10,8},{9,1... | collective-permute-start | bytes 73736 | tf_op jit(solution)/shard_map/ppermute | solution.py:486
  29.7 6.3 %collective-permute-start.7 = (f32[16,640]{1,0:T(8,128)S(1)}, f32[16,640]{1,0:T(8,128)S(1)}, u32[]{:S(2)}, u32[]{:S(2)}) collective-permute-start(f32[16,640]{1,0:T(8,128)S(1)} %get-tuple-element.41), channel_id=1, source_target_pairs={{12,0},{0,4},{4,8},{8,12},{13,1},{1,5},{5,9},{9,13},{14,2},{2,6},{... | collective-permute-start | bytes 122888 | tf_op jit(solution)/shard_map/ppermute | solution.py:573
  29.7 6.2 %collective-permute-start.8 = (f32[16,640]{1,0:T(8,128)S(1)}, f32[16,640]{1,0:T(8,128)S(1)}, u32[]{:S(2)}, u32[]{:S(2)}) collective-permute-start(f32[16,640]{1,0:T(8,128)S(1)} %get-tuple-element.42), channel_id=1, source_target_pairs={{0,12},{4,0},{8,4},{12,8},{1,13},{5,1},{9,5},{13,9},{2,14},{6,2},{... | collective-permute-start | bytes 122888 | tf_op jit(solution)/shard_map/ppermute | solution.py:572

commit v6 on v4

--- a/solution.py
+++ b/solution.py
@@ -106,7 +106,7 @@
     return jnp.concatenate([first, field[:, 128 : width - 256], last, side], axis=1)
 
 
-def build_bands(k_ref, taps_ref, base_ref, bands_ref):
+def kernel_rows(k_ref, taps_ref):
     layers, span, _ = k_ref.shape
     taps_ref[...] = jnp.zeros(taps_ref.shape, f32)
     for l in range(layers):
@@ -114,18 +114,22 @@
     shape = (taps_ref.shape[0], WIDE)
     source = iota(shape, 0)
     place = jnp.where(32 * (source >> 4) + (source & 15) == iota(shape, 1), 1.0, 0.0)
-    base_ref[...] = lax.dot_general(
+    return lax.dot_general(
         taps_ref[...].astype(bf16),
         place.astype(bf16),
         (((0,), (0,)), ((), ())),
         preferred_element_type=f32,
     )
+
+
+def build_bands(base_ref, bands_ref, span):
     tap = (iota((8, 128), 1) & 31) - iota((8, 128), 0) + 15
     keep = [(tap - 8 * g >= 0) & (tap - 8 * g < span) for g in range(PART // 8)]
     for block in range(WIDE // 128):
-        columns = slice(128 * block, 128 * block + 128)
         for j in range(span):
-            row = jnp.broadcast_to(base_ref[j : j + 1, columns], (8, 128))
+            row = jnp.broadcast_to(
+                base_ref[j : j + 1, 128 * block : 128 * block + 128], (8, 128)
+            )
             moved = [
                 jnp.where(
                     keep[g],
@@ -134,9 +138,9 @@
                 )
                 for g in range(PART // 8)
             ]
-            bands_ref[j * PART : (j + 1) * PART, columns] = jnp.concatenate(
-                moved, axis=0
-            ).astype(bf16)
+            bands_ref[
+                j * PART : (j + 1) * PART, 128 * block : 128 * block + 128
+            ] = jnp.concatenate(moved, axis=0).astype(bf16)
 
 
 def edge_message(bands, rounded, prod_ref, span, radius):
@@ -203,7 +207,8 @@
     for copy in copies:
         copy.start()
     copies[0].wait()
-    build_bands(k_ref, taps_ref, base_ref, bands_ref)
+    base_ref[...] = kernel_rows(k_ref, taps_ref)
+    build_bands(base_ref, bands_ref, span)
     for copy in copies[1:]:
         copy.wait()
     classes = contrasts_ref.shape[0]
@@ -266,6 +271,14 @@
         out_ref[row : row + 1, 128 * (n % 4) : 128 * (n % 4 + 1)] = folded[n : n + 1]
 
 
+def send_rows(sum_ref, up_ref, down_ref):
+    sub = iota((8, sum_ref.shape[1]), 0)
+    up_ref[:8, :] = sum_ref[8:16, :]
+    up_ref[8:16, :] = jnp.where(sub >= 1, sum_ref[:8, :], sum_ref[16:24, :])
+    down_ref[:8, :] = sum_ref[32:40, :]
+    down_ref[8:16, :] = jnp.where(sub < 7, sum_ref[40:48, :], sum_ref[24:32, :])
+
+
 def rows_kernel(
     part_ref, other_ref, q_ref, edge_ref, sum_ref, up_ref, down_ref, q_out_ref, fold_ref
 ):
@@ -278,12 +291,9 @@
     zero = jnp.zeros((1, cells_y), f32)
     sum_ref[:1, :cells_y] = zero
     sum_ref[PART - 1 :, :cells_y] = zero
-    sub = iota((8, sum_ref.shape[1]), 0)
-    up_ref[:8, :] = sum_ref[8:16, :]
-    up_ref[8:16, :] = jnp.where(sub >= 1, sum_ref[:8, :], sum_ref[16:24, :])
-    down_ref[:8, :] = sum_ref[32:40, :]
-    down_ref[8:16, :] = jnp.where(sub < 7, sum_ref[40:48, :], sum_ref[24:32, :])
+    send_rows(sum_ref, up_ref, down_ref)
     if q_ref is not None:
+        sub = iota((8, sum_ref.shape[1]), 0)
         q_out_ref[...] = add_edges(q_ref[...], edge_ref[PART:, :])
         up_ref[16:24, :] = jnp.where(sub < 7, q_out_ref[8:16, :], q_out_ref[:8, :])
         down_ref[16:24, :] = jnp.where(sub >= 1, q_out_ref[32:40, :], q_out_ref[40:48, :])
@@ -327,39 +337,17 @@
     for j in range(span):
         shift = (j - radius) % adjoint.shape[1]
         moved = pltpu.roll(adjoint, shift, 1) if shift else adjoint
-        stack_ref[j * PART : (j + 1) * PART, columns] = moved[:, columns].astype(bf16)
+        stack_ref[j * PART : (j + 1) * PART, columns] = moved[:, columns]
 
 
 def rounded_adjoint(s, q):
-    return (adjoint_square(s) - q).astype(bf16).astype(f32)
-
-
-def middle_kernel(
-    sum_ref, above_ref, below_ref, q_ref, density_edge_ref, bands_ref, turned_ref,
-    edge_ref,
-    stack_ref, prod_ref, *, span,
-):
-    radius = (span - 1) // 2
-    lanes = density_edge_ref.shape[0]
-    total, q = edges_of(sum_ref[...]), edges_of(q_ref[...])
-    above, below = edges_of(above_ref[...]), edges_of(below_ref[...])
-    adjoint = rounded_adjoint(full_surface(total, above, below), full_q(q, above, below))
-    stack_shifts(adjoint, stack_ref, slice(0, 128), span, radius)
-    gradient = jnp.dot(turned_ref[:lanes, :], stack_ref[...], preferred_element_type=f32)
-    density = density_edge_ref[...] - descent * gradient
-    lane = iota(density.shape, 1)
-    keep = ((lane >= 32) & (lane < 48)) | (lane >= 112)
-    density = jnp.where(keep, density, 0.0)
-    edge_ref[...] = edge_message(
-        bands_ref[:, :lanes], density.astype(bf16), prod_ref, span, radius
-    )
-
-
-def middle_field_kernel(
-    sum_ref, above_ref, below_ref, q_ref, density_ref, bands_ref, turned_ref,
-    part_ref, q_out_ref,
-    stack_ref, prod_ref, *, span,
-):
+    return (adjoint_square(s) - q).astype(bf16)
+
+
+def field_after_step(refs, out_refs, scratch_refs, span):
+    sum_ref, above_ref, below_ref, q_ref, density_ref, bands_ref, turned_ref = refs
+    part_ref, q_out_ref = out_refs
+    stack_ref, prod_ref = scratch_refs
     radius = (span - 1) // 2
     lanes, cells_y = density_ref.shape
     above, below = above_ref[...], below_ref[...]
@@ -372,6 +360,55 @@
     part_ref[...] = scatter_surface(
         bands_ref[:, :lanes], density.astype(bf16), prod_ref, span, radius
     )
+
+
+def middle_kernel(
+    sum_ref, above_ref, below_ref, q_ref, density_ref, bands_ref, turned_ref,
+    density_edge_ref,
+    edge_ref, part_ref, q_out_ref,
+    edge_stack_ref, edge_prod_ref, stack_ref, prod_ref, *, span,
+):
+    radius = (span - 1) // 2
+    lanes = density_edge_ref.shape[0]
+    total, q = edges_of(sum_ref[...]), edges_of(q_ref[...])
+    above, below = edges_of(above_ref[...]), edges_of(below_ref[...])
+    adjoint = rounded_adjoint(full_surface(total, above, below), full_q(q, above, below))
+    stack_shifts(adjoint, edge_stack_ref, slice(0, 128), span, radius)
+    gradient = jnp.dot(
+        turned_ref[:lanes, :], edge_stack_ref[...], preferred_element_type=f32
+    )
+    density = density_edge_ref[...] - descent * gradient
+    lane = iota(density.shape, 1)
+    keep = ((lane >= 32) & (lane < 48)) | (lane >= 112)
+    density = jnp.where(keep, density, 0.0)
+    edge_ref[...] = edge_message(
+        bands_ref[:, :lanes], density.astype(bf16), edge_prod_ref, span, radius
+    )
+
+    @pl.when(lax.axis_index("gy") == 1)
+    def _():
+        field_after_step(
+            (sum_ref, above_ref, below_ref, q_ref, density_ref, bands_ref, turned_ref),
+            (part_ref, q_out_ref),
+            (stack_ref, prod_ref),
+            span,
+        )
+
+
+def middle_field_kernel(
+    sum_ref, above_ref, below_ref, q_ref, density_ref, bands_ref, turned_ref,
+    part_in_ref, q_in_ref,
+    part_ref, q_out_ref,
+    stack_ref, prod_ref, *, span,
+):
+    @pl.when(lax.axis_index("gy") == 0)
+    def _():
+        field_after_step(
+            (sum_ref, above_ref, below_ref, q_ref, density_ref, bands_ref, turned_ref),
+            (part_ref, q_out_ref),
+            (stack_ref, prod_ref),
+            span,
+        )
 
 
 def last_kernel(
@@ -400,19 +437,22 @@
         )
         copies[-1].start()
     share = residual_ref.shape[1]
-    for start in range(0, cells_x, share):
-
-        @pl.when(start_ref[0] == start)
-        def _():
-            top = 16 + start
-            low, high = (top - 1) // 8 * 8, -(-(top + share + 1) // 8) * 8
-            fields = tensor_fields(full_ref[low:high, :])
-            for k in range(3):
-                misfit_ref[k, : high - low, :] = fields[k][:, :cells_y]
-                residual_ref[k] = (
-                    misfit_ref[k, top - low : top - low + share, :]
-                    - observed_ref[k, start : start + share, :]
-                )
+    if share % 8 == 0:
+        start = pl.multiple_of(start_ref[0], 8)
+        fields = tensor_fields(full_ref[pl.ds(start + 8, share + 16), :])
+        for k in range(3):
+            residual_ref[k] = (
+                fields[k][8 : 8 + share, :cells_y] - observed_ref[k, pl.ds(start, share), :]
+            )
+    else:
+        fields = tensor_fields(full_ref[...])
+        for k in range(3):
+            misfit_ref[k] = fields[k][16 : 16 + cells_x, :cells_y] - observed_ref[k]
+        for start in range(0, cells_x, share):
+
+            @pl.when(start_ref[0] == start)
+            def _():
+                residual_ref[...] = misfit_ref[:, start : start + share, :]
 
     copies.append(pltpu.make_async_copy(residual_ref, residual_hbm, sems.at[2]))
     copies[-1].start()
@@ -420,7 +460,9 @@
         copy.wait()
 
 
-def call(kernel, outs, scratch=(), inputs=pltpu.VMEM, smem=(), results=pltpu.VMEM):
+def call(
+    kernel, outs, scratch=(), inputs=pltpu.VMEM, smem=(), results=pltpu.VMEM, aliases={}
+):
     made = pl.BlockSpec(memory_space=results)
     given = pl.BlockSpec(memory_space=inputs)
     scalar = pl.BlockSpec(memory_space=pltpu.SMEM)
@@ -437,6 +479,7 @@
                 item if not isinstance(item, tuple) else pltpu.VMEM(*item) for item in scratch
             ],
             compiler_params=pltpu.CompilerParams(vmem_limit_bytes=GRANT),
+            input_output_aliases=aliases,
         )(*operands)
 
     return run
@@ -496,16 +539,16 @@
     part, q = call(
         kernel_of(first_field_kernel), (field, field), (prod, ((3, PART, width), f32))
     )(density, bands, observed)
+    start = (lax.axis_index("gz") * share).astype(jnp.int32).reshape(1)
+
     turned = call(transpose_kernel, shaped((WIDE, span * PART), bf16))(bands)
-    start = (lax.axis_index("gz") * share).astype(jnp.int32).reshape(1)
-
+    fold = (((8, 128), f32),)
     for iteration in range(ITERS):
         others = swap(edge, "gy", 1)
         part = call(edges_kernel, shaped((PART, cells_y)))(part, others)
         for bit in range(depth_peers.bit_length() - 2):
             part = part + swap(part, "gz", 2 << bit)
         other = swap(part, "gz", 1)
-        fold = (((8, 128), f32),)
         if iteration == 0:
             total, up, down, q = call(
                 rows_kernel, (field, shaped((24, width)), shaped((24, width)), field), fold
@@ -519,12 +562,18 @@
         below = lax.ppermute(up, "gx", upward)
         above = lax.ppermute(down, "gx", downward)
         if iteration == 0:
-            edge = call(
-                kernel_of(middle_kernel), shaped((PART, 128)), (edge_stack, edge_prod)
-            )(total, above, below, q, density_edge, bands, turned)
-            part, q = call(kernel_of(middle_field_kernel), (field, field), (stack, prod))(
-                total, above, below, q, density, bands, turned
-            )
+            known = (total, above, below, q, density, bands, turned)
+            edge, part, q = call(
+                kernel_of(middle_kernel),
+                (shaped((PART, 128)), field, field),
+                (edge_stack, edge_prod, stack, prod),
+            )(*known, density_edge)
+            part, q = call(
+                kernel_of(middle_field_kernel),
+                (field, field),
+                (stack, prod),
+                aliases={7: 0, 8: 1},
+            )(*known, part, q)
     return call(
         kernel_of(last_kernel),
         (shaped((3, share, cells_y)), shaped((layers, cells_x, cells_y))),

time: 32.5 us -> 31.6 us (0.972)
  waiting for transfers between devices: 11.8 us -> 11 us
    ppermute x4, waiting for transfers between devices: 6.82 us -> 6.36 us  [swap(): return lax.ppermute(value, axis, [(i, i ^ distance) for i in range(peers)])]
    ppermute x2, waiting for transfers between devices: 4.88 us -> 4.56 us  [body(): above = lax.ppermute(down, 'gx', downward)]
where the time goes in v6:
time: 31.6 us; the launch traced here: 31.5 us
  starting transfers between devices  12.9 us (41%)
  waiting for transfers between devices  11 us (35%)
  Pallas kernels  6.9 us (22%)
  between operations  0.69 us (2%)
    pallas_call x10, Pallas kernels, run(): pl.pallas_call(kernel, out_shape=outs, in_specs=[scalar if i in smem else...  6.9 us
    ppermute x4, waiting for transfers between devices, swap(): return lax.ppermute(value, axis, [(i, i ^ distance) for i in range(peers)])  6.36 us
    ppermute x4, starting transfers between devices, swap(): return lax.ppermute(value, axis, [(i, i ^ distance) for i in range(peers)])  5.16 us
    ppermute x2, starting transfers between devices, body(): below = lax.ppermute(up, 'gx', upward)  4.89 us
    ppermute x2, waiting for transfers between devices, body(): above = lax.ppermute(down, 'gx', downward)  4.56 us
    ppermute x2, starting transfers between devices, body(): above = lax.ppermute(down, 'gx', downward)  2.87 us
  transfers between devices with their start and end apart: 8, of which 6 were waited for; matrix products, arithmetic and copies ran while one was open for 0% of the time, Pallas kernels for 7%

profile of v6, /device:TPU:0, one launch (start us, length us, event | category | flops | bytes accessed | tf_op | source)
XLA Modules:
  0.0 31.5 jit_solution(7220864247850065517)
XLA Ops:
  0.6 1.6 %shard_map.68 = (f32[96,128]{1,0:T(8,128)S(1)}, f32[192,128]{1,0:T(8,128)S(1)}, f32[192,512]{1,0:T(8,128)S(1)}, bf16[720,256]{1,0:T(8,128)(2,1)S(1)}, f32[3,32,512]{2,1,0:T(8,128)S(1)}) custom-call(s32[6,32,512]{2,1,0:T(8,128)} %labels_hbm.1, bf16[6,32,512]{2,1,0:T(8,128)(2,1)} %background_hbm.1, f32[4]{0:T(128)} %contrasts_hbm.1, bf16[6,15,15]{2,1,0:T(8,128)(2,1)} %k_hbm.1, ...), custom_call_target="tpu_custom_call" | custom-call | tf_op jit(solution)/shard_map/pallas_call | solution.py:473
  2.3 0.6 %collective-permute-start = (f32[96,128]{1,0:T(8,128)S(1)}, f32[96,128]{1,0:T(8,128)S(1)}, u32[]{:S(2)}, u32[]{:S(2)}) collective-permute-start(f32[96,128]{1,0:T(8,128)S(1)} %get-tuple-element.25), channel_id=1, source_target_pairs={{0,2},{2,0},{1,3},{3,1},{4,6},{6,4},{5,7},{7,5},{8,10},{10,8},{9,1... | collective-permute-start | bytes 147464 | tf_op jit(solution)/shard_map/ppermute | solution.py:494
  2.8 0.7 %shard_map.69 = (f32[48,640]{1,0:T(8,128)S(1)}, f32[48,640]{1,0:T(8,128)S(1)}) custom-call(f32[192,512]{1,0:T(8,128)S(1)} %get-tuple-element.21.density_ref, bf16[720,256]{1,0:T(8,128)(2,1)S(1)} %get-tuple-element.22.bands_ref, f32[3,32,512]{2,1,0:T(8,128)S(1)} %get-tuple-element.23.observed_ref), custom_call_target="tpu_custom_call" | custom-call | tf_op jit(solution)/shard_map/pallas_call | solution.py:473
  3.5 0.2 collective-permute-done.edge_ref
  3.7 0.2 shard_map.70.part_ref
  3.9 2.8 %collective-permute-start.1 = (f32[48,512]{1,0:T(8,128)S(1)}, f32[48,512]{1,0:T(8,128)S(1)}, u32[]{:S(2)}, u32[]{:S(2)}) collective-permute-start(f32[48,512]{1,0:T(8,128)S(1)} %shard_map.70.part_ref), channel_id=1, source_target_pairs={{0,1},{1,0},{2,3},{3,2},{4,5},{5,4},{6,7},{7,6},{8,9},{9,8},{10,11... | collective-permute-start | bytes 294920 | tf_op jit(solution)/shard_map/ppermute | solution.py:494
  6.8 3.1 %collective-permute-done.1.other_ref = f32[48,512]{1,0:T(8,128)S(1)} collective-permute-done((f32[48,512]{1,0:T(8,128)S(1)}, f32[48,512]{1,0:T(8,128)S(1)}, u32[]{:S(2)}, u32[]{:S(2)}) %collective-permute-start.1) | collective-permute-done | bytes 98336 | tf_op jit(solution)/shard_map/ppermute | solution.py:494
  9.9 0.2 shard_map.71
  10.1 1.8 %collective-permute-start.2 = (f32[24,640]{1,0:T(8,128)S(1)}, f32[24,640]{1,0:T(8,128)S(1)}, u32[]{:S(2)}, u32[]{:S(2)}) collective-permute-start(f32[24,640]{1,0:T(8,128)S(1)} %get-tuple-element.28), channel_id=1, source_target_pairs={{12,0},{0,4},{4,8},{8,12},{13,1},{1,5},{5,9},{9,13},{14,2},{2,6},{... | collective-permute-start | bytes 184328 | tf_op jit(solution)/shard_map/ppermute | solution.py:563
  11.9 2.1 %collective-permute-start.3 = (f32[24,640]{1,0:T(8,128)S(1)}, f32[24,640]{1,0:T(8,128)S(1)}, u32[]{:S(2)}, u32[]{:S(2)}) collective-permute-start(f32[24,640]{1,0:T(8,128)S(1)} %get-tuple-element.29), channel_id=1, source_target_pairs={{0,12},{4,0},{8,4},{12,8},{1,13},{5,1},{9,5},{13,9},{2,14},{6,2},{... | collective-permute-start | bytes 184328 | tf_op jit(solution)/shard_map/ppermute | solution.py:562
  14.0 0.2 shard_map.72.turned_ref
  14.2 2.5 %collective-permute-done.2.above_ref = f32[24,640]{1,0:T(8,128)S(1)} collective-permute-done((f32[24,640]{1,0:T(8,128)S(1)}, f32[24,640]{1,0:T(8,128)S(1)}, u32[]{:S(2)}, u32[]{:S(2)}) %collective-permute-start.2) | collective-permute-done | bytes 61472 | tf_op jit(solution)/shard_map/ppermute | solution.py:563
  16.7 0.1 collective-permute-done.3.below_ref
  16.8 0.8 %shard_map.73 = (f32[48,128]{1,0:T(8,128)S(1)}, f32[48,640]{1,0:T(8,128)S(1)}, f32[48,640]{1,0:T(8,128)S(1)}) custom-call(f32[48,640]{1,0:T(8,128)S(1)} %get-tuple-element.27.sum_ref, f32[24,640]{1,0:T(8,128)S(1)} %collective-permute-done.2.above_ref, f32[24,640]{1,0:T(8,128)S(1)} %collective-permute-done.3.below_ref, ...), custom_call_target="tpu_custom_call" | custom-call | tf_op jit(solution)/shard_map/pallas_call | solution.py:473
  17.6 0.1 collective-permute-start.4
  17.7 1.3 %shard_map.74 = (f32[48,640]{1,0:T(8,128)S(1)}, f32[48,640]{1,0:T(8,128)S(1)}) custom-call(f32[48,640]{1,0:T(8,128)S(1)} %get-tuple-element.27.sum_ref, f32[24,640]{1,0:T(8,128)S(1)} %collective-permute-done.2.above_ref, f32[24,640]{1,0:T(8,128)S(1)} %collective-permute-done.3.below_ref, ...), custom_call_target="tpu_custom_call", output_to_operand_aliasing={{0}: (7, {}), {1}: (8, {})} | custom-call | tf_op jit(solution)/shard_map/pallas_call | solution.py:473
  19.0 0.2 shard_map.75.a
  19.2 1.7 %collective-permute-start.5 = (f32[48,512]{1,0:T(8,128)S(1)}, f32[48,512]{1,0:T(8,128)S(1)}, u32[]{:S(2)}, u32[]{:S(2)}) collective-permute-start(f32[48,512]{1,0:T(8,128)S(1)} %shard_map.75.a), channel_id=1, source_target_pairs={{0,1},{1,0},{2,3},{3,2},{4,5},{5,4},{6,7},{7,6},{8,9},{9,8},{10,11... | collective-permute-start | bytes 294920 | tf_op jit(solution)/shard_map/ppermute | solution.py:494
  20.9 3.1 %collective-permute-done.5.b = f32[48,512]{1,0:T(8,128)S(1)} collective-permute-done((f32[48,512]{1,0:T(8,128)S(1)}, f32[48,512]{1,0:T(8,128)S(1)}, u32[]{:S(2)}, u32[]{:S(2)}) %collective-permute-start.5) | collective-permute-done | bytes 98336 | tf_op jit(solution)/shard_map/ppermute | solution.py:494
  24.0 0.2 shard_map.76
  24.1 1.0 %collective-permute-start.6 = (f32[16,640]{1,0:T(8,128)S(1)}, f32[16,640]{1,0:T(8,128)S(1)}, u32[]{:S(2)}, u32[]{:S(2)}) collective-permute-start(f32[16,640]{1,0:T(8,128)S(1)} %get-tuple-element.37), channel_id=1, source_target_pairs={{12,0},{0,4},{4,8},{8,12},{13,1},{1,5},{5,9},{9,13},{14,2},{2,6},{... | collective-permute-start | bytes 122888 | tf_op jit(solution)/shard_map/ppermute | solution.py:563
  25.2 2.8 %collective-permute-start.7 = (f32[16,640]{1,0:T(8,128)S(1)}, f32[16,640]{1,0:T(8,128)S(1)}, u32[]{:S(2)}, u32[]{:S(2)}) collective-permute-start(f32[16,640]{1,0:T(8,128)S(1)} %get-tuple-element.38), channel_id=1, source_target_pairs={{0,12},{4,0},{8,4},{12,8},{1,13},{5,1},{9,5},{13,9},{2,14},{6,2},{... | collective-permute-start | bytes 122888 | tf_op jit(solution)/shard_map/ppermute | solution.py:562
  28.0 2.0 %collective-permute-done.6.above_ref = f32[16,640]{1,0:T(8,128)S(1)} collective-permute-done((f32[16,640]{1,0:T(8,128)S(1)}, f32[16,640]{1,0:T(8,128)S(1)}, u32[]{:S(2)}, u32[]{:S(2)}) %collective-permute-start.6) | collective-permute-done | bytes 40992 | tf_op jit(solution)/shard_map/ppermute | solution.py:563
  30.0 1.5 %shard_map.77 = (f32[3,16,512]{2,1,0:T(8,128)}, f32[6,32,512]{2,1,0:T(8,128)}) custom-call(s32[1]{0:T(128)} %bitcast.start_ref, f32[48,640]{1,0:T(8,128)S(1)} %get-tuple-element.36.sum_ref, f32[16,640]{1,0:T(8,128)S(1)} %collective-permute-done.6.above_ref, f32[16,640]{1,0:T(8,128)S(1)} %collective-permute-done.7.below_ref, ...), custom_call_target="tpu_custom_call" | custom-call | tf_op jit(solution)/shard_map/pallas_call | solution.py:473
  (2 shorter events, 0.0 us)
Async XLA Ops:
  2.3 1.4 %collective-permute-start = (f32[96,128]{1,0:T(8,128)S(1)}, f32[96,128]{1,0:T(8,128)S(1)}, u32[]{:S(2)}, u32[]{:S(2)}) collective-permute-start(f32[96,128]{1,0:T(8,128)S(1)} %get-tuple-element.25), channel_id=1, source_target_pairs={{0,2},{2,0},{1,3},{3,1},{4,6},{6,4},{5,7},{7,5},{8,10},{10,8},{9,1... | collective-permute-start | bytes 147464 | tf_op jit(solution)/shard_map/ppermute | solution.py:494
  3.9 6.0 %collective-permute-start.1 = (f32[48,512]{1,0:T(8,128)S(1)}, f32[48,512]{1,0:T(8,128)S(1)}, u32[]{:S(2)}, u32[]{:S(2)}) collective-permute-start(f32[48,512]{1,0:T(8,128)S(1)} %shard_map.70.part_ref), channel_id=1, source_target_pairs={{0,1},{1,0},{2,3},{3,2},{4,5},{5,4},{6,7},{7,6},{8,9},{9,8},{10,11... | collective-permute-start | bytes 294920 | tf_op jit(solution)/shard_map/ppermute | solution.py:494
  10.1 6.7 %collective-permute-start.2 = (f32[24,640]{1,0:T(8,128)S(1)}, f32[24,640]{1,0:T(8,128)S(1)}, u32[]{:S(2)}, u32[]{:S(2)}) collective-permute-start(f32[24,640]{1,0:T(8,128)S(1)} %get-tuple-element.28), channel_id=1, source_target_pairs={{12,0},{0,4},{4,8},{8,12},{13,1},{1,5},{5,9},{9,13},{14,2},{2,6},{... | collective-permute-start | bytes 184328 | tf_op jit(solution)/shard_map/ppermute | solution.py:563
  11.9 4.9 %collective-permute-start.3 = (f32[24,640]{1,0:T(8,128)S(1)}, f32[24,640]{1,0:T(8,128)S(1)}, u32[]{:S(2)}, u32[]{:S(2)}) collective-permute-start(f32[24,640]{1,0:T(8,128)S(1)} %get-tuple-element.29), channel_id=1, source_target_pairs={{0,12},{4,0},{8,4},{12,8},{1,13},{5,1},{9,5},{13,9},{2,14},{6,2},{... | collective-permute-start | bytes 184328 | tf_op jit(solution)/shard_map/ppermute | solution.py:562
  17.6 1.4 %collective-permute-start.4 = (f32[48,128]{1,0:T(8,128)S(1)}, f32[48,128]{1,0:T(8,128)S(1)}, u32[]{:S(2)}, u32[]{:S(2)}) collective-permute-start(f32[48,128]{1,0:T(8,128)S(1)} %get-tuple-element.35), channel_id=1, source_target_pairs={{0,2},{2,0},{1,3},{3,1},{4,6},{6,4},{5,7},{7,5},{8,10},{10,8},{9,1... | collective-permute-start | bytes 73736 | tf_op jit(solution)/shard_map/ppermute | solution.py:494
  19.2 4.7 %collective-permute-start.5 = (f32[48,512]{1,0:T(8,128)S(1)}, f32[48,512]{1,0:T(8,128)S(1)}, u32[]{:S(2)}, u32[]{:S(2)}) collective-permute-start(f32[48,512]{1,0:T(8,128)S(1)} %shard_map.75.a), channel_id=1, source_target_pairs={{0,1},{1,0},{2,3},{3,2},{4,5},{5,4},{6,7},{7,6},{8,9},{9,8},{10,11... | collective-permute-start | bytes 294920 | tf_op jit(solution)/shard_map/ppermute | solution.py:494
  24.1 5.8 %collective-permute-start.6 = (f32[16,640]{1,0:T(8,128)S(1)}, f32[16,640]{1,0:T(8,128)S(1)}, u32[]{:S(2)}, u32[]{:S(2)}) collective-permute-start(f32[16,640]{1,0:T(8,128)S(1)} %get-tuple-element.37), channel_id=1, source_target_pairs={{12,0},{0,4},{4,8},{8,12},{13,1},{1,5},{5,9},{9,13},{14,2},{2,6},{... | collective-permute-start | bytes 122888 | tf_op jit(solution)/shard_map/ppermute | solution.py:563
  25.2 4.8 %collective-permute-start.7 = (f32[16,640]{1,0:T(8,128)S(1)}, f32[16,640]{1,0:T(8,128)S(1)}, u32[]{:S(2)}, u32[]{:S(2)}) collective-permute-start(f32[16,640]{1,0:T(8,128)S(1)} %get-tuple-element.38), channel_id=1, source_target_pairs={{0,12},{4,0},{8,4},{12,8},{1,13},{5,1},{9,5},{13,9},{2,14},{6,2},{... | collective-permute-start | bytes 122888 | tf_op jit(solution)/shard_map/ppermute | solution.py:562

commit v7 on v6

--- a/solution.py
+++ b/solution.py
@@ -167,21 +167,22 @@
 
 def fold_side(side):
     lane = iota((8, 128), 1)
-    turned = pltpu.roll(side, EDGE, 1)
+    used = (lane < EDGE) | (lane >= 128 - EDGE)
     folded = jnp.zeros((8, 128), f32)
     for g in range(PART // 8):
-        piece = jnp.where(lane < 2 * EDGE, turned[8 * g : 8 * g + 8], 0.0)
-        folded = folded + (pltpu.roll(piece, 2 * EDGE * g, 1) if g else piece)
+        piece = jnp.where(used, side[8 * g : 8 * g + 8], 0.0)
+        folded = folded + pltpu.roll(piece, EDGE + 2 * EDGE * g, 1)
     return folded
 
 
 def unfold_side(folded):
     lane = iota((8, 128), 1)
+    used = (lane < EDGE) | (lane >= 128 - EDGE)
     pieces = []
     for g in range(PART // 8):
-        piece = pltpu.roll(folded, 128 - 2 * EDGE * g, 1) if g else folded
-        pieces.append(jnp.where(lane < 2 * EDGE, piece, 0.0))
-    return pltpu.roll(jnp.concatenate(pieces, axis=0), 128 - EDGE, 1)
+        piece = pltpu.roll(folded, 128 - EDGE - 2 * EDGE * g, 1)
+        pieces.append(jnp.where(used, piece, 0.0))
+    return jnp.concatenate(pieces, axis=0)
 
 
 def first_kernel(

time: 31.6 us -> 31.4 us (level)
  no operation moved by 1% of the time
where the time goes in v7:
time: 31.4 us; the launch traced here: 31.3 us
  starting transfers between devices  13 us (41%)
  waiting for transfers between devices  11 us (35%)
  Pallas kernels  6.63 us (21%)
  between operations  0.69 us (2%)
    pallas_call x10, Pallas kernels, run(): pl.pallas_call(kernel, out_shape=outs, in_specs=[scalar if i in smem else...  6.63 us
    ppermute x4, waiting for transfers between devices, swap(): return lax.ppermute(value, axis, [(i, i ^ distance) for i in range(peers)])  6.35 us
    ppermute x4, starting transfers between devices, swap(): return lax.ppermute(value, axis, [(i, i ^ distance) for i in range(peers)])  5.2 us
    ppermute x2, starting transfers between devices, body(): below = lax.ppermute(up, 'gx', upward)  4.88 us
    ppermute x2, waiting for transfers between devices, body(): above = lax.ppermute(down, 'gx', downward)  4.55 us
    ppermute x2, starting transfers between devices, body(): above = lax.ppermute(down, 'gx', downward)  2.91 us
  transfers between devices with their start and end apart: 8, of which 6 were waited for; matrix products, arithmetic and copies ran while one was open for 0% of the time, Pallas kernels for 7%

profile of v7, /device:TPU:0, one launch (start us, length us, event | category | flops | bytes accessed | tf_op | source)
XLA Modules:
  0.0 31.3 jit_solution(18011325069377616773)
XLA Ops:
  0.6 1.6 %shard_map.68 = (f32[96,128]{1,0:T(8,128)S(1)}, f32[192,128]{1,0:T(8,128)S(1)}, f32[192,512]{1,0:T(8,128)S(1)}, bf16[720,256]{1,0:T(8,128)(2,1)S(1)}, f32[3,32,512]{2,1,0:T(8,128)S(1)}) custom-call(s32[6,32,512]{2,1,0:T(8,128)} %labels_hbm.1, bf16[6,32,512]{2,1,0:T(8,128)(2,1)} %background_hbm.1, f32[4]{0:T(128)} %contrasts_hbm.1, bf16[6,15,15]{2,1,0:T(8,128)(2,1)} %k_hbm.1, ...), custom_call_target="tpu_custom_call" | custom-call | tf_op jit(solution)/shard_map/pallas_call | solution.py:474
  2.3 0.6 %collective-permute-start = (f32[96,128]{1,0:T(8,128)S(1)}, f32[96,128]{1,0:T(8,128)S(1)}, u32[]{:S(2)}, u32[]{:S(2)}) collective-permute-start(f32[96,128]{1,0:T(8,128)S(1)} %get-tuple-element.25), channel_id=1, source_target_pairs={{0,2},{2,0},{1,3},{3,1},{4,6},{6,4},{5,7},{7,5},{8,10},{10,8},{9,1... | collective-permute-start | bytes 147464 | tf_op jit(solution)/shard_map/ppermute | solution.py:495
  2.8 0.7 %shard_map.69 = (f32[48,640]{1,0:T(8,128)S(1)}, f32[48,640]{1,0:T(8,128)S(1)}) custom-call(f32[192,512]{1,0:T(8,128)S(1)} %get-tuple-element.21.density_ref, bf16[720,256]{1,0:T(8,128)(2,1)S(1)} %get-tuple-element.22.bands_ref, f32[3,32,512]{2,1,0:T(8,128)S(1)} %get-tuple-element.23.observed_ref), custom_call_target="tpu_custom_call" | custom-call | tf_op jit(solution)/shard_map/pallas_call | solution.py:474
  3.5 0.2 collective-permute-done.edge_ref
  3.7 0.1 shard_map.70.part_ref
  3.8 2.9 %collective-permute-start.1 = (f32[48,512]{1,0:T(8,128)S(1)}, f32[48,512]{1,0:T(8,128)S(1)}, u32[]{:S(2)}, u32[]{:S(2)}) collective-permute-start(f32[48,512]{1,0:T(8,128)S(1)} %shard_map.70.part_ref), channel_id=1, source_target_pairs={{0,1},{1,0},{2,3},{3,2},{4,5},{5,4},{6,7},{7,6},{8,9},{9,8},{10,11... | collective-permute-start | bytes 294920 | tf_op jit(solution)/shard_map/ppermute | solution.py:495
  6.7 3.1 %collective-permute-done.1.other_ref = f32[48,512]{1,0:T(8,128)S(1)} collective-permute-done((f32[48,512]{1,0:T(8,128)S(1)}, f32[48,512]{1,0:T(8,128)S(1)}, u32[]{:S(2)}, u32[]{:S(2)}) %collective-permute-start.1) | collective-permute-done | bytes 98336 | tf_op jit(solution)/shard_map/ppermute | solution.py:495
  9.8 0.1 shard_map.71
  9.9 1.9 %collective-permute-start.2 = (f32[24,640]{1,0:T(8,128)S(1)}, f32[24,640]{1,0:T(8,128)S(1)}, u32[]{:S(2)}, u32[]{:S(2)}) collective-permute-start(f32[24,640]{1,0:T(8,128)S(1)} %get-tuple-element.28), channel_id=1, source_target_pairs={{12,0},{0,4},{4,8},{8,12},{13,1},{1,5},{5,9},{9,13},{14,2},{2,6},{... | collective-permute-start | bytes 184328 | tf_op jit(solution)/shard_map/ppermute | solution.py:564
  11.8 2.1 %collective-permute-start.3 = (f32[24,640]{1,0:T(8,128)S(1)}, f32[24,640]{1,0:T(8,128)S(1)}, u32[]{:S(2)}, u32[]{:S(2)}) collective-permute-start(f32[24,640]{1,0:T(8,128)S(1)} %get-tuple-element.29), channel_id=1, source_target_pairs={{0,12},{4,0},{8,4},{12,8},{1,13},{5,1},{9,5},{13,9},{2,14},{6,2},{... | collective-permute-start | bytes 184328 | tf_op jit(solution)/shard_map/ppermute | solution.py:563
  13.9 0.2 shard_map.72.turned_ref
  14.1 2.5 %collective-permute-done.2.above_ref = f32[24,640]{1,0:T(8,128)S(1)} collective-permute-done((f32[24,640]{1,0:T(8,128)S(1)}, f32[24,640]{1,0:T(8,128)S(1)}, u32[]{:S(2)}, u32[]{:S(2)}) %collective-permute-start.2) | collective-permute-done | bytes 61472 | tf_op jit(solution)/shard_map/ppermute | solution.py:564
  16.6 0.1 collective-permute-done.3.below_ref
  16.7 0.8 %shard_map.73 = (f32[48,128]{1,0:T(8,128)S(1)}, f32[48,640]{1,0:T(8,128)S(1)}, f32[48,640]{1,0:T(8,128)S(1)}) custom-call(f32[48,640]{1,0:T(8,128)S(1)} %get-tuple-element.27.sum_ref, f32[24,640]{1,0:T(8,128)S(1)} %collective-permute-done.2.above_ref, f32[24,640]{1,0:T(8,128)S(1)} %collective-permute-done.3.below_ref, ...), custom_call_target="tpu_custom_call" | custom-call | tf_op jit(solution)/shard_map/pallas_call | solution.py:474
  17.5 0.1 collective-permute-start.4
  17.6 1.3 %shard_map.74 = (f32[48,640]{1,0:T(8,128)S(1)}, f32[48,640]{1,0:T(8,128)S(1)}) custom-call(f32[48,640]{1,0:T(8,128)S(1)} %get-tuple-element.27.sum_ref, f32[24,640]{1,0:T(8,128)S(1)} %collective-permute-done.2.above_ref, f32[24,640]{1,0:T(8,128)S(1)} %collective-permute-done.3.below_ref, ...), custom_call_target="tpu_custom_call", output_to_operand_aliasing={{0}: (7, {}), {1}: (8, {})} | custom-call | tf_op jit(solution)/shard_map/pallas_call | solution.py:474
  18.9 0.1 shard_map.75.a
  19.1 1.7 %collective-permute-start.5 = (f32[48,512]{1,0:T(8,128)S(1)}, f32[48,512]{1,0:T(8,128)S(1)}, u32[]{:S(2)}, u32[]{:S(2)}) collective-permute-start(f32[48,512]{1,0:T(8,128)S(1)} %shard_map.75.a), channel_id=1, source_target_pairs={{0,1},{1,0},{2,3},{3,2},{4,5},{5,4},{6,7},{7,6},{8,9},{9,8},{10,11... | collective-permute-start | bytes 294920 | tf_op jit(solution)/shard_map/ppermute | solution.py:495
  20.8 3.0 %collective-permute-done.5.b = f32[48,512]{1,0:T(8,128)S(1)} collective-permute-done((f32[48,512]{1,0:T(8,128)S(1)}, f32[48,512]{1,0:T(8,128)S(1)}, u32[]{:S(2)}, u32[]{:S(2)}) %collective-permute-start.5) | collective-permute-done | bytes 98336 | tf_op jit(solution)/shard_map/ppermute | solution.py:495
  23.8 0.1 shard_map.76
  23.9 1.0 %collective-permute-start.6 = (f32[16,640]{1,0:T(8,128)S(1)}, f32[16,640]{1,0:T(8,128)S(1)}, u32[]{:S(2)}, u32[]{:S(2)}) collective-permute-start(f32[16,640]{1,0:T(8,128)S(1)} %get-tuple-element.37), channel_id=1, source_target_pairs={{12,0},{0,4},{4,8},{8,12},{13,1},{1,5},{5,9},{9,13},{14,2},{2,6},{... | collective-permute-start | bytes 122888 | tf_op jit(solution)/shard_map/ppermute | solution.py:564
  25.0 2.8 %collective-permute-start.7 = (f32[16,640]{1,0:T(8,128)S(1)}, f32[16,640]{1,0:T(8,128)S(1)}, u32[]{:S(2)}, u32[]{:S(2)}) collective-permute-start(f32[16,640]{1,0:T(8,128)S(1)} %get-tuple-element.38), channel_id=1, source_target_pairs={{0,12},{4,0},{8,4},{12,8},{1,13},{5,1},{9,5},{13,9},{2,14},{6,2},{... | collective-permute-start | bytes 122888 | tf_op jit(solution)/shard_map/ppermute | solution.py:563
  27.8 2.0 %collective-permute-done.6.above_ref = f32[16,640]{1,0:T(8,128)S(1)} collective-permute-done((f32[16,640]{1,0:T(8,128)S(1)}, f32[16,640]{1,0:T(8,128)S(1)}, u32[]{:S(2)}, u32[]{:S(2)}) %collective-permute-start.6) | collective-permute-done | bytes 40992 | tf_op jit(solution)/shard_map/ppermute | solution.py:564
  29.8 1.5 %shard_map.77 = (f32[3,16,512]{2,1,0:T(8,128)}, f32[6,32,512]{2,1,0:T(8,128)}) custom-call(s32[1]{0:T(128)} %bitcast.start_ref, f32[48,640]{1,0:T(8,128)S(1)} %get-tuple-element.36.sum_ref, f32[16,640]{1,0:T(8,128)S(1)} %collective-permute-done.6.above_ref, f32[16,640]{1,0:T(8,128)S(1)} %collective-permute-done.7.below_ref, ...), custom_call_target="tpu_custom_call" | custom-call | tf_op jit(solution)/shard_map/pallas_call | solution.py:474
  (2 shorter events, 0.0 us)
Async XLA Ops:
  2.3 1.4 %collective-permute-start = (f32[96,128]{1,0:T(8,128)S(1)}, f32[96,128]{1,0:T(8,128)S(1)}, u32[]{:S(2)}, u32[]{:S(2)}) collective-permute-start(f32[96,128]{1,0:T(8,128)S(1)} %get-tuple-element.25), channel_id=1, source_target_pairs={{0,2},{2,0},{1,3},{3,1},{4,6},{6,4},{5,7},{7,5},{8,10},{10,8},{9,1... | collective-permute-start | bytes 147464 | tf_op jit(solution)/shard_map/ppermute | solution.py:495
  3.8 6.0 %collective-permute-start.1 = (f32[48,512]{1,0:T(8,128)S(1)}, f32[48,512]{1,0:T(8,128)S(1)}, u32[]{:S(2)}, u32[]{:S(2)}) collective-permute-start(f32[48,512]{1,0:T(8,128)S(1)} %shard_map.70.part_ref), channel_id=1, source_target_pairs={{0,1},{1,0},{2,3},{3,2},{4,5},{5,4},{6,7},{7,6},{8,9},{9,8},{10,11... | collective-permute-start | bytes 294920 | tf_op jit(solution)/shard_map/ppermute | solution.py:495
  9.9 6.7 %collective-permute-start.2 = (f32[24,640]{1,0:T(8,128)S(1)}, f32[24,640]{1,0:T(8,128)S(1)}, u32[]{:S(2)}, u32[]{:S(2)}) collective-permute-start(f32[24,640]{1,0:T(8,128)S(1)} %get-tuple-element.28), channel_id=1, source_target_pairs={{12,0},{0,4},{4,8},{8,12},{13,1},{1,5},{5,9},{9,13},{14,2},{2,6},{... | collective-permute-start | bytes 184328 | tf_op jit(solution)/shard_map/ppermute | solution.py:564
  11.8 4.9 %collective-permute-start.3 = (f32[24,640]{1,0:T(8,128)S(1)}, f32[24,640]{1,0:T(8,128)S(1)}, u32[]{:S(2)}, u32[]{:S(2)}) collective-permute-start(f32[24,640]{1,0:T(8,128)S(1)} %get-tuple-element.29), channel_id=1, source_target_pairs={{0,12},{4,0},{8,4},{12,8},{1,13},{5,1},{9,5},{13,9},{2,14},{6,2},{... | collective-permute-start | bytes 184328 | tf_op jit(solution)/shard_map/ppermute | solution.py:563
  17.5 1.4 %collective-permute-start.4 = (f32[48,128]{1,0:T(8,128)S(1)}, f32[48,128]{1,0:T(8,128)S(1)}, u32[]{:S(2)}, u32[]{:S(2)}) collective-permute-start(f32[48,128]{1,0:T(8,128)S(1)} %get-tuple-element.35), channel_id=1, source_target_pairs={{0,2},{2,0},{1,3},{3,1},{4,6},{6,4},{5,7},{7,5},{8,10},{10,8},{9,1... | collective-permute-start | bytes 73736 | tf_op jit(solution)/shard_map/ppermute | solution.py:495
  19.1 4.8 %collective-permute-start.5 = (f32[48,512]{1,0:T(8,128)S(1)}, f32[48,512]{1,0:T(8,128)S(1)}, u32[]{:S(2)}, u32[]{:S(2)}) collective-permute-start(f32[48,512]{1,0:T(8,128)S(1)} %shard_map.75.a), channel_id=1, source_target_pairs={{0,1},{1,0},{2,3},{3,2},{4,5},{5,4},{6,7},{7,6},{8,9},{9,8},{10,11... | collective-permute-start | bytes 294920 | tf_op jit(solution)/shard_map/ppermute | solution.py:495
  23.9 5.8 %collective-permute-start.6 = (f32[16,640]{1,0:T(8,128)S(1)}, f32[16,640]{1,0:T(8,128)S(1)}, u32[]{:S(2)}, u32[]{:S(2)}) collective-permute-start(f32[16,640]{1,0:T(8,128)S(1)} %get-tuple-element.37), channel_id=1, source_target_pairs={{12,0},{0,4},{4,8},{8,12},{13,1},{1,5},{5,9},{9,13},{14,2},{2,6},{... | collective-permute-start | bytes 122888 | tf_op jit(solution)/shard_map/ppermute | solution.py:564
  25.0 4.8 %collective-permute-start.7 = (f32[16,640]{1,0:T(8,128)S(1)}, f32[16,640]{1,0:T(8,128)S(1)}, u32[]{:S(2)}, u32[]{:S(2)}) collective-permute-start(f32[16,640]{1,0:T(8,128)S(1)} %get-tuple-element.38), channel_id=1, source_target_pairs={{0,12},{4,0},{8,4},{12,8},{1,13},{5,1},{9,5},{13,9},{2,14},{6,2},{... | collective-permute-start | bytes 122888 | tf_op jit(solution)/shard_map/ppermute | solution.py:563

commit v8 on v7

--- a/solution.py
+++ b/solution.py
@@ -11,7 +11,7 @@
 descent = 0.01
 ITERS = 2
 PART = 48
-EDGE = 9
+NEAR, HALO = 9, 25
 FULL = 64
 WIDE = 256
 GRANT = 16 * 2**20
@@ -98,10 +98,10 @@
     lane = iota(message.shape, 1)
     turned = pltpu.roll(message, 96, 1)
     zero = jnp.zeros_like(message)
-    first = field[:, :128] + jnp.where(lane < EDGE, message, zero)
-    last = field[:, width - 256 : width - 128] + jnp.where(lane >= 128 - EDGE, turned, zero)
+    first = field[:, :128] + jnp.where(lane < NEAR, message, zero)
+    last = field[:, width - 256 : width - 128] + jnp.where(lane >= 128 - NEAR, turned, zero)
     side = field[:, width - 128 :] + jnp.where(
-        lane < EDGE, turned, jnp.where(lane >= 128 - EDGE, message, zero)
+        lane < HALO, turned, jnp.where(lane >= 128 - HALO, message, zero)
     )
     return jnp.concatenate([first, field[:, 128 : width - 256], last, side], axis=1)
 
@@ -154,40 +154,66 @@
 
 
 def scatter_surface(bands, rounded, prod_ref, span, radius):
-    width = rounded.shape[1] + 128
+    width = rounded.shape[1]
     prod_ref[...] = jnp.dot(bands, rounded, preferred_element_type=f32)
-    total = jnp.zeros((PART, width), f32)
-    side = jnp.zeros((PART, 128), f32)
+    total = prod_ref[radius * PART : (radius + 1) * PART, :]
     for j in range(span):
-        piece = jnp.concatenate([prod_ref[j * PART : (j + 1) * PART, :], side], axis=1)
-        shift = (radius - j) % width
-        total = total + (pltpu.roll(piece, shift, 1) if shift else piece)
+        if j != radius:
+            piece = prod_ref[j * PART : (j + 1) * PART, :]
+            total = total + pltpu.roll(piece, (radius - j) % width, 1)
     return total
 
 
-def fold_side(side):
+def fold_side(side, reach):
     lane = iota((8, 128), 1)
-    used = (lane < EDGE) | (lane >= 128 - EDGE)
-    folded = jnp.zeros((8, 128), f32)
-    for g in range(PART // 8):
-        piece = jnp.where(used, side[8 * g : 8 * g + 8], 0.0)
-        folded = folded + pltpu.roll(piece, EDGE + 2 * EDGE * g, 1)
-    return folded
-
-
-def unfold_side(folded):
+    used = (lane < reach) | (lane >= 128 - reach)
+    count = 128 // (2 * reach)
+    blocks = []
+    for first in range(0, PART // 8, count):
+        folded = jnp.zeros((8, 128), f32)
+        for n, g in enumerate(range(first, min(first + count, PART // 8))):
+            piece = jnp.where(used, side[8 * g : 8 * g + 8], 0.0)
+            folded = folded + pltpu.roll(piece, reach + 2 * reach * n, 1)
+        blocks.append(folded)
+    return blocks
+
+
+def unfold_side(blocks, reach):
     lane = iota((8, 128), 1)
-    used = (lane < EDGE) | (lane >= 128 - EDGE)
+    used = (lane < reach) | (lane >= 128 - reach)
+    count = 128 // (2 * reach)
     pieces = []
     for g in range(PART // 8):
-        piece = pltpu.roll(folded, 128 - EDGE - 2 * EDGE * g, 1)
+        piece = pltpu.roll(blocks[g // count], 128 - reach - 2 * reach * (g % count), 1)
         pieces.append(jnp.where(used, piece, 0.0))
     return jnp.concatenate(pieces, axis=0)
 
 
+def depth_message_rows(cells_y, reach):
+    blocks = -(-(PART // 8) // (128 // (2 * reach)))
+    return PART * (cells_y // 128) + 8 * (blocks - 1)
+
+
+def fold_places(cells_y):
+    blocks = cells_y // 128
+    return [PART * (n % blocks) + (PART - 1) * (n // blocks) for n in range(8)]
+
+
+def store_depth_message(out_ref, part, cells_y, reach):
+    for start in range(0, cells_y, 128):
+        row = PART * (start // 128)
+        out_ref[row : row + PART, :] = part[:, start : start + 128]
+    folded, *others = fold_side(part[:, cells_y:], reach)
+    for n, row in enumerate(fold_places(cells_y)):
+        out_ref[row : row + 1, :] = folded[n : n + 1]
+    for n, block in enumerate(others):
+        row = PART * (cells_y // 128) + 8 * n
+        out_ref[row : row + 8, :] = block
+
+
 def first_kernel(
     labels_hbm, background_hbm, contrasts_hbm, k_hbm, observed_hbm,
-    edge_ref, density_edge_ref, density_ref, bands_ref, observed_ref,
+    edge_ref, density_ref, bands_ref, observed_ref,
     labels_ref, background_ref, contrasts_ref, k_ref, sems,
     taps_ref, base_ref, prod_ref,
 ):
@@ -221,16 +247,18 @@
         density = value + background_ref[l].astype(f32)
         rows = slice(l * cells_x, (l + 1) * cells_x)
         density_ref[rows, :] = density
-        density_edge_ref[rows, :] = edge_columns(density[:, :128], density[:, cells_y - 128 :])
+        edge_ref[2 * PART + l * cells_x : 2 * PART + (l + 1) * cells_x, :] = edge_columns(
+            density[:, :128], density[:, cells_y - 128 :]
+        )
     edge_ref[:PART, :] = edge_message(
         bands_ref[:, : layers * cells_x],
-        density_edge_ref[...].astype(bf16),
+        edge_ref[2 * PART :, :].astype(bf16),
         prod_ref,
         span,
         (span - 1) // 2,
     )
     empty = jnp.zeros((8, 128), f32)
-    edge_ref[PART:, :] = adjoint_of(
+    edge_ref[PART : 2 * PART, :] = adjoint_of(
         *(
             jnp.concatenate(
                 [
@@ -249,9 +277,18 @@
     density_ref, bands_ref, observed_ref, part_ref, q_ref, prod_ref, obs_ref, *, span
 ):
     lanes, cells_y = density_ref.shape
-    part_ref[...] = scatter_surface(
-        bands_ref[:, :lanes], density_ref[...].astype(bf16), prod_ref, span, (span - 1) // 2
-    )
+    radius = (span - 1) // 2
+    width = cells_y + 128
+    prod_ref[...] = jnp.dot(
+        bands_ref[:, :lanes], density_ref[...].astype(bf16), preferred_element_type=f32
+    )
+    total = jnp.zeros((PART, width), f32)
+    side = jnp.zeros((PART, 128), f32)
+    for j in range(span):
+        piece = jnp.concatenate([prod_ref[j * PART : (j + 1) * PART, :], side], axis=1)
+        shift = (radius - j) % width
+        total = total + (pltpu.roll(piece, shift, 1) if shift else piece)
+    part_ref[...] = total
     obs_ref[...] = jnp.zeros(obs_ref.shape, f32)
     for k in range(3):
         obs_ref[k, 8 : PART - 8, :cells_y] = observed_ref[k]
@@ -262,14 +299,9 @@
     out_ref[...] = bands_ref[...].astype(f32).T.astype(bf16)
 
 
-def edges_kernel(part_ref, edge_ref, out_ref):
-    cells_y = out_ref.shape[1]
+def edges_kernel(part_ref, edge_ref, out_ref, *, cells_y):
     part = add_edges(part_ref[...], edge_ref[:PART, :])
-    out_ref[...] = part[:, :cells_y]
-    folded = fold_side(part[:, cells_y:])
-    for n in range(8):
-        row = (PART - 1) * (n // 4)
-        out_ref[row : row + 1, 128 * (n % 4) : 128 * (n % 4 + 1)] = folded[n : n + 1]
+    store_depth_message(out_ref, part, cells_y, HALO)
 
 
 def send_rows(sum_ref, up_ref, down_ref):
@@ -281,21 +313,30 @@
 
 
 def rows_kernel(
-    part_ref, other_ref, q_ref, edge_ref, sum_ref, up_ref, down_ref, q_out_ref, fold_ref
+    part_ref, other_ref, q_ref, edge_ref, sum_ref, up_ref, down_ref, q_out_ref,
+    dense_ref, fold_ref, *, reach,
 ):
-    cells_y = part_ref.shape[1]
-    sum_ref[:, :cells_y] = part_ref[...] + other_ref[...]
-    for n in range(8):
-        row = (PART - 1) * (n // 4)
-        fold_ref[n : n + 1, :] = sum_ref[row : row + 1, 128 * (n % 4) : 128 * (n % 4 + 1)]
-    sum_ref[:, cells_y:] = unfold_side(fold_ref[...])
-    zero = jnp.zeros((1, cells_y), f32)
-    sum_ref[:1, :cells_y] = zero
-    sum_ref[PART - 1 :, :cells_y] = zero
-    send_rows(sum_ref, up_ref, down_ref)
+    cells_y = sum_ref.shape[1] - 128
+    dense_ref[...] = part_ref[...] + other_ref[...]
+    zero = jnp.zeros((1, 128), f32)
+    for n, row in enumerate(fold_places(cells_y)):
+        fold_ref[n : n + 1, :] = dense_ref[row : row + 1, :]
+    folded = [fold_ref[...]]
+    for row in range(PART * (cells_y // 128), dense_ref.shape[0], 8):
+        folded.append(dense_ref[row : row + 8, :])
+    for row in fold_places(cells_y):
+        dense_ref[row : row + 1, :] = zero
+    for start in range(0, cells_y, 128):
+        row = PART * (start // 128)
+        sum_ref[:, start : start + 128] = dense_ref[row : row + PART, :]
+    sum_ref[:, cells_y:] = unfold_side(folded, reach)
+    sub = iota((8, sum_ref.shape[1]), 0)
+    up_ref[:8, :] = sum_ref[8:16, :]
+    up_ref[8:16, :] = jnp.where(sub >= 1, sum_ref[:8, :], sum_ref[16:24, :])
+    down_ref[:8, :] = sum_ref[32:40, :]
+    down_ref[8:16, :] = jnp.where(sub < 7, sum_ref[40:48, :], sum_ref[24:32, :])
     if q_ref is not None:
-        sub = iota((8, sum_ref.shape[1]), 0)
-        q_out_ref[...] = add_edges(q_ref[...], edge_ref[PART:, :])
+        q_out_ref[...] = add_edges(q_ref[...], edge_ref[PART : 2 * PART, :])
         up_ref[16:24, :] = jnp.where(sub < 7, q_out_ref[8:16, :], q_out_ref[:8, :])
         down_ref[16:24, :] = jnp.where(sub >= 1, q_out_ref[32:40, :], q_out_ref[40:48, :])
 
@@ -345,71 +386,28 @@
     return (adjoint_square(s) - q).astype(bf16)
 
 
-def field_after_step(refs, out_refs, scratch_refs, span):
-    sum_ref, above_ref, below_ref, q_ref, density_ref, bands_ref, turned_ref = refs
-    part_ref, q_out_ref = out_refs
-    stack_ref, prod_ref = scratch_refs
+def middle_kernel(
+    sum_ref, above_ref, below_ref, q_ref, density_ref, edge_ref, bands_ref, turned_ref,
+    out_ref, q_out_ref,
+    stack_ref, prod_ref, *, span,
+):
     radius = (span - 1) // 2
     lanes, cells_y = density_ref.shape
     above, below = above_ref[...], below_ref[...]
     q = full_q(q_ref[...], above, below)
     q_out_ref[...] = q
     adjoint = rounded_adjoint(full_surface(sum_ref[...], above, below), q)
-    stack_shifts(adjoint, stack_ref, slice(0, cells_y), span, radius)
+    stack_shifts(adjoint, stack_ref, slice(0, cells_y + 128), span, radius)
     gradient = jnp.dot(turned_ref[:lanes, :], stack_ref[...], preferred_element_type=f32)
-    density = density_ref[...] - descent * gradient
-    part_ref[...] = scatter_surface(
-        bands_ref[:, :lanes], density.astype(bf16), prod_ref, span, radius
-    )
-
-
-def middle_kernel(
-    sum_ref, above_ref, below_ref, q_ref, density_ref, bands_ref, turned_ref,
-    density_edge_ref,
-    edge_ref, part_ref, q_out_ref,
-    edge_stack_ref, edge_prod_ref, stack_ref, prod_ref, *, span,
-):
-    radius = (span - 1) // 2
-    lanes = density_edge_ref.shape[0]
-    total, q = edges_of(sum_ref[...]), edges_of(q_ref[...])
-    above, below = edges_of(above_ref[...]), edges_of(below_ref[...])
-    adjoint = rounded_adjoint(full_surface(total, above, below), full_q(q, above, below))
-    stack_shifts(adjoint, edge_stack_ref, slice(0, 128), span, radius)
-    gradient = jnp.dot(
-        turned_ref[:lanes, :], edge_stack_ref[...], preferred_element_type=f32
-    )
-    density = density_edge_ref[...] - descent * gradient
-    lane = iota(density.shape, 1)
-    keep = ((lane >= 32) & (lane < 48)) | (lane >= 112)
-    density = jnp.where(keep, density, 0.0)
-    edge_ref[...] = edge_message(
-        bands_ref[:, :lanes], density.astype(bf16), edge_prod_ref, span, radius
-    )
-
-    @pl.when(lax.axis_index("gy") == 1)
-    def _():
-        field_after_step(
-            (sum_ref, above_ref, below_ref, q_ref, density_ref, bands_ref, turned_ref),
-            (part_ref, q_out_ref),
-            (stack_ref, prod_ref),
-            span,
-        )
-
-
-def middle_field_kernel(
-    sum_ref, above_ref, below_ref, q_ref, density_ref, bands_ref, turned_ref,
-    part_in_ref, q_in_ref,
-    part_ref, q_out_ref,
-    stack_ref, prod_ref, *, span,
-):
-    @pl.when(lax.axis_index("gy") == 0)
-    def _():
-        field_after_step(
-            (sum_ref, above_ref, below_ref, q_ref, density_ref, bands_ref, turned_ref),
-            (part_ref, q_out_ref),
-            (stack_ref, prod_ref),
-            span,
-        )
+    density = density_ref[...] - descent * gradient[:, :cells_y]
+    message = edge_ref[2 * PART :, :]
+    lane = iota(message.shape, 1)
+    outside = jnp.where(lane < 16, pltpu.roll(message, 96, 1), message)
+    outside = outside - descent * gradient[:, cells_y:]
+    outside = jnp.where((lane < 16) | (lane >= 112), outside, 0.0)
+    rounded = jnp.concatenate([density.astype(bf16), outside.astype(bf16)], axis=1)
+    part = scatter_surface(bands_ref[:, :lanes], rounded, prod_ref, span, radius)
+    store_depth_message(out_ref, part, cells_y, NEAR)
 
 
 def last_kernel(
@@ -516,11 +514,10 @@
     def kernel_of(body_of):
         return functools.partial(body_of, span=span)
 
-    edge, density_edge, density, bands, observed = call(
+    edge, density, bands, observed = call(
         first_kernel,
         (
-            shaped((2 * PART, 128)),
-            shaped((lanes, 128)),
+            shaped((2 * PART + lanes, 128)),
             shaped((lanes, cells_y)),
             shaped((span * PART, WIDE), bf16),
             shaped(observed.shape),
@@ -541,40 +538,40 @@
         kernel_of(first_field_kernel), (field, field), (prod, ((3, PART, width), f32))
     )(density, bands, observed)
     start = (lax.axis_index("gz") * share).astype(jnp.int32).reshape(1)
-
     turned = call(transpose_kernel, shaped((WIDE, span * PART), bf16))(bands)
-    fold = (((8, 128), f32),)
+
+    others = swap(edge, "gy", 1)
+    part = call(
+        functools.partial(edges_kernel, cells_y=cells_y),
+        shaped((depth_message_rows(cells_y, HALO), 128)),
+    )(part, others)
     for iteration in range(ITERS):
-        others = swap(edge, "gy", 1)
-        part = call(edges_kernel, shaped((PART, cells_y)))(part, others)
         for bit in range(depth_peers.bit_length() - 2):
             part = part + swap(part, "gz", 2 << bit)
         other = swap(part, "gz", 1)
+        scratch = ((part.shape, f32), ((8, 128), f32))
         if iteration == 0:
             total, up, down, q = call(
-                rows_kernel, (field, shaped((24, width)), shaped((24, width)), field), fold
+                functools.partial(rows_kernel, reach=HALO),
+                (field, shaped((24, width)), shaped((24, width)), field),
+                scratch,
             )(part, other, q, others)
         else:
             total, up, down = call(
-                lambda a, b, c, d, e, g: rows_kernel(a, b, None, None, c, d, e, None, g),
+                lambda a, b, c, d, e, f, g: rows_kernel(
+                    a, b, None, None, c, d, e, None, f, g, reach=NEAR
+                ),
                 (field, shaped((16, width)), shaped((16, width))),
-                fold,
+                scratch,
             )(part, other)
         below = lax.ppermute(up, "gx", upward)
         above = lax.ppermute(down, "gx", downward)
         if iteration == 0:
-            known = (total, above, below, q, density, bands, turned)
-            edge, part, q = call(
+            part, q = call(
                 kernel_of(middle_kernel),
-                (shaped((PART, 128)), field, field),
-                (edge_stack, edge_prod, stack, prod),
-            )(*known, density_edge)
-            part, q = call(
-                kernel_of(middle_field_kernel),
-                (field, field),
-                (stack, prod),
-                aliases={7: 0, 8: 1},
-            )(*known, part, q)
+                (shaped((depth_message_rows(cells_y, NEAR), 128)), field),
+                (((span * PART, width), bf16), ((span * PART, width), f32)),
+            )(total, above, below, q, density, others, bands, turned)
     return call(
         kernel_of(last_kernel),
         (shaped((3, share, cells_y)), shaped((layers, cells_x, cells_y))),

time: 31.4 us -> 30.6 us (0.975)
  Pallas kernels: 6.63 us -> 5.71 us
    pallas_call x10 -> x8, Pallas kernels: 6.63 us -> 5.71 us  [run(): pl.pallas_call(kernel, out_shape=outs, in_specs=[scalar if i in smem else...]
    ppermute x4 -> x3, waiting for transfers between devices: 6.35 us -> 6.54 us  [swap(): return lax.ppermute(value, axis, [(i, i ^ distance) for i in range(peers)])]
    ppermute x4 -> x3, starting transfers between devices: 5.2 us -> 5.11 us  [swap(): return lax.ppermute(value, axis, [(i, i ^ distance) for i in range(peers)])]
  transfers between devices with their start and end apart: 8 -> 7, of which waited for: 6 -> 5; matrix products, arithmetic and copies ran while one was open for 0% -> 0% of each run, Pallas kernels for 7% -> 3%
where the time goes in v8:
time: 30.6 us; the launch traced here: 30.4 us
  starting transfers between devices  12.9 us (42%)
  waiting for transfers between devices  11.2 us (37%)
  Pallas kernels  5.71 us (19%)
  between operations  0.66 us (2%)
    ppermute x3, waiting for transfers between devices, swap(): return lax.ppermute(value, axis, [(i, i ^ distance) for i in range(peers)])  6.54 us
    pallas_call x8, Pallas kernels, run(): pl.pallas_call(kernel, out_shape=outs, in_specs=[scalar if i in smem else...  5.71 us
    ppermute x3, starting transfers between devices, swap(): return lax.ppermute(value, axis, [(i, i ^ distance) for i in range(peers)])  5.11 us
    ppermute x2, starting transfers between devices, body(): below = lax.ppermute(up, 'gx', upward)  4.87 us
    ppermute x2, waiting for transfers between devices, body(): above = lax.ppermute(down, 'gx', downward)  4.57 us
    ppermute x2, starting transfers between devices, body(): above = lax.ppermute(down, 'gx', downward)  2.9 us
  transfers between devices with their start and end apart: 7, of which 5 were waited for; matrix products, arithmetic and copies ran while one was open for 0% of the time, Pallas kernels for 3%

profile of v8, /device:TPU:0, one launch (start us, length us, event | category | flops | bytes accessed | tf_op | source)
XLA Modules:
  0.0 30.4 jit_solution(3717207453958003421)
XLA Ops:
  0.6 1.6 %shard_map.68 = (f32[288,128]{1,0:T(8,128)S(1)}, f32[192,512]{1,0:T(8,128)S(1)}, bf16[720,256]{1,0:T(8,128)(2,1)S(1)}, f32[3,32,512]{2,1,0:T(8,128)S(1)}) custom-call(s32[6,32,512]{2,1,0:T(8,128)} %labels_hbm.1, bf16[6,32,512]{2,1,0:T(8,128)(2,1)} %background_hbm.1, f32[4]{0:T(128)} %contrasts_hbm.1, bf16[6,15,15]{2,1,0:T(8,128)(2,1)} %k_hbm.1, ...), custom_call_target="tpu_custom_call" | custom-call | tf_op jit(solution)/shard_map/pallas_call | solution.py:472
  2.3 0.6 %collective-permute-start = (f32[288,128]{1,0:T(8,128)S(1)}, f32[288,128]{1,0:T(8,128)S(1)}, u32[]{:S(2)}, u32[]{:S(2)}) collective-permute-start(f32[288,128]{1,0:T(8,128)S(1)} %get-tuple-element.21), channel_id=1, source_target_pairs={{0,2},{2,0},{1,3},{3,1},{4,6},{6,4},{5,7},{7,5},{8,10},{10,8},{9,1... | collective-permute-start | bytes 442376 | tf_op jit(solution)/shard_map/ppermute | solution.py:493
  2.8 0.7 %shard_map.69 = (f32[48,640]{1,0:T(8,128)S(1)}, f32[48,640]{1,0:T(8,128)S(1)}) custom-call(f32[192,512]{1,0:T(8,128)S(1)} %get-tuple-element.17.density_ref, bf16[720,256]{1,0:T(8,128)(2,1)S(1)} %get-tuple-element.18.bands_ref, f32[3,32,512]{2,1,0:T(8,128)S(1)} %get-tuple-element.19.observed_ref), custom_call_target="tpu_custom_call" | custom-call | tf_op jit(solution)/shard_map/pallas_call | solution.py:472
  3.5 0.3 collective-permute-done.edge_ref
  3.8 0.1 shard_map.70.part_ref
  4.0 2.9 %collective-permute-start.1 = (f32[208,128]{1,0:T(8,128)S(1)}, f32[208,128]{1,0:T(8,128)S(1)}, u32[]{:S(2)}, u32[]{:S(2)}) collective-permute-start(f32[208,128]{1,0:T(8,128)S(1)} %shard_map.70.part_ref), channel_id=1, source_target_pairs={{0,1},{1,0},{2,3},{3,2},{4,5},{5,4},{6,7},{7,6},{8,9},{9,8},{10,11... | collective-permute-start | bytes 319496 | tf_op jit(solution)/shard_map/ppermute | solution.py:493
  6.8 3.3 %collective-permute-done.1.other_ref = f32[208,128]{1,0:T(8,128)S(1)} collective-permute-done((f32[208,128]{1,0:T(8,128)S(1)}, f32[208,128]{1,0:T(8,128)S(1)}, u32[]{:S(2)}, u32[]{:S(2)}) %collective-permute-start.1) | collective-permute-done | bytes 106528 | tf_op jit(solution)/shard_map/ppermute | solution.py:493
  10.1 0.1 shard_map.71
  10.2 1.9 %collective-permute-start.2 = (f32[24,640]{1,0:T(8,128)S(1)}, f32[24,640]{1,0:T(8,128)S(1)}, u32[]{:S(2)}, u32[]{:S(2)}) collective-permute-start(f32[24,640]{1,0:T(8,128)S(1)} %get-tuple-element.24), channel_id=1, source_target_pairs={{12,0},{0,4},{4,8},{8,12},{13,1},{1,5},{5,9},{9,13},{14,2},{2,6},{... | collective-permute-start | bytes 184328 | tf_op jit(solution)/shard_map/ppermute | solution.py:568
  12.1 2.1 %collective-permute-start.3 = (f32[24,640]{1,0:T(8,128)S(1)}, f32[24,640]{1,0:T(8,128)S(1)}, u32[]{:S(2)}, u32[]{:S(2)}) collective-permute-start(f32[24,640]{1,0:T(8,128)S(1)} %get-tuple-element.25), channel_id=1, source_target_pairs={{0,12},{4,0},{8,4},{12,8},{1,13},{5,1},{9,5},{13,9},{2,14},{6,2},{... | collective-permute-start | bytes 184328 | tf_op jit(solution)/shard_map/ppermute | solution.py:567
  14.2 0.2 shard_map.72.turned_ref
  14.3 2.6 %collective-permute-done.2.above_ref = f32[24,640]{1,0:T(8,128)S(1)} collective-permute-done((f32[24,640]{1,0:T(8,128)S(1)}, f32[24,640]{1,0:T(8,128)S(1)}, u32[]{:S(2)}, u32[]{:S(2)}) %collective-permute-start.2) | collective-permute-done | bytes 61472 | tf_op jit(solution)/shard_map/ppermute | solution.py:568
  16.9 0.0 collective-permute-done.3.below_ref
  17.0 1.4 %shard_map.73 = (f32[192,128]{1,0:T(8,128)S(1)}, f32[48,640]{1,0:T(8,128)S(1)}) custom-call(f32[48,640]{1,0:T(8,128)S(1)} %get-tuple-element.23.sum_ref, f32[24,640]{1,0:T(8,128)S(1)} %collective-permute-done.2.above_ref, f32[24,640]{1,0:T(8,128)S(1)} %collective-permute-done.3.below_ref, f32[48,640]{1,0:T(8,128)S(1)} %get-tuple-element.26.q_ref, ...), custom_call_target="tpu_custom_call" | custom-call | tf_op jit(solution)/shard_map/pallas_call | solution.py:472
  18.3 1.7 %collective-permute-start.4 = (f32[192,128]{1,0:T(8,128)S(1)}, f32[192,128]{1,0:T(8,128)S(1)}, u32[]{:S(2)}, u32[]{:S(2)}) collective-permute-start(f32[192,128]{1,0:T(8,128)S(1)} %get-tuple-element.27.a), channel_id=1, source_target_pairs={{0,1},{1,0},{2,3},{3,2},{4,5},{5,4},{6,7},{7,6},{8,9},{9,8},{10,11... | collective-permute-start | bytes 294920 | tf_op jit(solution)/shard_map/ppermute | solution.py:493
  20.0 3.0 %collective-permute-done.4.b = f32[192,128]{1,0:T(8,128)S(1)} collective-permute-done((f32[192,128]{1,0:T(8,128)S(1)}, f32[192,128]{1,0:T(8,128)S(1)}, u32[]{:S(2)}, u32[]{:S(2)}) %collective-permute-start.4) | collective-permute-done | bytes 98336 | tf_op jit(solution)/shard_map/ppermute | solution.py:493
  23.0 0.1 shard_map.74
  23.1 1.0 %collective-permute-start.5 = (f32[16,640]{1,0:T(8,128)S(1)}, f32[16,640]{1,0:T(8,128)S(1)}, u32[]{:S(2)}, u32[]{:S(2)}) collective-permute-start(f32[16,640]{1,0:T(8,128)S(1)} %get-tuple-element.29), channel_id=1, source_target_pairs={{12,0},{0,4},{4,8},{8,12},{13,1},{1,5},{5,9},{9,13},{14,2},{2,6},{... | collective-permute-start | bytes 122888 | tf_op jit(solution)/shard_map/ppermute | solution.py:568
  24.1 2.8 %collective-permute-start.6 = (f32[16,640]{1,0:T(8,128)S(1)}, f32[16,640]{1,0:T(8,128)S(1)}, u32[]{:S(2)}, u32[]{:S(2)}) collective-permute-start(f32[16,640]{1,0:T(8,128)S(1)} %get-tuple-element.30), channel_id=1, source_target_pairs={{0,12},{4,0},{8,4},{12,8},{1,13},{5,1},{9,5},{13,9},{2,14},{6,2},{... | collective-permute-start | bytes 122888 | tf_op jit(solution)/shard_map/ppermute | solution.py:567
  26.9 2.0 %collective-permute-done.5.above_ref = f32[16,640]{1,0:T(8,128)S(1)} collective-permute-done((f32[16,640]{1,0:T(8,128)S(1)}, f32[16,640]{1,0:T(8,128)S(1)}, u32[]{:S(2)}, u32[]{:S(2)}) %collective-permute-start.5) | collective-permute-done | bytes 40992 | tf_op jit(solution)/shard_map/ppermute | solution.py:568
  28.9 0.0 collective-permute-done.6.below_ref
  28.9 1.5 %shard_map.75 = (f32[3,16,512]{2,1,0:T(8,128)}, f32[6,32,512]{2,1,0:T(8,128)}) custom-call(s32[1]{0:T(128)} %bitcast.start_ref, f32[48,640]{1,0:T(8,128)S(1)} %get-tuple-element.28.sum_ref, f32[16,640]{1,0:T(8,128)S(1)} %collective-permute-done.5.above_ref, f32[16,640]{1,0:T(8,128)S(1)} %collective-permute-done.6.below_ref, ...), custom_call_target="tpu_custom_call" | custom-call | tf_op jit(solution)/shard_map/pallas_call | solution.py:472
Async XLA Ops:
  2.3 1.6 %collective-permute-start = (f32[288,128]{1,0:T(8,128)S(1)}, f32[288,128]{1,0:T(8,128)S(1)}, u32[]{:S(2)}, u32[]{:S(2)}) collective-permute-start(f32[288,128]{1,0:T(8,128)S(1)} %get-tuple-element.21), channel_id=1, source_target_pairs={{0,2},{2,0},{1,3},{3,1},{4,6},{6,4},{5,7},{7,5},{8,10},{10,8},{9,1... | collective-permute-start | bytes 442376 | tf_op jit(solution)/shard_map/ppermute | solution.py:493
  4.0 6.1 %collective-permute-start.1 = (f32[208,128]{1,0:T(8,128)S(1)}, f32[208,128]{1,0:T(8,128)S(1)}, u32[]{:S(2)}, u32[]{:S(2)}) collective-permute-start(f32[208,128]{1,0:T(8,128)S(1)} %shard_map.70.part_ref), channel_id=1, source_target_pairs={{0,1},{1,0},{2,3},{3,2},{4,5},{5,4},{6,7},{7,6},{8,9},{9,8},{10,11... | collective-permute-start | bytes 319496 | tf_op jit(solution)/shard_map/ppermute | solution.py:493
  10.2 6.7 %collective-permute-start.2 = (f32[24,640]{1,0:T(8,128)S(1)}, f32[24,640]{1,0:T(8,128)S(1)}, u32[]{:S(2)}, u32[]{:S(2)}) collective-permute-start(f32[24,640]{1,0:T(8,128)S(1)} %get-tuple-element.24), channel_id=1, source_target_pairs={{12,0},{0,4},{4,8},{8,12},{13,1},{1,5},{5,9},{9,13},{14,2},{2,6},{... | collective-permute-start | bytes 184328 | tf_op jit(solution)/shard_map/ppermute | solution.py:568
  12.1 4.9 %collective-permute-start.3 = (f32[24,640]{1,0:T(8,128)S(1)}, f32[24,640]{1,0:T(8,128)S(1)}, u32[]{:S(2)}, u32[]{:S(2)}) collective-permute-start(f32[24,640]{1,0:T(8,128)S(1)} %get-tuple-element.25), channel_id=1, source_target_pairs={{0,12},{4,0},{8,4},{12,8},{1,13},{5,1},{9,5},{13,9},{2,14},{6,2},{... | collective-permute-start | bytes 184328 | tf_op jit(solution)/shard_map/ppermute | solution.py:567
  18.3 4.7 %collective-permute-start.4 = (f32[192,128]{1,0:T(8,128)S(1)}, f32[192,128]{1,0:T(8,128)S(1)}, u32[]{:S(2)}, u32[]{:S(2)}) collective-permute-start(f32[192,128]{1,0:T(8,128)S(1)} %get-tuple-element.27.a), channel_id=1, source_target_pairs={{0,1},{1,0},{2,3},{3,2},{4,5},{5,4},{6,7},{7,6},{8,9},{9,8},{10,11... | collective-permute-start | bytes 294920 | tf_op jit(solution)/shard_map/ppermute | solution.py:493
  23.1 5.8 %collective-permute-start.5 = (f32[16,640]{1,0:T(8,128)S(1)}, f32[16,640]{1,0:T(8,128)S(1)}, u32[]{:S(2)}, u32[]{:S(2)}) collective-permute-start(f32[16,640]{1,0:T(8,128)S(1)} %get-tuple-element.29), channel_id=1, source_target_pairs={{12,0},{0,4},{4,8},{8,12},{13,1},{1,5},{5,9},{9,13},{14,2},{2,6},{... | collective-permute-start | bytes 122888 | tf_op jit(solution)/shard_map/ppermute | solution.py:568
  24.1 4.8 %collective-permute-start.6 = (f32[16,640]{1,0:T(8,128)S(1)}, f32[16,640]{1,0:T(8,128)S(1)}, u32[]{:S(2)}, u32[]{:S(2)}) collective-permute-start(f32[16,640]{1,0:T(8,128)S(1)} %get-tuple-element.30), channel_id=1, source_target_pairs={{0,12},{4,0},{8,4},{12,8},{1,13},{5,1},{9,5},{13,9},{2,14},{6,2},{... | collective-permute-start | bytes 122888 | tf_op jit(solution)/shard_map/ppermute | solution.py:567
